TPU v7x, 32 devices: a whole 2x2x4 slice. The times are simulated.
32 devices in a mesh: clip: 2 (over y), ha: 4 (over z), wa: 4 (over x, core).
Axes of the slice: x: 2, y: 2, z: 4, core: 2. Of those that a mesh axis runs over, the one named last changes fastest.
Arguments:
- cotangent: float32 [8, 16, 256, 96], P('clip', 'ha', 'wa'), parts along dimension 0, may hold values from -6 to 6
- stored_first: float32 [8, 16, 256, 96], P('clip', 'ha', 'wa'), parts along dimension 0, may hold values from -8 to 8
- stored_second: float32 [8, 16, 256, 96], P('clip', 'ha', 'wa'), parts along dimension 0, may hold values from -8 to 8
- w_first: float32 [3, 3, 3, 96, 96], replicated, may hold values from -0.125 to 0.125
- w_second: float32 [3, 3, 3, 96, 96], replicated, may hold values from -0.125 to 0.125
- w_third: float32 [3, 3, 3, 96, 96], replicated, may hold values from -0.125 to 0.125
Outputs:
- input_grad: float32 [8, 16, 256, 96], P('clip', 'ha', 'wa'), parts along dimension 0
There are 2 independent parts, one for each index of `clip`. A program takes and returns all parts, laid end to end along the dimension named above; an argument that names none is the same for every part. Nothing has to cross between parts.
All inputs are finite; a program needn't handle non-finite values.
Results may differ from a plain program's by a relative error of at most 0.00013.
Values sent between devices are 32-bit elements; how exact they have to be, the bound alone decides.
No kernel may reach another device: no remote copies, remote signals or barrier semaphores. Data moves between devices by JAX's collectives and lax.ppermute only.
A program may use at most 64 MiB of HBM per device.

v0:
```python
import functools

import jax
import jax.numpy as jnp
from jax import lax
from jax.experimental import pallas as pl
from jax.experimental.pallas import tpu as pltpu
from jax.sharding import PartitionSpec as P

LANES = 128
SUB = 8
F32 = jnp.float32
BF16 = jnp.bfloat16
VMEM_SPEC = pl.BlockSpec(memory_space=pltpu.VMEM)
SMEM_SPEC = pl.BlockSpec(memory_space=pltpu.SMEM)


def silu_slope(value):
    sigma = 1.0 / (1.0 + jnp.exp(-value))
    return sigma * (1.0 + value * (1.0 - sigma))


def roll(value, shift, axis):
    return pltpu.roll(value, shift % value.shape[axis], axis)


def lane_of(shape):
    return lax.broadcasted_iota(jnp.int32, shape, len(shape) - 1)


def sub_of(shape):
    return lax.broadcasted_iota(jnp.int32, shape, len(shape) - 2)


def group_frames(frames, chans):
    first, second, third, fourth = frames
    part = LANES - chans
    lane = lane_of(first.shape)
    packed = []
    for index, frame in enumerate((first, second, third)):
        packed.append(jnp.where(lane < chans, frame, roll(fourth, chans - part * index, 1)))
    return packed


def ungroup_frames(groups, chans):
    part = LANES - chans
    lane = lane_of(groups[0].shape)
    frames = [jnp.where(lane < chans, group, 0.0) for group in groups]
    fourth = jnp.zeros_like(groups[0])
    for index in reversed(range(3)):
        moved = roll(groups[index], part * (index + 1), 1)
        fourth = jnp.where(lane < part * (index + 1), moved, fourth)
    return frames + [jnp.where(lane < chans, fourth, 0.0)]


def pack_kernel(par_ref, cot_ref, sec_ref, fst_ref, ha0, ha1, hb0, hb1, wp0, wp1, cp_ref, s2_ref, s1_ref):
    frames, rows, cols, chans = cot_ref.shape
    blank = jnp.zeros((frames, rows, cols, LANES), F32)
    cp_ref[...] = blank
    s2_ref[...] = blank
    s1_ref[...] = blank
    for t in range(frames):
        for h in range(rows):
            cp_ref[t, h, :, 0:chans] = cot_ref[t, h]
            s2_ref[t, h, :, 0:chans] = silu_slope(sec_ref[t, h])
            s1_ref[t, h, :, 0:chans] = silu_slope(fst_ref[t, h])

    def rows_out(top_a, top_b, low_a, low_b):
        def put(src, h, dst, at):
            for g, val in enumerate(group_frames([src[t, h] for t in range(frames)], chans)):
                dst[g, at] = val

        for r in range(3):
            put(cp_ref, r, top_a, r)
            put(cp_ref, rows - 3 + r, low_a, r)
        for r in range(2):
            put(s2_ref, r, top_b, r)
            put(s2_ref, rows - 2 + r, low_b, r)
        put(s1_ref, 0, top_b, 2)
        put(s1_ref, rows - 1, low_b, 2)

    @pl.when(par_ref[0] == 0)
    def _():
        rows_out(ha1, hb1, ha0, hb0)

    @pl.when(par_ref[0] != 0)
    def _():
        rows_out(ha0, hb0, ha1, hb1)

    def cols_out(left, right):
        sub = sub_of((SUB, LANES))
        for t in range(frames):
            for h in range(rows):
                last = pl.ds(cols - SUB, SUB)
                c7, a7, b7 = cp_ref[t, h, last], s2_ref[t, h, last], s1_ref[t, h, last]
                c0, a0, b0 = cp_ref[t, h, 0:SUB], s2_ref[t, h, 0:SUB], s1_ref[t, h, 0:SUB]
                right[t, h] = jnp.where(
                    sub >= 5, c7, jnp.where((sub == 2) | (sub == 3), roll(a7, 4, 0), jnp.where(sub == 1, roll(b7, 2, 0), 0.0))
                )
                left[t, h] = jnp.where(
                    sub < 3, c0, jnp.where((sub == 4) | (sub == 5), roll(a0, 4, 0), jnp.where(sub == 6, roll(b0, 6, 0), 0.0))
                )

    @pl.when(par_ref[1] == 0)
    def _():
        cols_out(wp1, wp0)

    @pl.when(par_ref[1] != 0)
    def _():
        cols_out(wp0, wp1)


def corner_kernel(par_ref, rw0, rw1, hc0, hc1, left, right):
    rows = rw0.shape[1]

    @pl.when(par_ref[1] == 0)
    def _():
        left[...] = rw1[...]
        right[...] = rw0[...]

    @pl.when(par_ref[1] != 0)
    def _():
        left[...] = rw0[...]
        right[...] = rw1[...]

    def out(top, low):
        for side, src in enumerate((left, right)):
            for r in range(3):
                top[:, r, side] = src[:, r]
                low[:, r, side] = src[:, rows - 3 + r]

    @pl.when(par_ref[0] == 0)
    def _():
        out(hc1, hc0)

    @pl.when(par_ref[0] != 0)
    def _():
        out(hc0, hc1)


def weight_kernel(w_ref, out_ref):
    chans = w_ref.shape[3]
    out_ref[...] = jnp.zeros(out_ref.shape, BF16)
    for k in range(3):
        for i in range(3):
            f0, f1, f2 = (w_ref[i, 2 - m, k] for m in range(3))
            even, odd = (f0 + f2) * (1 / 6), f1 * (1 / 6)
            far, odd2 = f0 * (1 / 24) + f2 * (1 / 6), f1 * (1 / 12)
            points = (f0 * 0.25, -even - odd, odd - even, far + odd2, far - odd2, f2)
            lanes = pl.ds((2 - i) * LANES, chans)
            for p, u in enumerate(points):
                high = u.astype(BF16)
                out_ref[p, k, 0, 0:chans, lanes] = high
                out_ref[p, k, 1, 0:chans, lanes] = (u - high.astype(F32)).astype(BF16)


def transform(rows, sizes, store):
    base = 0
    for tile, size in enumerate(sizes):
        if size == 4:
            x0, x1, x2, x3, x4, x5 = (rows(base + r) for r in range(6))
            a, b = x4 - 4.0 * x2, x3 - 4.0 * x1
            c, e = x4 - x2, 2.0 * (x3 - x1)
            points = ((4.0 * x0 - 5.0 * x2 + x4, 0), (a + b, 1), (a - b, 2), (c + e, 3), (c - e, 4),
                      (4.0 * x1 - 5.0 * x3 + x5, 5))
        else:
            x0, x1, x2, x3 = (rows(base + r) for r in range(4))
            points = ((4.0 * (x0 - x2), 0), (-3.0 * (x1 + x2), 1), (-3.0 * (x2 - x1), 2), (x3 - x1, 5))
        for value, point in points:
            store(point, tile, value)
        base += size


def conv(read, sizes, width, s_ref, y_ref, w_ref, emit):
    frames = 4
    chunk = 16

    def one(c, carry):
        start = pl.multiple_of(c * chunk, chunk)
        for t in range(frames):
            def store(point, tile, value):
                high = value.astype(BF16)
                low = (value - high.astype(F32)).astype(BF16)
                at = pl.ds(pl.multiple_of(tile * width + start, chunk), chunk)
                s_ref[point, at, t * LANES:(t + 1) * LANES] = high
                s_ref[point, at, (frames + t) * LANES:(frames + t + 1) * LANES] = low

            transform(lambda r: read(t, r, start, chunk), sizes, store)
        return carry

    lax.fori_loop(0, width // chunk, one, 0)

    zero = jnp.zeros((LANES, LANES), BF16)
    half = frames // 2 * LANES
    for p in range(6):
        tiles = sum(1 for size in sizes if size == 4 or p in (0, 1, 2, 5))
        m = tiles * width
        both, late = [], []
        for k in range(3):
            def stack(part):
                r = w_ref[p, k, part]
                return jnp.concatenate([jnp.concatenate([r, zero], 1), jnp.concatenate([zero, r], 1)], 0)

            def stack_late(part):
                r = w_ref[p, k, part]
                return jnp.concatenate([r[:, :2 * LANES], jnp.concatenate([zero, r[:, :LANES]], 1)], 0)

            both.append(jnp.concatenate([stack(0), stack(0), stack(1)], 1))
            late.append(jnp.concatenate([stack_late(0), stack_late(0), stack_late(1)], 1))
        lhs = s_ref[p, 0:m, :]
        high = lhs[:, :2 * half]
        late_high, late_low = lhs[:, half:2 * half], lhs[:, 3 * half:]
        for pair, (left, right) in enumerate((
            (jnp.concatenate([lhs, high], 1), jnp.concatenate(both, 0)),
            (jnp.concatenate([late_high, late_low, late_high], 1), jnp.concatenate(late, 0)),
        )):
            out = lax.dot_general(left, right, (((1,), (1,)), ((), ())), preferred_element_type=F32)
            two = 2 * LANES
            y_ref[pair, p, 0:m] = roll(out[:, :two], -1, 0) + out[:, two:2 * two] + roll(out[:, 2 * two:], 1, 0)

    base = 0
    for tile, size in enumerate(sizes):
        for pair in range(frames // 2):
            for side in range(2):
                lanes = pl.ds(side * LANES, LANES)
                y = {p: y_ref[pair, p, pl.ds(tile * width, width), lanes] for p in (range(6) if size == 4 else (0, 1, 2, 5))}
                plus, minus = y[1] + y[2], y[1] - y[2]
                t = 2 * pair + side
                if size == 4:
                    far, odd = y[3] + y[4], y[3] - y[4]
                    emit(t, base, y[0] + plus + far)
                    emit(t, base + 1, minus + 2.0 * odd)
                    emit(t, base + 2, plus + 4.0 * far)
                    emit(t, base + 3, minus + 8.0 * odd + y[5])
                else:
                    emit(t, base, y[0] + plus)
                    emit(t, base + 1, minus + y[5])
        base += size


def by_parity(par, even, odd, at):
    return jnp.where(par == 0, even[at], odd[at])


def third_kernel(chans, par_ref, cp_ref, ra0, ra1, left, right, rc0, rc1, w_ref, out_ref, x_ref, s_ref, y_ref):
    frames, rows, cols, _ = cp_ref.shape
    width = cols + 2 * SUB
    par = par_ref[0]
    sub = sub_of((SUB, LANES))

    def edges(t, r, lval, rval):
        x_ref[t, r, 0:SUB] = jnp.where(sub >= 5, lval, 0.0)
        x_ref[t, r, width - SUB:width] = jnp.where(sub < 3, rval, 0.0)

    for t in range(frames):
        for h in range(rows):
            x_ref[t, h + 3, SUB:SUB + cols] = cp_ref[t, h]
            edges(t, h + 3, left[t, h], right[t, h])
    for r in range(3):
        for at, even, odd, ceven, codd in ((r, ra1, ra0, rc1, rc0), (r + 3 + rows, ra0, ra1, rc0, rc1)):
            groups = [by_parity(par, even, odd, (g, r)) for g in range(3)]
            for t, frame in enumerate(ungroup_frames(groups, chans)):
                x_ref[t, at, SUB:SUB + cols] = frame
                edges(t, at, by_parity(par, ceven, codd, (t, r, 0)), by_parity(par, ceven, codd, (t, r, 1)))

    def emit(t, o, value):
        out_ref[t, o] = value

    conv(lambda t, r, start, n: x_ref[t, r, pl.ds(start, n)], (4, 4), width, s_ref, y_ref, w_ref, emit)


def last_kernel(chans, par_ref, g_ref, s2_ref, s1_ref, rb0, rb1, left, right, rc0, rc1, w2_ref, w1_ref, out_ref,
                e2_ref, e1_ref, x2_ref, x1_ref, s_ref, y_ref):
    frames, rows, cols, _ = s2_ref.shape
    width = cols + 2 * SUB
    par = par_ref[0]
    sub = sub_of((SUB, LANES))

    def edges2(t, r, lval, rval):
        e2_ref[t, r, 0:SUB] = jnp.where(sub >= 6, roll(lval, 4, 0), 0.0)
        e2_ref[t, r, width - SUB:width] = jnp.where(sub < 2, roll(rval, 4, 0), 0.0)

    def edges1(t, r, lval, rval):
        e1_ref[t, r, 0:SUB] = jnp.where(sub == 7, roll(lval, 6, 0), 0.0)
        e1_ref[t, r, width - SUB:width] = jnp.where(sub == 0, roll(rval, 2, 0), 0.0)

    for t in range(frames):
        for h in range(rows):
            e2_ref[t, h + 2, SUB:SUB + cols] = s2_ref[t, h]
            e1_ref[t, h + 1, SUB:SUB + cols] = s1_ref[t, h]
            edges2(t, h + 2, left[t, h], right[t, h])
            edges1(t, h + 1, left[t, h], right[t, h])
    for top, even, odd, ceven, codd in ((True, rb1, rb0, rc1, rc0), (False, rb0, rb1, rc0, rc1)):
        def corner(t, r, side):
            return by_parity(par, ceven, codd, (t, r, side))

        for r in range(3):
            groups = [by_parity(par, even, odd, (g, r)) for g in range(3)]
            for t, frame in enumerate(ungroup_frames(groups, chans)):
                if r < 2:
                    at, src = (r, r + 1) if top else (r + 2 + rows, r)
                    e2_ref[t, at, SUB:SUB + cols] = frame
                    edges2(t, at, corner(t, src, 0), corner(t, src, 1))
                else:
                    at, src = (0, 2) if top else (1 + rows, 0)
                    e1_ref[t, at, SUB:SUB + cols] = frame
                    edges1(t, at, corner(t, src, 0), corner(t, src, 1))

    def emit2(t, o, value):
        x1_ref[t, o] = value * e1_ref[t, o]

    def emit1(t, o, value):
        out_ref[t, o] = value[SUB:SUB + cols, 0:chans]

    def read2(t, r, start, n):
        return g_ref[t, r, pl.ds(start, n)] * e2_ref[t, r, pl.ds(start, n)]

    conv(read2, (4, 2), width, s_ref, y_ref, w2_ref, emit2)
    conv(lambda t, r, start, n: x1_ref[t, r, pl.ds(start, n)], (4,), width, s_ref, y_ref, w1_ref, emit1)


def swap(value, axis, which):
    count = lax.axis_size(axis)
    pairs = []
    for low in range(which, count - 1, 2):
        pairs += [(low, low + 1), (low + 1, low)]
    return lax.ppermute(value, axis, pairs)


def call(body, out_shape, args, scratch=(), vmem=40 << 20, flops=0, cost=0):
    return pl.pallas_call(
        body,
        out_shape=out_shape,
        in_specs=[SMEM_SPEC if a.dtype == jnp.int32 else VMEM_SPEC for a in args],
        out_specs=jax.tree.map(lambda _: VMEM_SPEC, out_shape),
        scratch_shapes=list(scratch),
        compiler_params=pltpu.CompilerParams(vmem_limit_bytes=vmem),
        cost_estimate=pl.CostEstimate(flops=flops, bytes_accessed=cost, transcendentals=0),
    )(*args)


def local(cotangent, stored_first, stored_second, w_first, w_second, w_third):
    frames, rows, cols, chans = cotangent.shape
    width = cols + 2 * SUB
    par = jnp.stack([lax.axis_index("ha") % 2, lax.axis_index("wa") % 2]).astype(jnp.int32)

    def arr(*shape, dtype=F32):
        return jax.ShapeDtypeStruct(shape, dtype)

    halo = arr(3, 3, cols, LANES)
    edge = arr(frames, rows, SUB, LANES)
    own = arr(frames, rows, cols, LANES)
    ha0, ha1, hb0, hb1, wp0, wp1, cp, s2, s1 = call(
        pack_kernel, (halo, halo, halo, halo, edge, edge, own, own, own), (par, cotangent, stored_second, stored_first)
    )
    ra1, ra0 = swap(ha1, "ha", 1), swap(ha0, "ha", 0)
    rw1, rw0 = swap(wp1, "wa", 1), swap(wp0, "wa", 0)
    rb1, rb0 = swap(hb1, "ha", 1), swap(hb0, "ha", 0)
    corner = arr(frames, 3, 2, SUB, LANES)
    hc0, hc1, left, right = call(corner_kernel, (corner, corner, edge, edge), (par, rw0, rw1))
    rc1, rc0 = swap(hc1, "ha", 1), swap(hc0, "ha", 0)

    weights = arr(6, 3, 2, LANES, 3 * LANES, dtype=BF16)
    u3, u2, u1 = (call(weight_kernel, weights, (w,)) for w in (w_third, w_second, w_first))

    scratch = [pltpu.VMEM((6, 2 * width, 2 * frames * LANES), BF16), pltpu.VMEM((2, 6, 2 * width, 2 * LANES), F32)]
    grad = call(
        functools.partial(third_kernel, chans),
        arr(frames, rows + 4, width, LANES),
        (par, cp, ra0, ra1, left, right, rc0, rc1, u3),
        [pltpu.VMEM((frames, rows + 6, width, LANES), F32)] + scratch,
    )
    return call(
        functools.partial(last_kernel, chans),
        arr(frames, rows, cols, chans),
        (par, grad, s2, s1, rb0, rb1, left, right, rc0, rc1, u2, u1),
        [
            pltpu.VMEM((frames, rows + 4, width, LANES), F32),
            pltpu.VMEM((frames, rows + 2, width, LANES), F32),
            pltpu.VMEM((frames, rows + 4, width, LANES), F32),
            pltpu.VMEM((frames, rows + 2, width, LANES), F32),
        ]
        + scratch,
    )


def solution(mesh):
    in_specs = (
        P("clip", "ha", "wa", None),
        P("clip", "ha", "wa", None),
        P("clip", "ha", "wa", None),
        P(),
        P(),
        P(),
    )
    out_specs = P("clip", "ha", "wa", None)
    return jax.shard_map(local, mesh=mesh, in_specs=in_specs, out_specs=out_specs, check_vma=False)
```

profile of v0, /device:TPU:10, one launch (start us, length us, event | category | flops | bytes accessed | tf_op | source)
XLA Modules:
  0.0 54.6 jit_solution(15375283203856843035)
XLA Ops:
  0.0 0.1 pad_add_fusion.par_ref
  0.1 1.1 %copy-done.3 = f32[4,4,64,96]{3,2,1,0:T(8,128)S(1)} copy-done((f32[4,4,64,96]{3,2,1,0:T(8,128)S(1)}, f32[4,4,64,96]{3,2,1,0:T(8,128)}, u32[]{:S(2)}) %copy-start.3) | copy-done | bytes 393240
  1.2 1.0 %copy-done.4 = f32[4,4,64,96]{3,2,1,0:T(8,128)S(1)} copy-done((f32[4,4,64,96]{3,2,1,0:T(8,128)S(1)}, f32[4,4,64,96]{3,2,1,0:T(8,128)}, u32[]{:S(2)}) %copy-start.4) | copy-done | bytes 393240
  2.3 1.0 %copy-done.5 = f32[4,4,64,96]{3,2,1,0:T(8,128)S(1)} copy-done((f32[4,4,64,96]{3,2,1,0:T(8,128)S(1)}, f32[4,4,64,96]{3,2,1,0:T(8,128)}, u32[]{:S(2)}) %copy-start.5) | copy-done | bytes 393240
  3.3 1.4 %shard_map.64 = (f32[3,3,64,128]{3,2,1,0:T(8,128)S(1)}, f32[3,3,64,128]{3,2,1,0:T(8,128)S(1)}, f32[3,3,64,128]{3,2,1,0:T(8,128)S(1)}, f32[3,3,64,128]{3,2,1,0:T(...) custom-call(s32[2]{0:T(128)S(1)} %pad_add_fusion.par_ref, ...), custom_call_target="tpu_custom_call" | custom-call | tf_op jit(solution)/shard_map/pallas_call | solution.py:331
  4.7 0.1 collective-permute-start.2
  4.8 0.5 collective-permute-start
  5.3 4.6 %collective-permute-start.1 = (f32[3,3,64,128]{3,2,1,0:T(8,128)S(1)}, f32[3,3,64,128]{3,2,1,0:T(8,128)S(1)}, u32[]{:S(2)}, u32[]{:S(2)}) collective-permute-start(f32[3,3,64,128]{3,2,1,0:T(8,128)S(1)} %get-tuple-element.20), channel_id=1, source_target_pairs={{4,8},{8,4},{5,9},{9,5},{6,10},{10,6},{7,11},{11,7},{20,24},{24,20... | collective-permute-start | bytes 884744 | tf_op jit(solution)/shard_map/ppermute | solution.py:327
  9.9 0.1 collective-permute-start.6
  10.0 1.9 %collective-permute-start.7 = (f32[3,3,64,128]{3,2,1,0:T(8,128)S(1)}, f32[3,3,64,128]{3,2,1,0:T(8,128)S(1)}, u32[]{:S(2)}, u32[]{:S(2)}) collective-permute-start(f32[3,3,64,128]{3,2,1,0:T(8,128)S(1)} %get-tuple-element.30), channel_id=1, source_target_pairs={{4,8},{8,4},{5,9},{9,5},{6,10},{10,6},{7,11},{11,7},{20,24},{24,20... | collective-permute-start | bytes 884744 | tf_op jit(solution)/shard_map/ppermute | solution.py:327
  11.9 1.9 %collective-permute-start.3 = (f32[4,4,8,128]{3,2,1,0:T(8,128)S(1)}, f32[4,4,8,128]{3,2,1,0:T(8,128)S(1)}, u32[]{:S(2)}, u32[]{:S(2)}) collective-permute-start(f32[4,4,8,128]{3,2,1,0:T(8,128)S(1)} %get-tuple-element.22), channel_id=1, source_target_pairs={{1,2},{2,1},{5,6},{6,5},{9,10},{10,9},{13,14},{14,13},{17,18},{18,... | collective-permute-start | bytes 196616 | tf_op jit(solution)/shard_map/ppermute | solution.py:327
  13.8 3.7 %collective-permute-done.3.rw1 = f32[4,4,8,128]{3,2,1,0:T(8,128)S(1)} collective-permute-done((f32[4,4,8,128]{3,2,1,0:T(8,128)S(1)}, f32[4,4,8,128]{3,2,1,0:T(8,128)S(1)}, u32[]{:S(2)}, u32[]{:S(2)}) %collective-permute-start.3) | collective-permute-done | bytes 65568 | tf_op jit(solution)/shard_map/ppermute | solution.py:327
  17.5 0.6 %shard_map.65 = (f32[4,3,2,8,128]{4,3,2,1,0:T(8,128)S(1)}, f32[4,3,2,8,128]{4,3,2,1,0:T(8,128)S(1)}, f32[4,4,8,128]{3,2,1,0:T(8,128)S(1)}, f32[4,4,8,128]{3,2,1,0:T(8,128)S(1)}) custom-call(s32[2]{0:T(128)S(1)} %pad_add_fusion.par_ref, f32[4,4,8,128]{3,2,1,0:T(8,128)S(1)} %collective-permute-done.2.rw0, f32[4,4,8,128]{3,2,1,0:T(8,128)S(1)} %collective-permute-done.3.rw1), custom_call_target="tpu_custom_call" | custom-call | tf_op jit(solution)/shard_map/pallas_call | solution.py:331
  18.1 0.8 %collective-permute-start.4 = (f32[4,3,2,8,128]{4,3,2,1,0:T(8,128)S(1)}, f32[4,3,2,8,128]{4,3,2,1,0:T(8,128)S(1)}, u32[]{:S(2)}, u32[]{:S(2)}) collective-permute-start(f32[4,3,2,8,128]{4,3,2,1,0:T(8,128)S(1)} %get-tuple-element.25), channel_id=1, source_target_pairs={{0,4},{4,0},{8,12},{12,8},{1,5},{5,1},{9,13},{13,9},{2,6},{6,2},{1... | collective-permute-start | bytes 294920 | tf_op jit(solution)/shard_map/ppermute | solution.py:327
  18.9 3.9 %collective-permute-done.4.rc0 = f32[4,3,2,8,128]{4,3,2,1,0:T(8,128)S(1)} collective-permute-done((f32[4,3,2,8,128]{4,3,2,1,0:T(8,128)S(1)}, f32[4,3,2,8,128]{4,3,2,1,0:T(8,128)S(1)}, u32[]{:S(2)}, u32[]{:S(2)}) %collective-permute-start.4) | collective-permute-done | bytes 98336 | tf_op jit(solution)/shard_map/ppermute | solution.py:327
  22.8 4.0 %collective-permute-start.5 = (f32[4,3,2,8,128]{4,3,2,1,0:T(8,128)S(1)}, f32[4,3,2,8,128]{4,3,2,1,0:T(8,128)S(1)}, u32[]{:S(2)}, u32[]{:S(2)}) collective-permute-start(f32[4,3,2,8,128]{4,3,2,1,0:T(8,128)S(1)} %get-tuple-element.26), channel_id=1, source_target_pairs={{4,8},{8,4},{5,9},{9,5},{6,10},{10,6},{7,11},{11,7},{20,24},{24,20... | collective-permute-start | bytes 294920 | tf_op jit(solution)/shard_map/ppermute | solution.py:327
  26.8 0.9 %shard_map.66.w_ref = bf16[6,3,2,128,384]{4,3,2,1,0:T(8,128)(2,1)S(1)} custom-call(f32[3,3,3,96,96]{4,3,2,1,0:T(8,128)S(1)} %copy-done), custom_call_target="tpu_custom_call" | custom-call | tf_op jit(solution)/shard_map/pallas_call | solution.py:331
  27.8 0.0 copy-start.2
  27.8 0.9 %shard_map.68.w2_ref = bf16[6,3,2,128,384]{4,3,2,1,0:T(8,128)(2,1)S(1)} custom-call(f32[3,3,3,96,96]{4,3,2,1,0:T(8,128)S(1)} %copy-done.1), custom_call_target="tpu_custom_call" | custom-call | tf_op jit(solution)/shard_map/pallas_call | solution.py:331
  28.8 0.4 copy-done.2
  29.1 0.9 %shard_map.69.w1_ref = bf16[6,3,2,128,384]{4,3,2,1,0:T(8,128)(2,1)S(1)} custom-call(f32[3,3,3,96,96]{4,3,2,1,0:T(8,128)S(1)} %copy-done.2), custom_call_target="tpu_custom_call" | custom-call | tf_op jit(solution)/shard_map/pallas_call | solution.py:331
  30.1 0.0 collective-permute-done.5.rc1
  30.1 8.6 %shard_map.67.g_ref = f32[4,8,80,128]{3,2,1,0:T(8,128)S(1)} custom-call(s32[2]{0:T(128)S(1)} %pad_add_fusion.par_ref, f32[4,4,64,128]{3,2,1,0:T(8,128)S(1)} %get-tuple-element.18.cp_ref, f32[3,3,64,128]{3,2,1,0:T(8,128)S(1)} %collective-permute-done.ra0, f32[3,3,64,128]{3,2,1,0:T(8,128)S(1)} %collective-permute-done.1.ra1, ...), custom_call_target="tpu_custom_call" | custom-call | tf_op jit(solution)/shard_map/pallas_call | solution.py:331
  38.8 15.8 %shard_map.70 = f32[4,4,64,96]{3,2,1,0:T(8,128)} custom-call(s32[2]{0:T(128)S(1)} %pad_add_fusion.par_ref, f32[4,8,80,128]{3,2,1,0:T(8,128)S(1)} %shard_map.67.g_ref, f32[4,4,64,128]{3,2,1,0:T(8,128)S(1)} %get-tuple-element.27.s2_ref, f32[4,4,64,128]{3,2,1,0:T(8,128)S(1)} %get-tuple-element.28.s1_ref, f32[3,3,64,128]{3,2,1,0:T(8,128)S(1)} %collective-permute-done.6.rb0, ...), custom_call_target="tpu_custom_call" | custom-call | tf_op jit(solution)/shard_map/pallas_call | solution.py:331
  (12 shorter events, 0.0 us)
Async XLA Ops:
  0.0 26.8 %copy-start = (f32[3,3,3,96,96]{4,3,2,1,0:T(8,128)S(1)}, f32[3,3,3,96,96]{4,3,2,1,0:T(8,128)}, u32[]{:S(2)}) copy-start(f32[3,3,3,96,96]{4,3,2,1,0:T(8,128)} %w_ref.3) | copy-start | bytes 2985988
  0.1 1.1 %copy-start.3 = (f32[4,4,64,96]{3,2,1,0:T(8,128)S(1)}, f32[4,4,64,96]{3,2,1,0:T(8,128)}, u32[]{:S(2)}) copy-start(f32[4,4,64,96]{3,2,1,0:T(8,128)} %cot_ref.1) | copy-start | bytes 1179652
  1.2 1.0 %copy-start.4 = (f32[4,4,64,96]{3,2,1,0:T(8,128)S(1)}, f32[4,4,64,96]{3,2,1,0:T(8,128)}, u32[]{:S(2)}) copy-start(f32[4,4,64,96]{3,2,1,0:T(8,128)} %sec_ref.1) | copy-start | bytes 1179652
  2.3 1.0 %copy-start.5 = (f32[4,4,64,96]{3,2,1,0:T(8,128)S(1)}, f32[4,4,64,96]{3,2,1,0:T(8,128)}, u32[]{:S(2)}) copy-start(f32[4,4,64,96]{3,2,1,0:T(8,128)} %fst_ref.1) | copy-start | bytes 1179652
  4.7 7.2 %collective-permute-start.2 = (f32[4,4,8,128]{3,2,1,0:T(8,128)S(1)}, f32[4,4,8,128]{3,2,1,0:T(8,128)S(1)}, u32[]{:S(2)}, u32[]{:S(2)}) collective-permute-start(f32[4,4,8,128]{3,2,1,0:T(8,128)S(1)} %get-tuple-element.21), channel_id=1, source_target_pairs={{0,1},{1,0},{2,3},{3,2},{4,5},{5,4},{6,7},{7,6},{8,9},{9,8},{10,11... | collective-permute-start | bytes 196616 | tf_op jit(solution)/shard_map/ppermute | solution.py:327
  4.8 25.3 %collective-permute-start = (f32[3,3,64,128]{3,2,1,0:T(8,128)S(1)}, f32[3,3,64,128]{3,2,1,0:T(8,128)S(1)}, u32[]{:S(2)}, u32[]{:S(2)}) collective-permute-start(f32[3,3,64,128]{3,2,1,0:T(8,128)S(1)} %get-tuple-element.19), channel_id=1, source_target_pairs={{0,4},{4,0},{8,12},{12,8},{1,5},{5,1},{9,13},{13,9},{2,6},{6,2},{1... | collective-permute-start | bytes 884744 | tf_op jit(solution)/shard_map/ppermute | solution.py:327
  5.3 24.8 %collective-permute-start.1 = (f32[3,3,64,128]{3,2,1,0:T(8,128)S(1)}, f32[3,3,64,128]{3,2,1,0:T(8,128)S(1)}, u32[]{:S(2)}, u32[]{:S(2)}) collective-permute-start(f32[3,3,64,128]{3,2,1,0:T(8,128)S(1)} %get-tuple-element.20), channel_id=1, source_target_pairs={{4,8},{8,4},{5,9},{9,5},{6,10},{10,6},{7,11},{11,7},{20,24},{24,20... | collective-permute-start | bytes 884744 | tf_op jit(solution)/shard_map/ppermute | solution.py:327
  9.9 28.8 %collective-permute-start.6 = (f32[3,3,64,128]{3,2,1,0:T(8,128)S(1)}, f32[3,3,64,128]{3,2,1,0:T(8,128)S(1)}, u32[]{:S(2)}, u32[]{:S(2)}) collective-permute-start(f32[3,3,64,128]{3,2,1,0:T(8,128)S(1)} %get-tuple-element.29), channel_id=1, source_target_pairs={{0,4},{4,0},{8,12},{12,8},{1,5},{5,1},{9,13},{13,9},{2,6},{6,2},{1... | collective-permute-start | bytes 884744 | tf_op jit(solution)/shard_map/ppermute | solution.py:327
  10.0 28.8 %collective-permute-start.7 = (f32[3,3,64,128]{3,2,1,0:T(8,128)S(1)}, f32[3,3,64,128]{3,2,1,0:T(8,128)S(1)}, u32[]{:S(2)}, u32[]{:S(2)}) collective-permute-start(f32[3,3,64,128]{3,2,1,0:T(8,128)S(1)} %get-tuple-element.30), channel_id=1, source_target_pairs={{4,8},{8,4},{5,9},{9,5},{6,10},{10,6},{7,11},{11,7},{20,24},{24,20... | collective-permute-start | bytes 884744 | tf_op jit(solution)/shard_map/ppermute | solution.py:327
  11.9 5.6 %collective-permute-start.3 = (f32[4,4,8,128]{3,2,1,0:T(8,128)S(1)}, f32[4,4,8,128]{3,2,1,0:T(8,128)S(1)}, u32[]{:S(2)}, u32[]{:S(2)}) collective-permute-start(f32[4,4,8,128]{3,2,1,0:T(8,128)S(1)} %get-tuple-element.22), channel_id=1, source_target_pairs={{1,2},{2,1},{5,6},{6,5},{9,10},{10,9},{13,14},{14,13},{17,18},{18,... | collective-permute-start | bytes 196616 | tf_op jit(solution)/shard_map/ppermute | solution.py:327
  18.1 4.7 %collective-permute-start.4 = (f32[4,3,2,8,128]{4,3,2,1,0:T(8,128)S(1)}, f32[4,3,2,8,128]{4,3,2,1,0:T(8,128)S(1)}, u32[]{:S(2)}, u32[]{:S(2)}) collective-permute-start(f32[4,3,2,8,128]{4,3,2,1,0:T(8,128)S(1)} %get-tuple-element.25), channel_id=1, source_target_pairs={{0,4},{4,0},{8,12},{12,8},{1,5},{5,1},{9,13},{13,9},{2,6},{6,2},{1... | collective-permute-start | bytes 294920 | tf_op jit(solution)/shard_map/ppermute | solution.py:327
  22.8 5.0 %copy-start.1 = (f32[3,3,3,96,96]{4,3,2,1,0:T(8,128)S(1)}, f32[3,3,3,96,96]{4,3,2,1,0:T(8,128)}, u32[]{:S(2)}) copy-start(f32[3,3,3,96,96]{4,3,2,1,0:T(8,128)} %w_ref.4) | copy-start | bytes 2985988
  22.8 7.3 %collective-permute-start.5 = (f32[4,3,2,8,128]{4,3,2,1,0:T(8,128)S(1)}, f32[4,3,2,8,128]{4,3,2,1,0:T(8,128)S(1)}, u32[]{:S(2)}, u32[]{:S(2)}) collective-permute-start(f32[4,3,2,8,128]{4,3,2,1,0:T(8,128)S(1)} %get-tuple-element.26), channel_id=1, source_target_pairs={{4,8},{8,4},{5,9},{9,5},{6,10},{10,6},{7,11},{11,7},{20,24},{24,20... | collective-permute-start | bytes 294920 | tf_op jit(solution)/shard_map/ppermute | solution.py:327
  27.8 1.3 %copy-start.2 = (f32[3,3,3,96,96]{4,3,2,1,0:T(8,128)S(1)}, f32[3,3,3,96,96]{4,3,2,1,0:T(8,128)}, u32[]{:S(2)}) copy-start(f32[3,3,3,96,96]{4,3,2,1,0:T(8,128)} %w_ref.5) | copy-start | bytes 2985988
where the time goes:
time: 54.9 us; the launch traced here: 54.6 us
  Pallas kernels  29.3 us (53%)
  starting transfers between devices  14 us (26%)
  waiting for transfers between devices  7.53 us (14%)
  local copies, waits for them, and re-layouts  3.58 us (7%)
    pallas_call x7, Pallas kernels, call(): pl.pallas_call(body, out_shape=out_shape, in_specs=[SMEM_SPEC if a.dtype...  29.3 us
    ppermute x8, starting transfers between devices, swap(): return lax.ppermute(value, axis, pairs)  14 us
    ppermute x8, waiting for transfers between devices, swap(): return lax.ppermute(value, axis, pairs)  7.53 us
    unnamed x12, local copies, waits for them, and re-layouts  3.58 us
  transfers between devices with their start and end apart: 8, of which 2 were waited for; matrix products, arithmetic and copies ran while one was open for 0% of the time, Pallas kernels for 22%

commit v1 on v0

v1 whole, which is shorter than its diff:
```python
import functools

import jax
import jax.numpy as jnp
from jax import lax
from jax.experimental import pallas as pl
from jax.experimental.pallas import tpu as pltpu
from jax.sharding import PartitionSpec as P

LANES = 128
SUB = 8
F32 = jnp.float32
BF16 = jnp.bfloat16
VMEM_SPEC = pl.BlockSpec(memory_space=pltpu.VMEM)
SMEM_SPEC = pl.BlockSpec(memory_space=pltpu.SMEM)


def silu_slope(value):
    sigma = 1.0 / (1.0 + jnp.exp(-value))
    return sigma * (1.0 + value * (1.0 - sigma))


def roll(value, shift, axis):
    return pltpu.roll(value, shift % value.shape[axis], axis)


def lane_of(shape):
    return lax.broadcasted_iota(jnp.int32, shape, len(shape) - 1)


def sub_of(shape):
    return lax.broadcasted_iota(jnp.int32, shape, len(shape) - 2)


def group_frames(frames, chans):
    first, second, third, fourth = frames
    part = LANES - chans
    lane = lane_of(first.shape)
    packed = []
    for index, frame in enumerate((first, second, third)):
        packed.append(jnp.where(lane < chans, frame, roll(fourth, chans - part * index, 1)))
    return packed


def ungroup_frames(groups, chans):
    part = LANES - chans
    lane = lane_of(groups[0].shape)
    frames = [jnp.where(lane < chans, group, 0.0) for group in groups]
    fourth = jnp.zeros_like(groups[0])
    for index in reversed(range(3)):
        moved = roll(groups[index], part * (index + 1), 1)
        fourth = jnp.where(lane < part * (index + 1), moved, fourth)
    return frames + [jnp.where(lane < chans, fourth, 0.0)]


def edge_kernel(par_ref, cot_hbm, sec_hbm, fst_hbm, wp0, wp1, raw_ref, pad_ref, sems):
    frames, rows, cols, chans = cot_hbm.shape
    copies = []
    for a, src in enumerate((cot_hbm, sec_hbm, fst_hbm)):
        for side, start in enumerate((0, cols - SUB)):
            copies.append(
                pltpu.make_async_copy(src.at[:, :, pl.ds(start, SUB), :], raw_ref.at[a, side], sems.at[a, side])
            )
            copies[-1].start()
    pad_ref[...] = jnp.zeros(pad_ref.shape, F32)
    for copy in copies:
        copy.wait()
    pad_ref[0, :, :, :, :, 0:chans] = raw_ref[0]
    pad_ref[1:3, :, :, :, :, 0:chans] = silu_slope(raw_ref[1:3])

    def cols_out(left, right):
        sub = sub_of((SUB, LANES))
        for t in range(frames):
            for h in range(rows):
                c0, a0, b0 = (pad_ref[a, 0, t, h] for a in range(3))
                c7, a7, b7 = (pad_ref[a, 1, t, h] for a in range(3))
                right[t, h] = jnp.where(
                    sub >= 5, c7, jnp.where((sub == 2) | (sub == 3), roll(a7, 4, 0), jnp.where(sub == 1, roll(b7, 2, 0), 0.0))
                )
                left[t, h] = jnp.where(
                    sub < 3, c0, jnp.where((sub == 4) | (sub == 5), roll(a0, 4, 0), jnp.where(sub == 6, roll(b0, 6, 0), 0.0))
                )

    @pl.when(par_ref[1] == 0)
    def _():
        cols_out(wp1, wp0)

    @pl.when(par_ref[1] != 0)
    def _():
        cols_out(wp0, wp1)


def put_rows(read_cot, read_s2, read_s1, rows, top_a, top_b, low_a, low_b, span, chans):
    def put(read, h, dst, at):
        for g, val in enumerate(group_frames([read(t, h) for t in range(4)], chans)):
            dst[g, at, span] = val

    for r in range(3):
        put(read_cot, r, top_a, r)
        put(read_cot, rows - 3 + r, low_a, r)
    for r in range(2):
        put(read_s2, r, top_b, r)
        put(read_s2, rows - 2 + r, low_b, r)
    put(read_s1, 0, top_b, 2)
    put(read_s1, rows - 1, low_b, 2)


def pack_kernel(par_ref, cot_ref, sec_ref, fst_ref, ma0, ma1, mb0, mb1, cp_ref, s2_ref, s1_ref):
    frames, rows, cols, chans = cot_ref.shape
    blank = jnp.zeros((cols, LANES), F32)
    for t in range(frames):
        for h in range(rows):
            for ref, val in ((cp_ref, cot_ref[t, h]), (s2_ref, silu_slope(sec_ref[t, h])), (s1_ref, silu_slope(fst_ref[t, h]))):
                ref[t, h] = blank
                ref[t, h, :, 0:chans] = val

    def rows_out(*dst):
        reads = [lambda t, h, ref=ref: ref[t, h] for ref in (cp_ref, s2_ref, s1_ref)]
        put_rows(*reads, rows, *dst, slice(0, cols), chans)

    @pl.when(par_ref[0] == 0)
    def _():
        rows_out(ma1, mb1, ma0, mb0)

    @pl.when(par_ref[0] != 0)
    def _():
        rows_out(ma0, mb0, ma1, mb1)


def corner_kernel(chans, par_ref, rw0, rw1, _a0, _a1, _b0, _b1, ma0, ma1, mb0, mb1, cc, c2, c1):
    frames, rows = rw0.shape[:2]
    cols = ma0.shape[2] - SUB
    even = par_ref[1] == 0
    sub = sub_of((SUB, LANES))
    for t in range(frames):
        for h in range(rows):
            left = jnp.where(even, rw1[t, h], rw0[t, h])
            right = jnp.where(even, rw0[t, h], rw1[t, h])
            cc[t, h] = jnp.where(sub < 3, right, jnp.where(sub >= 5, left, 0.0))
            c2[t, h] = jnp.where(sub < 2, roll(right, 4, 0), jnp.where(sub >= 6, roll(left, 4, 0), 0.0))
            c1[t, h] = jnp.where(sub == 0, roll(right, 2, 0), jnp.where(sub == 7, roll(left, 6, 0), 0.0))

    def rows_out(*dst):
        reads = [lambda t, h, ref=ref: ref[t, h] for ref in (cc, c2, c1)]
        put_rows(*reads, rows, *dst, slice(cols, cols + SUB), chans)

    @pl.when(par_ref[0] == 0)
    def _():
        rows_out(ma1, mb1, ma0, mb0)

    @pl.when(par_ref[0] != 0)
    def _():
        rows_out(ma0, mb0, ma1, mb1)


def weight_kernel(w_ref, out_ref):
    chans = w_ref.shape[3]
    out_ref[...] = jnp.zeros(out_ref.shape, BF16)
    for k in range(3):
        for i in range(3):
            f0, f1, f2 = (w_ref[i, 2 - m, k] for m in range(3))
            even, odd = (f0 + f2) * (1 / 6), f1 * (1 / 6)
            far, odd2 = f0 * (1 / 24) + f2 * (1 / 6), f1 * (1 / 12)
            points = (f0 * 0.25, -even - odd, odd - even, far + odd2, far - odd2, f2)
            lanes = pl.ds((2 - i) * LANES, chans)
            for p, u in enumerate(points):
                high = u.astype(BF16)
                out_ref[p, k, 0, 0:chans, lanes] = high
                out_ref[p, k, 1, 0:chans, lanes] = (u - high.astype(F32)).astype(BF16)


def transform(rows, sizes, store):
    base = 0
    for tile, size in enumerate(sizes):
        if size == 4:
            x0, x1, x2, x3, x4, x5 = (rows(base + r) for r in range(6))
            a, b = x4 - 4.0 * x2, x3 - 4.0 * x1
            c, e = x4 - x2, 2.0 * (x3 - x1)
            points = ((4.0 * x0 - 5.0 * x2 + x4, 0), (a + b, 1), (a - b, 2), (c + e, 3), (c - e, 4),
                      (4.0 * x1 - 5.0 * x3 + x5, 5))
        else:
            x0, x1, x2, x3 = (rows(base + r) for r in range(4))
            points = ((4.0 * (x0 - x2), 0), (-3.0 * (x1 + x2), 1), (-3.0 * (x2 - x1), 2), (x3 - x1, 5))
        for value, point in points:
            store(point, tile, value)
        base += size


def right_operands(w_ref, p):
    zero = jnp.zeros((LANES, LANES), BF16)
    near, far = [], []
    for k in range(3):
        parts = [w_ref[p, k, part] for part in range(2)]
        own = [
            jnp.concatenate([r[:, : 2 * LANES], jnp.concatenate([zero, r[:, :LANES]], 1)], 0) for r in parts
        ]
        later = [
            jnp.concatenate([jnp.concatenate([r[:, 2 * LANES :], zero], 1), r[:, LANES:]], 0) for r in parts
        ]
        near.append(jnp.concatenate([own[0], own[0], own[1]], 1))
        far.append(jnp.concatenate([later[0], later[0], later[1]], 1))
    return jnp.concatenate(near, 0), jnp.concatenate(far, 0)


def product(left, right):
    left = jnp.concatenate([left, left[:, : 2 * LANES]], 1)
    return lax.dot_general(left, right, (((1,), (1,)), ((), ())), preferred_element_type=F32)


def shifted_sum(taps):
    two = 2 * LANES
    return roll(taps[:, :two], -1, 0) + taps[:, two : 2 * two] + roll(taps[:, 2 * two :], 1, 0)


def conv(read, sizes, width, s_ref, y_ref, w_ref, emit):
    chunks = width // SUB

    def tiles_of(p):
        return [n for n, size in enumerate(sizes) if size == 4 or p in (0, 1, 2, 5)]

    def one(c, carry):
        at = pl.ds(pl.multiple_of(c * SUB, SUB), SUB)
        for a in range(2):
            found = {}
            for pair in range(2):
                def store(point, tile, value):
                    found[pair, point, tile] = value

                transform(lambda r: read(2 * pair + a, r, at), sizes, store)
            for p in range(6):
                tiles = tiles_of(p)
                if len(tiles) == 2:
                    blocks = [jnp.concatenate([found[pair, p, n] for n in tiles], 0) for pair in range(2)]
                else:
                    blocks = [jnp.concatenate([found[pair, p, tiles[0]] for pair in range(2)], 0)]
                for n, value in enumerate(blocks):
                    high = value.astype(BF16)
                    s_ref[p, c, n, :, a * LANES : (a + 1) * LANES] = high
                    s_ref[p, c, n, :, (2 + a) * LANES : (3 + a) * LANES] = (value - high.astype(F32)).astype(BF16)
        return carry

    lax.fori_loop(0, chunks, one, 0)

    wide = 4 * LANES
    for p in range(6):
        near, far = right_operands(w_ref, p)
        tiles = tiles_of(p)
        if len(tiles) == 2:
            own = product(s_ref[p].reshape(chunks * 4 * SUB, wide), near).reshape(chunks, 2, 2, SUB, 6 * LANES)
            later = product(s_ref[p, :, 1].reshape(chunks * 2 * SUB, wide), far).reshape(chunks, 2, SUB, 6 * LANES)
            for n in tiles:
                y_ref[0, p, n] = shifted_sum((own[:, 0, n] + later[:, n]).reshape(width, 6 * LANES))
                y_ref[1, p, n] = shifted_sum(own[:, 1, n].reshape(width, 6 * LANES))
        else:
            lhs = s_ref[p, :, 0].reshape(chunks * 2 * SUB, wide)
            own = product(lhs, near).reshape(chunks, 2, SUB, 6 * LANES)
            later = product(lhs, far).reshape(chunks, 2, SUB, 6 * LANES)
            y_ref[0, p, tiles[0]] = shifted_sum((own[:, 0] + later[:, 1]).reshape(width, 6 * LANES))
            y_ref[1, p, tiles[0]] = shifted_sum(own[:, 1].reshape(width, 6 * LANES))

    base = 0
    for tile, size in enumerate(sizes):
        for t in range(4):
            lanes = pl.ds(t % 2 * LANES, LANES)
            y = {p: y_ref[t // 2, p, tile, :, lanes] for p in (range(6) if size == 4 else (0, 1, 2, 5))}
            plus, minus = y[1] + y[2], y[1] - y[2]
            if size == 4:
                far, odd = y[3] + y[4], y[3] - y[4]
                emit(t, base, y[0] + plus + far)
                emit(t, base + 1, minus + 2.0 * odd)
                emit(t, base + 2, plus + 4.0 * far)
                emit(t, base + 3, minus + 8.0 * odd + y[5])
            else:
                emit(t, base, y[0] + plus)
                emit(t, base + 1, minus + y[5])
        base += size


def halo_rows(chans, par, from_even, from_odd, r):
    return ungroup_frames([jnp.where(par == 0, from_even[g, r], from_odd[g, r]) for g in range(3)], chans)


def third_kernel(chans, par_ref, cp_ref, cc_ref, ra0, ra1, w_ref, out_ref, x_ref, s_ref, y_ref):
    frames, rows, cols, _ = cp_ref.shape
    width = cols + SUB
    par = par_ref[0]
    x_ref[:, 3 : 3 + rows, 0:cols] = cp_ref[...]
    x_ref[:, 3 : 3 + rows, cols:width] = cc_ref[...]
    for r in range(3):
        for at, even, odd in ((r, ra1, ra0), (r + 3 + rows, ra0, ra1)):
            for t, frame in enumerate(halo_rows(chans, par, even, odd, r)):
                x_ref[t, at] = frame

    def emit(t, o, value):
        out_ref[t, o] = value

    conv(lambda t, r, at: x_ref[t, r, at], (4, 4), width, s_ref, y_ref, w_ref, emit)


def last_kernel(chans, par_ref, g_ref, s2_ref, c2_ref, s1_ref, c1_ref, rb0, rb1, w2_ref, w1_ref, out_ref,
                e2_ref, e1_ref, x1_ref, s_ref, y_ref):
    frames, rows, cols, _ = s2_ref.shape
    width = cols + SUB
    par = par_ref[0]
    for e_ref, s_own, c_own, n in ((e2_ref, s2_ref, c2_ref, 2), (e1_ref, s1_ref, c1_ref, 1)):
        e_ref[:, n : n + rows, 0:cols] = s_own[...]
        e_ref[:, n : n + rows, cols:width] = c_own[...]
    for r in range(3):
        for top, even, odd in ((True, rb1, rb0), (False, rb0, rb1)):
            for t, frame in enumerate(halo_rows(chans, par, even, odd, r)):
                if r < 2:
                    e2_ref[t, r if top else r + 2 + rows] = frame
                else:
                    e1_ref[t, 0 if top else 1 + rows] = frame

    def emit2(t, o, value):
        x1_ref[t, o] = value * e1_ref[t, o]

    def emit1(t, o, value):
        out_ref[t, o] = value[0:cols, 0:chans]

    conv(lambda t, r, at: g_ref[t, r, at] * e2_ref[t, r, at], (4, 2), width, s_ref, y_ref, w2_ref, emit2)
    conv(lambda t, r, at: x1_ref[t, r, at], (4,), width, s_ref, y_ref, w1_ref, emit1)


def swap(value, axis, which):
    count = lax.axis_size(axis)
    pairs = []
    for low in range(which, count - 1, 2):
        pairs += [(low, low + 1), (low + 1, low)]
    return lax.ppermute(value, axis, pairs)


def call(body, out_shape, args, scratch=(), hbm=False, alias=None, vmem=40 << 20, flops=0, cost=0):
    where = pl.BlockSpec(memory_space=pltpu.HBM) if hbm else VMEM_SPEC
    return pl.pallas_call(
        body,
        out_shape=out_shape,
        in_specs=[SMEM_SPEC if a.dtype == jnp.int32 else where for a in args],
        out_specs=jax.tree.map(lambda _: VMEM_SPEC, out_shape),
        scratch_shapes=list(scratch),
        input_output_aliases=alias or {},
        compiler_params=pltpu.CompilerParams(vmem_limit_bytes=vmem),
        cost_estimate=pl.CostEstimate(flops=flops, bytes_accessed=cost, transcendentals=0),
    )(*args)


def local(cotangent, stored_first, stored_second, w_first, w_second, w_third):
    frames, rows, cols, chans = cotangent.shape
    width = cols + SUB
    par = jnp.stack([lax.axis_index("ha") % 2, lax.axis_index("wa") % 2]).astype(jnp.int32)

    def arr(*shape, dtype=F32):
        return jax.ShapeDtypeStruct(shape, dtype)

    def vmem(*shape, dtype=F32):
        return pltpu.VMEM(shape, dtype)

    edge = arr(frames, rows, SUB, LANES)
    own = arr(frames, rows, cols, LANES)
    message = arr(3, 3, width, LANES)
    fields = (cotangent, stored_second, stored_first)
    wp0, wp1 = call(
        edge_kernel,
        (edge, edge),
        (par,) + fields,
        [vmem(3, 2, frames, rows, SUB, chans), vmem(3, 2, frames, rows, SUB, LANES), pltpu.SemaphoreType.DMA((3, 2))],
        hbm=True,
    )
    rw1 = swap(wp1, "wa", 1)
    rw0 = swap(wp0, "wa", 0)
    ma0, ma1, mb0, mb1, cp, s2, s1 = call(pack_kernel, (message,) * 4 + (own,) * 3, (par,) + fields)
    ma0, ma1, mb0, mb1, cc, c2, c1 = call(
        functools.partial(corner_kernel, chans),
        (message,) * 4 + (edge,) * 3,
        (par, rw0, rw1, ma0, ma1, mb0, mb1),
        alias={3: 0, 4: 1, 5: 2, 6: 3},
    )
    ra1 = swap(ma1, "ha", 1)
    ra0 = swap(ma0, "ha", 0)
    rb1 = swap(mb1, "ha", 1)
    rb0 = swap(mb0, "ha", 0)

    weights = arr(6, 3, 2, LANES, 3 * LANES, dtype=BF16)
    u3, u2, u1 = (call(weight_kernel, weights, (w,)) for w in (w_third, w_second, w_first))

    scratch = [
        vmem(6, width // SUB, 2, 2 * SUB, 4 * LANES, dtype=BF16),
        vmem(2, 6, 2, width, 2 * LANES),
    ]
    grad = call(
        functools.partial(third_kernel, chans),
        arr(frames, rows + 4, width, LANES),
        (par, cp, cc, ra0, ra1, u3),
        [vmem(frames, rows + 6, width, LANES)] + scratch,
    )
    return call(
        functools.partial(last_kernel, chans),
        arr(frames, rows, cols, chans),
        (par, grad, s2, c2, s1, c1, rb0, rb1, u2, u1),
        [
            vmem(frames, rows + 4, width, LANES),
            vmem(frames, rows + 2, width, LANES),
            vmem(frames, rows + 2, width, LANES),
        ]
        + scratch,
    )


def solution(mesh):
    in_specs = (
        P("clip", "ha", "wa", None),
        P("clip", "ha", "wa", None),
        P("clip", "ha", "wa", None),
        P(),
        P(),
        P(),
    )
    out_specs = P("clip", "ha", "wa", None)
    return jax.shard_map(local, mesh=mesh, in_specs=in_specs, out_specs=out_specs, check_vma=False)
```

time: 54.9 us -> 42 us (0.77)
  the two profiles are of different devices: /device:TPU:10 before, /device:TPU:17 now
where the time goes in v1:
time: 42 us; the launch traced here: 41.7 us
  Pallas kernels  23.2 us (55%)
  starting transfers between devices  10.7 us (25%)
  waiting for transfers between devices  4.09 us (10%)
  local copies, waits for them, and re-layouts  3.49 us (8%)
    pallas_call x8, Pallas kernels, call(): pl.pallas_call(body, out_shape=out_shape, in_specs=[SMEM_SPEC if a.dtype...  23.2 us
    ppermute x6, starting transfers between devices, swap(): return lax.ppermute(value, axis, pairs)  10.7 us
    ppermute x6, waiting for transfers between devices, swap(): return lax.ppermute(value, axis, pairs)  4.09 us
    unnamed x12, local copies, waits for them, and re-layouts  3.49 us
  transfers between devices with their start and end apart: 6, of which 2 were waited for; matrix products, arithmetic and copies ran while one was open for 0% of the time, Pallas kernels for 24%

profile of v1, /device:TPU:17, one launch (start us, length us, event | category | flops | bytes accessed | tf_op | source)
XLA Modules:
  0.0 41.7 jit_solution(18192149835003998895)
XLA Ops:
  0.0 0.1 pad_add_fusion.par_ref
  0.1 1.0 %copy-done = f32[4,4,64,96]{3,2,1,0:T(8,128)S(1)} copy-done((f32[4,4,64,96]{3,2,1,0:T(8,128)S(1)}, f32[4,4,64,96]{3,2,1,0:T(8,128)}, u32[]{:S(2)}) %copy-start) | copy-done | bytes 393240
  1.1 1.0 %copy-done.1 = f32[4,4,64,96]{3,2,1,0:T(8,128)S(1)} copy-done((f32[4,4,64,96]{3,2,1,0:T(8,128)S(1)}, f32[4,4,64,96]{3,2,1,0:T(8,128)}, u32[]{:S(2)}) %copy-start.1) | copy-done | bytes 393240
  2.2 1.0 %copy-done.2 = f32[4,4,64,96]{3,2,1,0:T(8,128)S(1)} copy-done((f32[4,4,64,96]{3,2,1,0:T(8,128)S(1)}, f32[4,4,64,96]{3,2,1,0:T(8,128)}, u32[]{:S(2)}) %copy-start.2) | copy-done | bytes 393240
  3.2 0.8 %shard_map.65 = (f32[4,4,8,128]{3,2,1,0:T(8,128)S(1)}, f32[4,4,8,128]{3,2,1,0:T(8,128)S(1)}) custom-call(s32[2]{0:T(128)S(1)} %pad_add_fusion.par_ref, f32[4,4,64,96]{3,2,1,0:T(8,128)S(1)} %copy-done, f32[4,4,64,96]{3,2,1,0:T(8,128)S(1)} %copy-done.1, f32[4,4,64,96]{3,2,1,0:T(8,128)S(1)} %copy-done.2), custom_call_target="tpu_custom_call" | custom-call | tf_op jit(solution)/shard_map/pallas_call | solution.py:336
  4.0 0.7 %collective-permute-start = (f32[4,4,8,128]{3,2,1,0:T(8,128)S(1)}, f32[4,4,8,128]{3,2,1,0:T(8,128)S(1)}, u32[]{:S(2)}, u32[]{:S(2)}) collective-permute-start(f32[4,4,8,128]{3,2,1,0:T(8,128)S(1)} %get-tuple-element.22), channel_id=1, source_target_pairs={{0,1},{1,0},{2,3},{3,2},{4,5},{5,4},{6,7},{7,6},{8,9},{9,8},{10,11... | collective-permute-start | bytes 196616 | tf_op jit(solution)/shard_map/ppermute | solution.py:331
  4.8 3.2 %collective-permute-start.1 = (f32[4,4,8,128]{3,2,1,0:T(8,128)S(1)}, f32[4,4,8,128]{3,2,1,0:T(8,128)S(1)}, u32[]{:S(2)}, u32[]{:S(2)}) collective-permute-start(f32[4,4,8,128]{3,2,1,0:T(8,128)S(1)} %get-tuple-element.23), channel_id=1, source_target_pairs={{1,2},{2,1},{5,6},{6,5},{9,10},{10,9},{13,14},{14,13},{17,18},{18,... | collective-permute-start | bytes 196616 | tf_op jit(solution)/shard_map/ppermute | solution.py:331
  7.9 1.4 %shard_map.64 = (f32[3,3,72,128]{3,2,1,0:T(8,128)S(1)}, f32[3,3,72,128]{3,2,1,0:T(8,128)S(1)}, f32[3,3,72,128]{3,2,1,0:T(8,128)S(1)}, f32[3,3,72,128]{3,2,1,0:T(...) custom-call(s32[2]{0:T(128)S(1)} %pad_add_fusion.par_ref, ...), custom_call_target="tpu_custom_call" | custom-call | tf_op jit(solution)/shard_map/pallas_call | solution.py:336
  9.3 1.2 %collective-permute-done.1.rw1 = f32[4,4,8,128]{3,2,1,0:T(8,128)S(1)} collective-permute-done((f32[4,4,8,128]{3,2,1,0:T(8,128)S(1)}, f32[4,4,8,128]{3,2,1,0:T(8,128)S(1)}, u32[]{:S(2)}, u32[]{:S(2)}) %collective-permute-start.1) | collective-permute-done | bytes 65568 | tf_op jit(solution)/shard_map/ppermute | solution.py:331
  10.5 0.7 %shard_map.66 = (f32[3,3,72,128]{3,2,1,0:T(8,128)S(1)}, f32[3,3,72,128]{3,2,1,0:T(8,128)S(1)}, f32[3,3,72,128]{3,2,1,0:T(8,128)S(1)}, f32[3,3,72,128]{3,2,1,0:T(...) custom-call(s32[2]{0:T(128)S(1)} %pad_add_fusion.par_ref, ...), custom_call_target="tpu_custom_call", output_to_operand_aliasing={{0}: (3, {}), {1}: (4, {}), {2}: (5, {}), {3}: (6, {})} | custom-call | tf_op jit(solution)/shard_map/pallas_call | solution.py:336
  11.2 1.4 %collective-permute-start.2 = (f32[3,3,72,128]{3,2,1,0:T(8,128)S(1)}, f32[3,3,72,128]{3,2,1,0:T(8,128)S(1)}, u32[]{:S(2)}, u32[]{:S(2)}) collective-permute-start(f32[3,3,72,128]{3,2,1,0:T(8,128)S(1)} %get-tuple-element.29), channel_id=1, source_target_pairs={{0,4},{4,0},{8,12},{12,8},{1,5},{5,1},{9,13},{13,9},{2,6},{6,2},{1... | collective-permute-start | bytes 995336 | tf_op jit(solution)/shard_map/ppermute | solution.py:331
  12.5 1.9 %collective-permute-start.3 = (f32[3,3,72,128]{3,2,1,0:T(8,128)S(1)}, f32[3,3,72,128]{3,2,1,0:T(8,128)S(1)}, u32[]{:S(2)}, u32[]{:S(2)}) collective-permute-start(f32[3,3,72,128]{3,2,1,0:T(8,128)S(1)} %get-tuple-element.30), channel_id=1, source_target_pairs={{4,8},{8,4},{5,9},{9,5},{6,10},{10,6},{7,11},{11,7},{20,24},{24,20... | collective-permute-start | bytes 995336 | tf_op jit(solution)/shard_map/ppermute | solution.py:331
  14.4 0.1 collective-permute-start.4
  14.5 0.0 copy-start.4
  14.5 3.5 %collective-permute-start.5 = (f32[3,3,72,128]{3,2,1,0:T(8,128)S(1)}, f32[3,3,72,128]{3,2,1,0:T(8,128)S(1)}, u32[]{:S(2)}, u32[]{:S(2)}) collective-permute-start(f32[3,3,72,128]{3,2,1,0:T(8,128)S(1)} %get-tuple-element.36), channel_id=1, source_target_pairs={{4,8},{8,4},{5,9},{9,5},{6,10},{10,6},{7,11},{11,7},{20,24},{24,20... | collective-permute-start | bytes 995336 | tf_op jit(solution)/shard_map/ppermute | solution.py:331
  18.0 0.9 %shard_map.67.w_ref = bf16[6,3,2,128,384]{4,3,2,1,0:T(8,128)(2,1)S(1)} custom-call(f32[3,3,3,96,96]{4,3,2,1,0:T(8,128)S(1)} %copy-done.3), custom_call_target="tpu_custom_call" | custom-call | tf_op jit(solution)/shard_map/pallas_call | solution.py:336
  19.0 0.0 copy-start.5
  19.0 0.9 %shard_map.69.w2_ref = bf16[6,3,2,128,384]{4,3,2,1,0:T(8,128)(2,1)S(1)} custom-call(f32[3,3,3,96,96]{4,3,2,1,0:T(8,128)S(1)} %copy-done.4), custom_call_target="tpu_custom_call" | custom-call | tf_op jit(solution)/shard_map/pallas_call | solution.py:336
  20.0 0.4 copy-done.5
  20.3 0.9 %shard_map.70.w1_ref = bf16[6,3,2,128,384]{4,3,2,1,0:T(8,128)(2,1)S(1)} custom-call(f32[3,3,3,96,96]{4,3,2,1,0:T(8,128)S(1)} %copy-done.5), custom_call_target="tpu_custom_call" | custom-call | tf_op jit(solution)/shard_map/pallas_call | solution.py:336
  21.3 0.0 collective-permute-done.2.ra0
  21.3 2.9 %collective-permute-done.3.ra1 = f32[3,3,72,128]{3,2,1,0:T(8,128)S(1)} collective-permute-done((f32[3,3,72,128]{3,2,1,0:T(8,128)S(1)}, f32[3,3,72,128]{3,2,1,0:T(8,128)S(1)}, u32[]{:S(2)}, u32[]{:S(2)}) %collective-permute-start.3) | collective-permute-done | bytes 331808 | tf_op jit(solution)/shard_map/ppermute | solution.py:331
  24.2 5.9 %shard_map.68.g_ref = f32[4,8,72,128]{3,2,1,0:T(8,128)S(1)} custom-call(s32[2]{0:T(128)S(1)} %pad_add_fusion.par_ref, f32[4,4,64,128]{3,2,1,0:T(8,128)S(1)} %get-tuple-element.21.cp_ref, f32[4,4,8,128]{3,2,1,0:T(8,128)S(1)} %get-tuple-element.28.cc_ref, f32[3,3,72,128]{3,2,1,0:T(8,128)S(1)} %collective-permute-done.2.ra0, ...), custom_call_target="tpu_custom_call" | custom-call | tf_op jit(solution)/shard_map/pallas_call | solution.py:336
  30.1 11.6 %shard_map.71 = f32[4,4,64,96]{3,2,1,0:T(8,128)} custom-call(s32[2]{0:T(128)S(1)} %pad_add_fusion.par_ref, f32[4,8,72,128]{3,2,1,0:T(8,128)S(1)} %shard_map.68.g_ref, f32[4,4,64,128]{3,2,1,0:T(8,128)S(1)} %get-tuple-element.31.s2_ref, f32[4,4,8,128]{3,2,1,0:T(8,128)S(1)} %get-tuple-element.32.c2_ref, f32[4,4,64,128]{3,2,1,0:T(8,128)S(1)} %get-tuple-element.33.s1_ref, ...), custom_call_target="tpu_custom_call" | custom-call | tf_op jit(solution)/shard_map/pallas_call | solution.py:336
  (9 shorter events, 0.0 us)
Async XLA Ops:
  0.1 1.0 %copy-start = (f32[4,4,64,96]{3,2,1,0:T(8,128)S(1)}, f32[4,4,64,96]{3,2,1,0:T(8,128)}, u32[]{:S(2)}) copy-start(f32[4,4,64,96]{3,2,1,0:T(8,128)} %cot_hbm.1) | copy-start | bytes 1179652
  1.1 1.0 %copy-start.1 = (f32[4,4,64,96]{3,2,1,0:T(8,128)S(1)}, f32[4,4,64,96]{3,2,1,0:T(8,128)}, u32[]{:S(2)}) copy-start(f32[4,4,64,96]{3,2,1,0:T(8,128)} %sec_hbm.1) | copy-start | bytes 1179652
  2.2 1.0 %copy-start.2 = (f32[4,4,64,96]{3,2,1,0:T(8,128)S(1)}, f32[4,4,64,96]{3,2,1,0:T(8,128)}, u32[]{:S(2)}) copy-start(f32[4,4,64,96]{3,2,1,0:T(8,128)} %fst_hbm.1) | copy-start | bytes 1179652
  4.0 5.3 %collective-permute-start = (f32[4,4,8,128]{3,2,1,0:T(8,128)S(1)}, f32[4,4,8,128]{3,2,1,0:T(8,128)S(1)}, u32[]{:S(2)}, u32[]{:S(2)}) collective-permute-start(f32[4,4,8,128]{3,2,1,0:T(8,128)S(1)} %get-tuple-element.22), channel_id=1, source_target_pairs={{0,1},{1,0},{2,3},{3,2},{4,5},{5,4},{6,7},{7,6},{8,9},{9,8},{10,11... | collective-permute-start | bytes 196616 | tf_op jit(solution)/shard_map/ppermute | solution.py:331
  4.8 13.3 %copy-start.3 = (f32[3,3,3,96,96]{4,3,2,1,0:T(8,128)S(1)}, f32[3,3,3,96,96]{4,3,2,1,0:T(8,128)}, u32[]{:S(2)}) copy-start(f32[3,3,3,96,96]{4,3,2,1,0:T(8,128)} %w_ref.3) | copy-start | bytes 2985988
  4.8 5.7 %collective-permute-start.1 = (f32[4,4,8,128]{3,2,1,0:T(8,128)S(1)}, f32[4,4,8,128]{3,2,1,0:T(8,128)S(1)}, u32[]{:S(2)}, u32[]{:S(2)}) collective-permute-start(f32[4,4,8,128]{3,2,1,0:T(8,128)S(1)} %get-tuple-element.23), channel_id=1, source_target_pairs={{1,2},{2,1},{5,6},{6,5},{9,10},{10,9},{13,14},{14,13},{17,18},{18,... | collective-permute-start | bytes 196616 | tf_op jit(solution)/shard_map/ppermute | solution.py:331
  11.2 10.1 %collective-permute-start.2 = (f32[3,3,72,128]{3,2,1,0:T(8,128)S(1)}, f32[3,3,72,128]{3,2,1,0:T(8,128)S(1)}, u32[]{:S(2)}, u32[]{:S(2)}) collective-permute-start(f32[3,3,72,128]{3,2,1,0:T(8,128)S(1)} %get-tuple-element.29), channel_id=1, source_target_pairs={{0,4},{4,0},{8,12},{12,8},{1,5},{5,1},{9,13},{13,9},{2,6},{6,2},{1... | collective-permute-start | bytes 995336 | tf_op jit(solution)/shard_map/ppermute | solution.py:331
  12.5 11.7 %collective-permute-start.3 = (f32[3,3,72,128]{3,2,1,0:T(8,128)S(1)}, f32[3,3,72,128]{3,2,1,0:T(8,128)S(1)}, u32[]{:S(2)}, u32[]{:S(2)}) collective-permute-start(f32[3,3,72,128]{3,2,1,0:T(8,128)S(1)} %get-tuple-element.30), channel_id=1, source_target_pairs={{4,8},{8,4},{5,9},{9,5},{6,10},{10,6},{7,11},{11,7},{20,24},{24,20... | collective-permute-start | bytes 995336 | tf_op jit(solution)/shard_map/ppermute | solution.py:331
  14.4 15.7 %collective-permute-start.4 = (f32[3,3,72,128]{3,2,1,0:T(8,128)S(1)}, f32[3,3,72,128]{3,2,1,0:T(8,128)S(1)}, u32[]{:S(2)}, u32[]{:S(2)}) collective-permute-start(f32[3,3,72,128]{3,2,1,0:T(8,128)S(1)} %get-tuple-element.35), channel_id=1, source_target_pairs={{0,4},{4,0},{8,12},{12,8},{1,5},{5,1},{9,13},{13,9},{2,6},{6,2},{1... | collective-permute-start | bytes 995336 | tf_op jit(solution)/shard_map/ppermute | solution.py:331
  14.5 4.5 %copy-start.4 = (f32[3,3,3,96,96]{4,3,2,1,0:T(8,128)S(1)}, f32[3,3,3,96,96]{4,3,2,1,0:T(8,128)}, u32[]{:S(2)}) copy-start(f32[3,3,3,96,96]{4,3,2,1,0:T(8,128)} %w_ref.4) | copy-start | bytes 2985988
  14.5 15.6 %collective-permute-start.5 = (f32[3,3,72,128]{3,2,1,0:T(8,128)S(1)}, f32[3,3,72,128]{3,2,1,0:T(8,128)S(1)}, u32[]{:S(2)}, u32[]{:S(2)}) collective-permute-start(f32[3,3,72,128]{3,2,1,0:T(8,128)S(1)} %get-tuple-element.36), channel_id=1, source_target_pairs={{4,8},{8,4},{5,9},{9,5},{6,10},{10,6},{7,11},{11,7},{20,24},{24,20... | collective-permute-start | bytes 995336 | tf_op jit(solution)/shard_map/ppermute | solution.py:331
  19.0 1.3 %copy-start.5 = (f32[3,3,3,96,96]{4,3,2,1,0:T(8,128)S(1)}, f32[3,3,3,96,96]{4,3,2,1,0:T(8,128)}, u32[]{:S(2)}) copy-start(f32[3,3,3,96,96]{4,3,2,1,0:T(8,128)} %w_ref.5) | copy-start | bytes 2985988

commit v2 on v1

v2 whole, which is shorter than its diff:
```python
import functools

import jax
import jax.numpy as jnp
from jax import lax
from jax.experimental import pallas as pl
from jax.experimental.pallas import tpu as pltpu
from jax.sharding import PartitionSpec as P

LANES = 128
SUB = 8
F32 = jnp.float32
BF16 = jnp.bfloat16
VMEM_SPEC = pl.BlockSpec(memory_space=pltpu.VMEM)
SMEM_SPEC = pl.BlockSpec(memory_space=pltpu.SMEM)


def silu_slope(value):
    sigma = 1.0 / (1.0 + jnp.exp(-value))
    return sigma * (1.0 + value * (1.0 - sigma))


def roll(value, shift, axis):
    return pltpu.roll(value, shift % value.shape[axis], axis)


def lane_of(shape):
    return lax.broadcasted_iota(jnp.int32, shape, len(shape) - 1)


def sub_of(shape):
    return lax.broadcasted_iota(jnp.int32, shape, len(shape) - 2)


def group_frames(frames, chans):
    first, second, third, fourth = frames
    part = LANES - chans
    lane = lane_of(first.shape)
    packed = []
    for index, frame in enumerate((first, second, third)):
        packed.append(jnp.where(lane < chans, frame, roll(fourth, chans - part * index, 1)))
    return packed


def ungroup_frames(groups, chans):
    part = LANES - chans
    lane = lane_of(groups[0].shape)
    frames = [jnp.where(lane < chans, group, 0.0) for group in groups]
    fourth = jnp.zeros_like(groups[0])
    for index in reversed(range(3)):
        moved = roll(groups[index], part * (index + 1), 1)
        fourth = jnp.where(lane < part * (index + 1), moved, fourth)
    return frames + [jnp.where(lane < chans, fourth, 0.0)]


def edge_kernel(par_ref, cot_hbm, sec_hbm, fst_hbm, wp0, wp1, raw_ref, pad_ref, sems):
    frames, rows, cols, chans = cot_hbm.shape
    copies = []
    for a, src in enumerate((cot_hbm, sec_hbm, fst_hbm)):
        for side, start in enumerate((0, cols - SUB)):
            copies.append(
                pltpu.make_async_copy(src.at[:, :, pl.ds(start, SUB), :], raw_ref.at[a, side], sems.at[a, side])
            )
            copies[-1].start()
    pad_ref[...] = jnp.zeros(pad_ref.shape, F32)
    for copy in copies:
        copy.wait()
    pad_ref[0, :, :, :, :, 0:chans] = raw_ref[0]
    pad_ref[1:3, :, :, :, :, 0:chans] = silu_slope(raw_ref[1:3])

    def cols_out(left, right):
        sub = sub_of((SUB, LANES))
        for t in range(frames):
            for h in range(rows):
                c0, a0, b0 = (pad_ref[a, 0, t, h] for a in range(3))
                c7, a7, b7 = (pad_ref[a, 1, t, h] for a in range(3))
                right[t, h] = jnp.where(
                    sub >= 5, c7, jnp.where((sub == 2) | (sub == 3), roll(a7, 4, 0), jnp.where(sub == 1, roll(b7, 2, 0), 0.0))
                )
                left[t, h] = jnp.where(
                    sub < 3, c0, jnp.where((sub == 4) | (sub == 5), roll(a0, 4, 0), jnp.where(sub == 6, roll(b0, 6, 0), 0.0))
                )

    @pl.when(par_ref[1] == 0)
    def _():
        cols_out(wp1, wp0)

    @pl.when(par_ref[1] != 0)
    def _():
        cols_out(wp0, wp1)


def put_rows(read_cot, read_s2, read_s1, rows, top_a, top_b, low_a, low_b, span, chans):
    def put(read, h, dst, at):
        for g, val in enumerate(group_frames([read(t, h) for t in range(4)], chans)):
            dst[g, at, span] = val

    for r in range(3):
        put(read_cot, r, top_a, r)
        put(read_cot, rows - 3 + r, low_a, r)
    for r in range(2):
        put(read_s2, r, top_b, r)
        put(read_s2, rows - 2 + r, low_b, r)
    put(read_s1, 0, top_b, 2)
    put(read_s1, rows - 1, low_b, 2)


def pack_kernel(par_ref, cot_ref, sec_ref, fst_ref, ma0, ma1, mb0, mb1, cp_ref, s2_ref, s1_ref):
    frames, rows, cols, chans = cot_ref.shape
    outs = (cp_ref, s2_ref, s1_ref)
    blank = jnp.zeros((cols, LANES), F32)
    for a, ref in enumerate(outs):
        for t in range(frames):
            for h in range(rows):
                value = (cot_ref, sec_ref, fst_ref)[a][t, h]
                ref[t, h, 0:cols] = blank
                ref[t, h, 0:cols, 0:chans] = silu_slope(value) if a else value

    def rows_out(*dst):
        reads = [lambda t, h, ref=ref: ref[t, h, 0:cols] for ref in outs]
        put_rows(*reads, rows, *dst, slice(0, cols), chans)

    @pl.when(par_ref[0] == 0)
    def _():
        rows_out(ma1, mb1, ma0, mb0)

    @pl.when(par_ref[0] != 0)
    def _():
        rows_out(ma0, mb0, ma1, mb1)


def corner_kernel(chans, par_ref, rw0, rw1, _a0, _a1, _b0, _b1, _c, _s2, _s1, ma0, ma1, mb0, mb1, cp_ref, s2_ref, s1_ref):
    frames, rows = rw0.shape[:2]
    cols = ma0.shape[2] - SUB
    even = par_ref[1] == 0
    sub = sub_of((SUB, LANES))
    for t in range(frames):
        for h in range(rows):
            left = jnp.where(even, rw1[t, h], rw0[t, h])
            right = jnp.where(even, rw0[t, h], rw1[t, h])
            cp_ref[t, h, cols:] = jnp.where(sub < 3, right, jnp.where(sub >= 5, left, 0.0))
            s2_ref[t, h, cols:] = jnp.where(sub < 2, roll(right, 4, 0), jnp.where(sub >= 6, roll(left, 4, 0), 0.0))
            s1_ref[t, h, cols:] = jnp.where(sub == 0, roll(right, 2, 0), jnp.where(sub == 7, roll(left, 6, 0), 0.0))

    def rows_out(*dst):
        reads = [lambda t, h, ref=ref: ref[t, h, cols:] for ref in (cp_ref, s2_ref, s1_ref)]
        put_rows(*reads, rows, *dst, slice(cols, cols + SUB), chans)

    @pl.when(par_ref[0] == 0)
    def _():
        rows_out(ma1, mb1, ma0, mb0)

    @pl.when(par_ref[0] != 0)
    def _():
        rows_out(ma0, mb0, ma1, mb1)


def weight_kernel(wanted, w_ref, out_ref):
    chans = w_ref.shape[3]
    out_ref[...] = jnp.zeros(out_ref.shape, BF16)
    for k in range(3):
        for i in range(3):
            f0, f1, f2 = (w_ref[i, 2 - m, k] for m in range(3))
            even, odd = (f0 + f2) * (1 / 6), f1 * (1 / 6)
            far, odd2 = f0 * (1 / 24) + f2 * (1 / 6), f1 * (1 / 12)
            points = (f0 * 0.25, -even - odd, odd - even, far + odd2, far - odd2, f2)
            lanes = pl.ds((2 - i) * LANES, chans)
            for n, p in enumerate(wanted):
                u = points[p]
                high = u.astype(BF16)
                out_ref[n, k, 0, 0:chans, lanes] = high
                out_ref[n, k, 1, 0:chans, lanes] = (u - high.astype(F32)).astype(BF16)


POINTS = {2: (0, 1, 2, 5), 3: (0, 1, 2, 3, 5), 4: (0, 1, 2, 3, 4, 5)}


def transform(x, size):
    if size == 2:
        return 4.0 * (x[0] - x[2]), -3.0 * (x[1] + x[2]), 3.0 * (x[1] - x[2]), x[3] - x[1]
    if size == 3:
        a, b = x[3] - x[1], x[3] - 2.0 * x[1]
        return (
            4.0 * (x[0] - x[2]) + 2.0 * a,
            3.0 * (b - x[2]),
            2.0 * x[1] - 3.0 * x[2] + x[3],
            4.0 * a,
            x[4] - x[2] - 2.0 * a,
        )
    a, b = x[4] - 4.0 * x[2], x[3] - 4.0 * x[1]
    c, e = x[4] - x[2], 2.0 * (x[3] - x[1])
    return 4.0 * x[0] - 5.0 * x[2] + x[4], a + b, a - b, c + e, c - e, 4.0 * x[1] - 5.0 * x[3] + x[5]


def outputs(y, size):
    plus, minus = y[1] + y[2], y[1] - y[2]
    if size == 2:
        return y[0] + plus, minus + y[3]
    if size == 3:
        return y[0] + plus + y[3], minus + 2.0 * y[3], plus + 4.0 * y[3] + y[4]
    far, odd = y[3] + y[4], y[3] - y[4]
    return y[0] + plus + far, minus + 2.0 * odd, plus + 4.0 * far, minus + 8.0 * odd + y[5]


def right_operands(w_ref, p):
    zero = jnp.zeros((LANES, LANES), BF16)
    near, far = [], []
    for k in range(3):
        parts = [w_ref[p, k, part] for part in range(2)]
        own = [
            jnp.concatenate([r[:, : 2 * LANES], jnp.concatenate([zero, r[:, :LANES]], 1)], 0) for r in parts
        ]
        later = [
            jnp.concatenate([jnp.concatenate([r[:, 2 * LANES :], zero], 1), r[:, LANES:]], 0) for r in parts
        ]
        near.append(jnp.concatenate([own[0], own[0], own[1]], 1))
        far.append(jnp.concatenate([later[0], later[0], later[1]], 1))
    return jnp.concatenate(near, 0), jnp.concatenate(far, 0)


def product(left, right):
    left = jnp.concatenate([left, left[:, : 2 * LANES]], 1)
    return lax.dot_general(left, right, (((1,), (1,)), ((), ())), preferred_element_type=F32)


def shifted_sum(taps):
    two = 2 * LANES
    return roll(taps[:, :two], -1, 0) + taps[:, two : 2 * two] + roll(taps[:, 2 * two :], 1, 0)


def conv(read, size, width, s_ref, y_ref, w_ref, emit, done=None):
    chunks = width // SUB
    points = len(POINTS[size])

    def one(c, carry):
        at = pl.ds(pl.multiple_of(c * SUB, SUB), SUB)
        for t in range(4):
            pair, a = t // 2, t % 2
            x = [read(t, r, at) for r in range(2 * size + 2)]
            for p, pieces in enumerate(zip(transform(x[: size + 2], size), transform(x[size:], size))):
                value = jnp.concatenate(pieces, 0)
                high = value.astype(BF16)
                s_ref[p, c, pair, :, a * LANES : (a + 1) * LANES] = high
                s_ref[p, c, pair, :, (2 + a) * LANES : (3 + a) * LANES] = (value - high.astype(F32)).astype(BF16)
        return carry

    lax.fori_loop(0, chunks, one, 0)

    wide = 4 * LANES
    for p in range(points):
        near, far = right_operands(w_ref, p)
        own = product(s_ref[p].reshape(chunks * 4 * SUB, wide), near).reshape(chunks, 2, 2, SUB, 6 * LANES)
        later = product(s_ref[p, :, 1].reshape(chunks * 2 * SUB, wide), far).reshape(chunks, 2, SUB, 6 * LANES)
        for n in range(2):
            y_ref[0, p, n] = shifted_sum((own[:, 0, n] + later[:, n]).reshape(width, 6 * LANES))
            y_ref[1, p, n] = shifted_sum(own[:, 1, n].reshape(width, 6 * LANES))

    for t in range(4):
        lanes = pl.ds(t % 2 * LANES, LANES)
        for tile in range(2):
            rows = outputs([y_ref[t // 2, p, tile, :, lanes] for p in range(points)], size)
            for o, value in enumerate(rows):
                emit(t, tile * size + o, value)
        if done is not None:
            done(t)


def halo_rows(chans, par, from_even, from_odd, r):
    return ungroup_frames([jnp.where(par == 0, from_even[g, r], from_odd[g, r]) for g in range(3)], chans)


def third_kernel(chans, par_ref, cp_ref, ra0, ra1, w_ref, out_ref, x_ref, s_ref, y_ref):
    rows, width = cp_ref.shape[1:3]
    for r in range(3):
        for at, even, odd in ((r, ra1, ra0), (r + 3, ra0, ra1)):
            for t, frame in enumerate(halo_rows(chans, par_ref[0], even, odd, r)):
                x_ref[t, at] = frame

    def read(t, r, at):
        if 3 <= r < 3 + rows:
            return cp_ref[t, r - 3, at]
        return x_ref[t, r if r < 3 else r - rows, at]

    def emit(t, o, value):
        out_ref[t, o] = value

    conv(read, rows, width, s_ref, y_ref, w_ref, emit)


def last_kernel(chans, par_ref, g_ref, s2_ref, s1_ref, rb0, rb1, w2_ref, w1_ref, out_hbm,
                e_ref, x1_ref, s_ref, y_ref, stage_ref, sems):
    frames, rows, width, _ = s2_ref.shape
    cols = width - SUB
    for r in range(3):
        for side, even, odd in ((0, rb1, rb0), (1, rb0, rb1)):
            for t, frame in enumerate(halo_rows(chans, par_ref[0], even, odd, r)):
                e_ref[side, r, t] = frame

    def slope2(t, r, at):
        if 2 <= r < 2 + rows:
            return s2_ref[t, r - 2, at]
        return e_ref[0, r, t, at] if r < 2 else e_ref[1, r - 2 - rows, t, at]

    def emit2(t, o, value):
        slope = s1_ref[t, o - 1] if 1 <= o < 1 + rows else e_ref[0 if o < 1 else 1, 2, t]
        x1_ref[t, o] = value * slope

    def emit1(t, o, value):
        stage_ref[t, o] = value[0:cols, 0:chans]

    def copy_out(t):
        return pltpu.make_async_copy(stage_ref.at[t], out_hbm.at[t], sems.at[t])

    conv(lambda t, r, at: g_ref[t, r, at] * slope2(t, r, at), (rows + 2) // 2, width, s_ref, y_ref, w2_ref, emit2)
    conv(
        lambda t, r, at: x1_ref[t, r, at], rows // 2, width, s_ref, y_ref, w1_ref, emit1, lambda t: copy_out(t).start()
    )
    for t in range(frames):
        copy_out(t).wait()


def swap(value, axis, which):
    count = lax.axis_size(axis)
    pairs = []
    for low in range(1 - which, count - 1, 2):
        pairs += [(low, low + 1), (low + 1, low)]
    return lax.ppermute(value, axis, pairs)


def swaps(first, second, axis):
    got = swap(first, axis, 0), swap(second, axis, 1)
    return got


def call(body, out_shape, args, scratch=(), hbm=False, hbm_out=False, alias=None, vmem=40 << 20, flops=0, cost=0):
    hbm_spec = pl.BlockSpec(memory_space=pltpu.HBM)
    where, out = hbm_spec if hbm else VMEM_SPEC, hbm_spec if hbm_out else VMEM_SPEC
    return pl.pallas_call(
        body,
        out_shape=out_shape,
        in_specs=[SMEM_SPEC if a.dtype == jnp.int32 else where for a in args],
        out_specs=jax.tree.map(lambda _: out, out_shape),
        scratch_shapes=list(scratch),
        input_output_aliases=alias or {},
        compiler_params=pltpu.CompilerParams(vmem_limit_bytes=vmem),
        cost_estimate=pl.CostEstimate(flops=flops, bytes_accessed=cost, transcendentals=0),
    )(*args)


def local(cotangent, stored_first, stored_second, w_first, w_second, w_third):
    frames, rows, cols, chans = cotangent.shape
    width = cols + SUB
    par = jnp.stack([(lax.axis_index("ha") + 1) % 2, (lax.axis_index("wa") + 1) % 2]).astype(jnp.int32)

    def arr(*shape, dtype=F32):
        return jax.ShapeDtypeStruct(shape, dtype)

    def vmem(*shape, dtype=F32):
        return pltpu.VMEM(shape, dtype)

    edge = arr(frames, rows, SUB, LANES)
    own = arr(frames, rows, width, LANES)
    message = arr(3, 3, width, LANES)
    fields = (cotangent, stored_second, stored_first)
    wp0, wp1 = call(
        edge_kernel,
        (edge, edge),
        (par,) + fields,
        [vmem(3, 2, frames, rows, SUB, chans), vmem(3, 2, frames, rows, SUB, LANES), pltpu.SemaphoreType.DMA((3, 2))],
        hbm=True,
        vmem=66_700_000,
    )
    rw0, rw1 = swaps(wp0, wp1, "wa")
    packed = call(
        pack_kernel,
        (message,) * 4 + (own,) * 3,
        (par,) + fields,
    )
    ma0, ma1, mb0, mb1, cp, s2, s1 = call(
        functools.partial(corner_kernel, chans),
        (message,) * 4 + (own,) * 3,
        (par, rw0, rw1) + tuple(packed),
        alias={n + 3: n for n in range(7)},
    )
    ra0, ra1 = swaps(ma0, ma1, "ha")
    rb0, rb1 = swaps(mb0, mb1, "ha")

    def prepare(w, size):
        points = POINTS[size]
        shape = arr(len(points), 3, 2, LANES, 3 * LANES, dtype=BF16)
        return call(functools.partial(weight_kernel, points), shape, (w,))

    u3, u2, u1 = prepare(w_third, rows), prepare(w_second, (rows + 2) // 2), prepare(w_first, rows // 2)

    def scratch(size):
        points = len(POINTS[size])
        return [
            vmem(points, width // SUB, 2, 2 * SUB, 4 * LANES, dtype=BF16),
            vmem(2, points, 2, width, 2 * LANES),
        ]

    grad = call(
        functools.partial(third_kernel, chans),
        arr(frames, rows + 4, width, LANES),
        (par, cp, ra0, ra1, u3),
        [vmem(frames, 6, width, LANES)] + scratch(rows),
    )
    return call(
        functools.partial(last_kernel, chans),
        arr(frames, rows, cols, chans),
        (par, grad, s2, s1, rb0, rb1, u2, u1),
        [vmem(2, 3, frames, width, LANES), vmem(frames, rows + 2, width, LANES)]
        + scratch((rows + 2) // 2)
        + [vmem(frames, rows, cols, chans), pltpu.SemaphoreType.DMA((frames,))],
        hbm_out=True,
    )


def solution(mesh):
    in_specs = (
        P("clip", "ha", "wa", None),
        P("clip", "ha", "wa", None),
        P("clip", "ha", "wa", None),
        P(),
        P(),
        P(),
    )
    out_specs = P("clip", "ha", "wa", None)
    return jax.shard_map(local, mesh=mesh, in_specs=in_specs, out_specs=out_specs, check_vma=False)
```

time: 42 us -> 43.2 us (1.029)
  the two profiles are of different devices: /device:TPU:17 before, /device:TPU:0 now
where the time goes in v2:
time: 43.2 us; the launch traced here: 42.7 us
  Pallas kernels  22 us (51%)
  starting transfers between devices  12.6 us (29%)
  waiting for transfers between devices  3.71 us (9%)
  local copies, waits for them, and re-layouts  3.65 us (8%)
  other arithmetic  0.66 us (2%)
    pallas_call x8, Pallas kernels, call(): pl.pallas_call(body, out_shape=out_shape, in_specs=[SMEM_SPEC if a.dtype...  22 us
    ppermute x6, starting transfers between devices, swap(): return lax.ppermute(value, axis, pairs)  12.6 us
    ppermute x6, waiting for transfers between devices, swap(): return lax.ppermute(value, axis, pairs)  3.71 us
    unnamed x14, local copies, waits for them, and re-layouts  3.65 us
  transfers between devices with their start and end apart: 6, of which 2 were waited for; matrix products, arithmetic and copies ran while one was open for 0% of the time, Pallas kernels for 22%

profile of v2, /device:TPU:0, one launch (start us, length us, event | category | flops | bytes accessed | tf_op | source)
XLA Modules:
  0.0 42.7 jit_solution(7085213379594895490)
XLA Ops:
  0.0 0.7 %pad_add_fusion.par_ref = s32[2]{0:T(128)} fusion(s32[1]{0:T(128)} %bitcast.1, s32[1]{0:T(128)} %bitcast), kind=kLoop, calls=%fused_computation | loop fusion | flops 2 | bytes 16 | tf_op jit(solution)/shard_map/stack | solution.py:353
  0.7 2.6 %shard_map.64 = (f32[4,4,8,128]{3,2,1,0:T(8,128)}, f32[4,4,8,128]{3,2,1,0:T(8,128)}) custom-call(s32[2]{0:T(128)} %pad_add_fusion.par_ref, f32[4,4,64,96]{3,2,1,0:T(8,128)} %cot_ref.1, f32[4,4,64,96]{3,2,1,0:T(8,128)} %sec_ref.1, f32[4,4,64,96]{3,2,1,0:T(8,128)} %fst_ref.1), custom_call_target="tpu_custom_call" | custom-call | tf_op jit(solution)/shard_map/pallas_call | solution.py:338
  3.3 0.7 %collective-permute-start = (f32[4,4,8,128]{3,2,1,0:T(8,128)}, f32[4,4,8,128]{3,2,1,0:T(8,128)S(1)}, u32[]{:S(2)}, u32[]{:S(2)}) collective-permute-start(f32[4,4,8,128]{3,2,1,0:T(8,128)} %get-tuple-element.21), channel_id=1, source_target_pairs={{1,2},{2,1},{5,6},{6,5},{9,10},{10,9},{13,14},{14,13},{17,18},{18,... | collective-permute-start | bytes 196616 | tf_op jit(solution)/shard_map/ppermute | solution.py:327
  4.0 4.4 %collective-permute-start.1 = (f32[4,4,8,128]{3,2,1,0:T(8,128)}, f32[4,4,8,128]{3,2,1,0:T(8,128)S(1)}, u32[]{:S(2)}, u32[]{:S(2)}) collective-permute-start(f32[4,4,8,128]{3,2,1,0:T(8,128)} %get-tuple-element.22), channel_id=1, source_target_pairs={{0,1},{1,0},{2,3},{3,2},{4,5},{5,4},{6,7},{7,6},{8,9},{9,8},{10,11... | collective-permute-start | bytes 196616 | tf_op jit(solution)/shard_map/ppermute | solution.py:327
  8.4 1.0 %copy-done = f32[4,4,64,96]{3,2,1,0:T(8,128)S(1)} copy-done((f32[4,4,64,96]{3,2,1,0:T(8,128)S(1)}, f32[4,4,64,96]{3,2,1,0:T(8,128)}, u32[]{:S(2)}) %copy-start) | copy-done | bytes 393240
  9.4 1.0 %copy-done.1 = f32[4,4,64,96]{3,2,1,0:T(8,128)S(1)} copy-done((f32[4,4,64,96]{3,2,1,0:T(8,128)S(1)}, f32[4,4,64,96]{3,2,1,0:T(8,128)}, u32[]{:S(2)}) %copy-start.1) | copy-done | bytes 393240
  10.4 1.0 %copy-done.2 = f32[4,4,64,96]{3,2,1,0:T(8,128)S(1)} copy-done((f32[4,4,64,96]{3,2,1,0:T(8,128)S(1)}, f32[4,4,64,96]{3,2,1,0:T(8,128)}, u32[]{:S(2)}) %copy-start.2) | copy-done | bytes 393240
  11.5 1.4 %shard_map.65 = (f32[3,3,72,128]{3,2,1,0:T(8,128)S(1)}, f32[3,3,72,128]{3,2,1,0:T(8,128)S(1)}, f32[3,3,72,128]{3,2,1,0:T(8,128)S(1)}, f32[3,3,72,128]{3,2,1,0:T(...) custom-call(s32[2]{0:T(128)S(1)} %copy-done.6, ...), custom_call_target="tpu_custom_call" | custom-call | tf_op jit(solution)/shard_map/pallas_call | solution.py:338
  12.9 0.0 copy-start.4
  12.9 0.7 %shard_map.66 = (f32[3,3,72,128]{3,2,1,0:T(8,128)S(1)}, f32[3,3,72,128]{3,2,1,0:T(8,128)S(1)}, f32[3,3,72,128]{3,2,1,0:T(8,128)S(1)}, f32[3,3,72,128]{3,2,1,0:T(...) custom-call(s32[2]{0:T(128)S(1)} %copy-done.6, ...), custom_call_target="tpu_custom_call", output_to_operand_aliasing={{0}: (3, {}), {1}: (4, {}), {2}: (5, {}), {3}: (6, {}), {4}... | custom-call | tf_op jit(solution)/shard_map/pallas_call | solution.py:338
  13.6 0.7 %collective-permute-start.2 = (f32[3,3,72,128]{3,2,1,0:T(8,128)S(1)}, f32[3,3,72,128]{3,2,1,0:T(8,128)S(1)}, u32[]{:S(2)}, u32[]{:S(2)}) collective-permute-start(f32[3,3,72,128]{3,2,1,0:T(8,128)S(1)} %get-tuple-element.31), channel_id=1, source_target_pairs={{4,8},{8,4},{5,9},{9,5},{6,10},{10,6},{7,11},{11,7},{20,24},{24,20... | collective-permute-start | bytes 995336 | tf_op jit(solution)/shard_map/ppermute | solution.py:327
  14.3 4.4 %collective-permute-start.3 = (f32[3,3,72,128]{3,2,1,0:T(8,128)S(1)}, f32[3,3,72,128]{3,2,1,0:T(8,128)S(1)}, u32[]{:S(2)}, u32[]{:S(2)}) collective-permute-start(f32[3,3,72,128]{3,2,1,0:T(8,128)S(1)} %get-tuple-element.32), channel_id=1, source_target_pairs={{0,4},{4,0},{8,12},{12,8},{1,5},{5,1},{9,13},{13,9},{2,6},{6,2},{1... | collective-permute-start | bytes 995336 | tf_op jit(solution)/shard_map/ppermute | solution.py:327
  18.7 0.7 %collective-permute-start.4 = (f32[3,3,72,128]{3,2,1,0:T(8,128)S(1)}, f32[3,3,72,128]{3,2,1,0:T(8,128)S(1)}, u32[]{:S(2)}, u32[]{:S(2)}) collective-permute-start(f32[3,3,72,128]{3,2,1,0:T(8,128)S(1)} %get-tuple-element.35), channel_id=1, source_target_pairs={{4,8},{8,4},{5,9},{9,5},{6,10},{10,6},{7,11},{11,7},{20,24},{24,20... | collective-permute-start | bytes 995336 | tf_op jit(solution)/shard_map/ppermute | solution.py:327
  19.4 0.0 copy-start.5
  19.4 1.8 %collective-permute-start.5 = (f32[3,3,72,128]{3,2,1,0:T(8,128)S(1)}, f32[3,3,72,128]{3,2,1,0:T(8,128)S(1)}, u32[]{:S(2)}, u32[]{:S(2)}) collective-permute-start(f32[3,3,72,128]{3,2,1,0:T(8,128)S(1)} %get-tuple-element.36), channel_id=1, source_target_pairs={{0,4},{4,0},{8,12},{12,8},{1,5},{5,1},{9,13},{13,9},{2,6},{6,2},{1... | collective-permute-start | bytes 995336 | tf_op jit(solution)/shard_map/ppermute | solution.py:327
  21.2 0.9 %shard_map.67.w_ref = bf16[6,3,2,128,384]{4,3,2,1,0:T(8,128)(2,1)S(1)} custom-call(f32[3,3,3,96,96]{4,3,2,1,0:T(8,128)S(1)} %copy-done.4), custom_call_target="tpu_custom_call" | custom-call | tf_op jit(solution)/shard_map/pallas_call | solution.py:338
  22.2 0.0 copy-start.3
  22.2 0.8 %shard_map.69.w2_ref = bf16[5,3,2,128,384]{4,3,2,1,0:T(8,128)(2,1)S(1)} custom-call(f32[3,3,3,96,96]{4,3,2,1,0:T(8,128)S(1)} %copy-done.5), custom_call_target="tpu_custom_call" | custom-call | tf_op jit(solution)/shard_map/pallas_call | solution.py:338
  23.0 0.5 %copy-done.3 = f32[3,3,3,96,96]{4,3,2,1,0:T(8,128)S(1)} copy-done((f32[3,3,3,96,96]{4,3,2,1,0:T(8,128)S(1)}, f32[3,3,3,96,96]{4,3,2,1,0:T(8,128)}, u32[]{:S(2)}) %copy-start.3) | copy-done | bytes 995352
  23.5 0.6 %shard_map.70.w1_ref = bf16[4,3,2,128,384]{4,3,2,1,0:T(8,128)(2,1)S(1)} custom-call(f32[3,3,3,96,96]{4,3,2,1,0:T(8,128)S(1)} %copy-done.3), custom_call_target="tpu_custom_call" | custom-call | tf_op jit(solution)/shard_map/pallas_call | solution.py:338
  24.1 3.3 %collective-permute-done.3.ra1 = f32[3,3,72,128]{3,2,1,0:T(8,128)S(1)} collective-permute-done((f32[3,3,72,128]{3,2,1,0:T(8,128)S(1)}, f32[3,3,72,128]{3,2,1,0:T(8,128)S(1)}, u32[]{:S(2)}, u32[]{:S(2)}) %collective-permute-start.3) | collective-permute-done | bytes 331808 | tf_op jit(solution)/shard_map/ppermute | solution.py:327
  27.4 5.7 %shard_map.68.g_ref = f32[4,8,72,128]{3,2,1,0:T(8,128)S(1)} custom-call(s32[2]{0:T(128)S(1)} %copy-done.6, f32[4,4,72,128]{3,2,1,0:T(8,128)S(1)} %get-tuple-element.30.cp_ref, f32[3,3,72,128]{3,2,1,0:T(8,128)S(1)} %collective-permute-done.2.ra0, f32[3,3,72,128]{3,2,1,0:T(8,128)S(1)} %collective-permute-done.3.ra1, ...), custom_call_target="tpu_custom_call" | custom-call | tf_op jit(solution)/shard_map/pallas_call | solution.py:338
  33.1 0.4 %collective-permute-done.5.rb1 = f32[3,3,72,128]{3,2,1,0:T(8,128)S(1)} collective-permute-done((f32[3,3,72,128]{3,2,1,0:T(8,128)S(1)}, f32[3,3,72,128]{3,2,1,0:T(8,128)S(1)}, u32[]{:S(2)}, u32[]{:S(2)}) %collective-permute-start.5) | collective-permute-done | bytes 331808 | tf_op jit(solution)/shard_map/ppermute | solution.py:327
  33.5 9.2 %shard_map.71 = f32[4,4,64,96]{3,2,1,0:T(8,128)} custom-call(s32[2]{0:T(128)S(1)} %copy-done.6, f32[4,8,72,128]{3,2,1,0:T(8,128)S(1)} %shard_map.68.g_ref, f32[4,4,72,128]{3,2,1,0:T(8,128)S(1)} %get-tuple-element.33.s2_ref, f32[4,4,72,128]{3,2,1,0:T(8,128)S(1)} %get-tuple-element.34.s1_ref, f32[3,3,72,128]{3,2,1,0:T(8,128)S(1)} %collective-permute-done.4.rb0, ...), custom_call_target="tpu_custom_call" | custom-call | tf_op jit(solution)/shard_map/pallas_call | solution.py:338
  (11 shorter events, 0.0 us)
Async XLA Ops:
  0.7 7.7 %copy-start.6 = (s32[2]{0:T(128)S(1)}, s32[2]{0:T(128)}, u32[]{:S(2)}) copy-start(s32[2]{0:T(128)} %pad_add_fusion.par_ref) | copy-start | bytes 28
  3.3 9.6 %collective-permute-start = (f32[4,4,8,128]{3,2,1,0:T(8,128)}, f32[4,4,8,128]{3,2,1,0:T(8,128)S(1)}, u32[]{:S(2)}, u32[]{:S(2)}) collective-permute-start(f32[4,4,8,128]{3,2,1,0:T(8,128)} %get-tuple-element.21), channel_id=1, source_target_pairs={{1,2},{2,1},{5,6},{6,5},{9,10},{10,9},{13,14},{14,13},{17,18},{18,... | collective-permute-start | bytes 196616 | tf_op jit(solution)/shard_map/ppermute | solution.py:327
  4.0 8.9 %collective-permute-start.1 = (f32[4,4,8,128]{3,2,1,0:T(8,128)}, f32[4,4,8,128]{3,2,1,0:T(8,128)S(1)}, u32[]{:S(2)}, u32[]{:S(2)}) collective-permute-start(f32[4,4,8,128]{3,2,1,0:T(8,128)} %get-tuple-element.22), channel_id=1, source_target_pairs={{0,1},{1,0},{2,3},{3,2},{4,5},{5,4},{6,7},{7,6},{8,9},{9,8},{10,11... | collective-permute-start | bytes 196616 | tf_op jit(solution)/shard_map/ppermute | solution.py:327
  8.4 1.0 %copy-start = (f32[4,4,64,96]{3,2,1,0:T(8,128)S(1)}, f32[4,4,64,96]{3,2,1,0:T(8,128)}, u32[]{:S(2)}) copy-start(f32[4,4,64,96]{3,2,1,0:T(8,128)} %cot_ref.1) | copy-start | bytes 1179652
  9.4 1.0 %copy-start.1 = (f32[4,4,64,96]{3,2,1,0:T(8,128)S(1)}, f32[4,4,64,96]{3,2,1,0:T(8,128)}, u32[]{:S(2)}) copy-start(f32[4,4,64,96]{3,2,1,0:T(8,128)} %sec_ref.1) | copy-start | bytes 1179652
  10.4 1.0 %copy-start.2 = (f32[4,4,64,96]{3,2,1,0:T(8,128)S(1)}, f32[4,4,64,96]{3,2,1,0:T(8,128)}, u32[]{:S(2)}) copy-start(f32[4,4,64,96]{3,2,1,0:T(8,128)} %fst_ref.1) | copy-start | bytes 1179652
  12.9 8.3 %copy-start.4 = (f32[3,3,3,96,96]{4,3,2,1,0:T(8,128)S(1)}, f32[3,3,3,96,96]{4,3,2,1,0:T(8,128)}, u32[]{:S(2)}) copy-start(f32[3,3,3,96,96]{4,3,2,1,0:T(8,128)} %w_ref.3) | copy-start | bytes 2985988
  13.6 10.5 %collective-permute-start.2 = (f32[3,3,72,128]{3,2,1,0:T(8,128)S(1)}, f32[3,3,72,128]{3,2,1,0:T(8,128)S(1)}, u32[]{:S(2)}, u32[]{:S(2)}) collective-permute-start(f32[3,3,72,128]{3,2,1,0:T(8,128)S(1)} %get-tuple-element.31), channel_id=1, source_target_pairs={{4,8},{8,4},{5,9},{9,5},{6,10},{10,6},{7,11},{11,7},{20,24},{24,20... | collective-permute-start | bytes 995336 | tf_op jit(solution)/shard_map/ppermute | solution.py:327
  14.3 13.1 %collective-permute-start.3 = (f32[3,3,72,128]{3,2,1,0:T(8,128)S(1)}, f32[3,3,72,128]{3,2,1,0:T(8,128)S(1)}, u32[]{:S(2)}, u32[]{:S(2)}) collective-permute-start(f32[3,3,72,128]{3,2,1,0:T(8,128)S(1)} %get-tuple-element.32), channel_id=1, source_target_pairs={{0,4},{4,0},{8,12},{12,8},{1,5},{5,1},{9,13},{13,9},{2,6},{6,2},{1... | collective-permute-start | bytes 995336 | tf_op jit(solution)/shard_map/ppermute | solution.py:327
  18.7 14.4 %collective-permute-start.4 = (f32[3,3,72,128]{3,2,1,0:T(8,128)S(1)}, f32[3,3,72,128]{3,2,1,0:T(8,128)S(1)}, u32[]{:S(2)}, u32[]{:S(2)}) collective-permute-start(f32[3,3,72,128]{3,2,1,0:T(8,128)S(1)} %get-tuple-element.35), channel_id=1, source_target_pairs={{4,8},{8,4},{5,9},{9,5},{6,10},{10,6},{7,11},{11,7},{20,24},{24,20... | collective-permute-start | bytes 995336 | tf_op jit(solution)/shard_map/ppermute | solution.py:327
  19.4 2.7 %copy-start.5 = (f32[3,3,3,96,96]{4,3,2,1,0:T(8,128)S(1)}, f32[3,3,3,96,96]{4,3,2,1,0:T(8,128)}, u32[]{:S(2)}) copy-start(f32[3,3,3,96,96]{4,3,2,1,0:T(8,128)} %w_ref.4) | copy-start | bytes 2985988
  19.4 14.1 %collective-permute-start.5 = (f32[3,3,72,128]{3,2,1,0:T(8,128)S(1)}, f32[3,3,72,128]{3,2,1,0:T(8,128)S(1)}, u32[]{:S(2)}, u32[]{:S(2)}) collective-permute-start(f32[3,3,72,128]{3,2,1,0:T(8,128)S(1)} %get-tuple-element.36), channel_id=1, source_target_pairs={{0,4},{4,0},{8,12},{12,8},{1,5},{5,1},{9,13},{13,9},{2,6},{6,2},{1... | collective-permute-start | bytes 995336 | tf_op jit(solution)/shard_map/ppermute | solution.py:327
  22.2 1.3 %copy-start.3 = (f32[3,3,3,96,96]{4,3,2,1,0:T(8,128)S(1)}, f32[3,3,3,96,96]{4,3,2,1,0:T(8,128)}, u32[]{:S(2)}) copy-start(f32[3,3,3,96,96]{4,3,2,1,0:T(8,128)} %w_ref.5) | copy-start | bytes 2985988

commit v3 on v2

--- a/solution.py
+++ b/solution.py
@@ -105,15 +105,19 @@
     put(read_s1, rows - 1, low_b, 2)
 
 
-def pack_kernel(par_ref, cot_ref, sec_ref, fst_ref, ma0, ma1, mb0, mb1, cp_ref, s2_ref, s1_ref):
-    frames, rows, cols, chans = cot_ref.shape
+def pack_kernel(par_ref, cot_hbm, sec_hbm, fst_hbm, ma0, ma1, mb0, mb1, cp_ref, s2_ref, s1_ref, raw_ref, sems):
+    frames, rows, cols, chans = cot_hbm.shape
+    copies = [pltpu.make_async_copy(src, raw_ref.at[a], sems.at[a]) for a, src in enumerate((cot_hbm, sec_hbm, fst_hbm))]
+    for copy in copies:
+        copy.start()
     outs = (cp_ref, s2_ref, s1_ref)
-    blank = jnp.zeros((cols, LANES), F32)
+    for ref in outs:
+        ref[...] = jnp.zeros(ref.shape, F32)
     for a, ref in enumerate(outs):
+        copies[a].wait()
         for t in range(frames):
             for h in range(rows):
-                value = (cot_ref, sec_ref, fst_ref)[a][t, h]
-                ref[t, h, 0:cols] = blank
+                value = raw_ref[a, t, h]
                 ref[t, h, 0:cols, 0:chans] = silu_slope(value) if a else value
 
     def rows_out(*dst):
@@ -361,20 +365,21 @@
     edge = arr(frames, rows, SUB, LANES)
     own = arr(frames, rows, width, LANES)
     message = arr(3, 3, width, LANES)
-    fields = (cotangent, stored_second, stored_first)
+    fields = tuple(pltpu.with_memory_space_constraint(x, pltpu.HBM) for x in (cotangent, stored_second, stored_first))
     wp0, wp1 = call(
         edge_kernel,
         (edge, edge),
         (par,) + fields,
         [vmem(3, 2, frames, rows, SUB, chans), vmem(3, 2, frames, rows, SUB, LANES), pltpu.SemaphoreType.DMA((3, 2))],
         hbm=True,
-        vmem=66_700_000,
     )
     rw0, rw1 = swaps(wp0, wp1, "wa")
     packed = call(
         pack_kernel,
         (message,) * 4 + (own,) * 3,
         (par,) + fields,
+        [vmem(3, frames, rows, cols, chans), pltpu.SemaphoreType.DMA((3,))],
+        hbm=True,
     )
     ma0, ma1, mb0, mb1, cp, s2, s1 = call(
         functools.partial(corner_kernel, chans),

time: 43.2 us -> 39.5 us (0.914)
  local copies, waits for them, and re-layouts: 3.65 us -> 0.52 us
  other arithmetic: 0.66 us -> 0.07 us
    unnamed x14 -> x6, local copies, waits for them, and re-layouts: 3.65 us -> 0.52 us
    another operation x1, other arithmetic: 0.66 us -> 0.07 us  [local(): jnp.stack([(lax.axis_index('ha') + 1) % 2, (lax.axis_index('wa') + 1) % 2])]
  transfers between devices with their start and end apart: 6 -> 6, of which waited for: 2 -> 2; matrix products, arithmetic and copies ran while one was open for 0% -> 0% of each run, Pallas kernels for 22% -> 27%
where the time goes in v3:
time: 39.5 us; the launch traced here: 39.2 us
  Pallas kernels  22.2 us (56%)
  starting transfers between devices  12.6 us (32%)
  waiting for transfers between devices  3.74 us (9%)
  local copies, waits for them, and re-layouts  0.52 us (1%)
    pallas_call x8, Pallas kernels, call(): pl.pallas_call(body, out_shape=out_shape, in_specs=[SMEM_SPEC if a.dtype...  22.2 us
    ppermute x6, starting transfers between devices, swap(): return lax.ppermute(value, axis, pairs)  12.6 us
    ppermute x6, waiting for transfers between devices, swap(): return lax.ppermute(value, axis, pairs)  3.74 us
  transfers between devices with their start and end apart: 6, of which 2 were waited for; matrix products, arithmetic and copies ran while one was open for 0% of the time, Pallas kernels for 27%

profile of v3, /device:TPU:0, one launch (start us, length us, event | category | flops | bytes accessed | tf_op | source)
XLA Modules:
  0.0 39.2 jit_solution(17300347749707830877)
XLA Ops:
  0.0 0.1 pad_add_fusion.par_ref
  0.1 1.7 %shard_map.64 = (f32[4,4,8,128]{3,2,1,0:T(8,128)S(1)}, f32[4,4,8,128]{3,2,1,0:T(8,128)S(1)}) custom-call(s32[2]{0:T(128)S(1)} %pad_add_fusion.par_ref, f32[4,4,64,96]{3,2,1,0:T(8,128)} %cot_hbm.3, f32[4,4,64,96]{3,2,1,0:T(8,128)} %sec_hbm.3, f32[4,4,64,96]{3,2,1,0:T(8,128)} %fst_hbm.3), custom_call_target="tpu_custom_call" | custom-call | tf_op jit(solution)/shard_map/pallas_call | solution.py:342
  1.8 0.7 %collective-permute-start = (f32[4,4,8,128]{3,2,1,0:T(8,128)S(1)}, f32[4,4,8,128]{3,2,1,0:T(8,128)S(1)}, u32[]{:S(2)}, u32[]{:S(2)}) collective-permute-start(f32[4,4,8,128]{3,2,1,0:T(8,128)S(1)} %get-tuple-element.21), channel_id=1, source_target_pairs={{1,2},{2,1},{5,6},{6,5},{9,10},{10,9},{13,14},{14,13},{17,18},{18,... | collective-permute-start | bytes 196616 | tf_op jit(solution)/shard_map/ppermute | solution.py:331
  2.5 4.4 %collective-permute-start.1 = (f32[4,4,8,128]{3,2,1,0:T(8,128)S(1)}, f32[4,4,8,128]{3,2,1,0:T(8,128)S(1)}, u32[]{:S(2)}, u32[]{:S(2)}) collective-permute-start(f32[4,4,8,128]{3,2,1,0:T(8,128)S(1)} %get-tuple-element.22), channel_id=1, source_target_pairs={{0,1},{1,0},{2,3},{3,2},{4,5},{5,4},{6,7},{7,6},{8,9},{9,8},{10,11... | collective-permute-start | bytes 196616 | tf_op jit(solution)/shard_map/ppermute | solution.py:331
  6.9 2.5 %shard_map.65 = (f32[3,3,72,128]{3,2,1,0:T(8,128)S(1)}, f32[3,3,72,128]{3,2,1,0:T(8,128)S(1)}, f32[3,3,72,128]{3,2,1,0:T(8,128)S(1)}, f32[3,3,72,128]{3,2,1,0:T(...) custom-call(s32[2]{0:T(128)S(1)} %pad_add_fusion.par_ref, ...), custom_call_target="tpu_custom_call" | custom-call | tf_op jit(solution)/shard_map/pallas_call | solution.py:342
  9.4 0.0 collective-permute-done.rw0
  9.4 0.0 collective-permute-done.1.rw1
  9.4 0.0 copy-start.1
  9.4 0.7 %shard_map.66 = (f32[3,3,72,128]{3,2,1,0:T(8,128)S(1)}, f32[3,3,72,128]{3,2,1,0:T(8,128)S(1)}, f32[3,3,72,128]{3,2,1,0:T(8,128)S(1)}, f32[3,3,72,128]{3,2,1,0:T(...) custom-call(s32[2]{0:T(128)S(1)} %pad_add_fusion.par_ref, ...), custom_call_target="tpu_custom_call", output_to_operand_aliasing={{0}: (3, {}), {1}: (4, {}), {2}: (5, {}), {3}: (6, {}), {4}... | custom-call | tf_op jit(solution)/shard_map/pallas_call | solution.py:342
  10.1 0.7 %collective-permute-start.2 = (f32[3,3,72,128]{3,2,1,0:T(8,128)S(1)}, f32[3,3,72,128]{3,2,1,0:T(8,128)S(1)}, u32[]{:S(2)}, u32[]{:S(2)}) collective-permute-start(f32[3,3,72,128]{3,2,1,0:T(8,128)S(1)} %get-tuple-element.31), channel_id=1, source_target_pairs={{4,8},{8,4},{5,9},{9,5},{6,10},{10,6},{7,11},{11,7},{20,24},{24,20... | collective-permute-start | bytes 995336 | tf_op jit(solution)/shard_map/ppermute | solution.py:331
  10.8 4.4 %collective-permute-start.3 = (f32[3,3,72,128]{3,2,1,0:T(8,128)S(1)}, f32[3,3,72,128]{3,2,1,0:T(8,128)S(1)}, u32[]{:S(2)}, u32[]{:S(2)}) collective-permute-start(f32[3,3,72,128]{3,2,1,0:T(8,128)S(1)} %get-tuple-element.32), channel_id=1, source_target_pairs={{0,4},{4,0},{8,12},{12,8},{1,5},{5,1},{9,13},{13,9},{2,6},{6,2},{1... | collective-permute-start | bytes 995336 | tf_op jit(solution)/shard_map/ppermute | solution.py:331
  15.2 0.7 %collective-permute-start.4 = (f32[3,3,72,128]{3,2,1,0:T(8,128)S(1)}, f32[3,3,72,128]{3,2,1,0:T(8,128)S(1)}, u32[]{:S(2)}, u32[]{:S(2)}) collective-permute-start(f32[3,3,72,128]{3,2,1,0:T(8,128)S(1)} %get-tuple-element.35), channel_id=1, source_target_pairs={{4,8},{8,4},{5,9},{9,5},{6,10},{10,6},{7,11},{11,7},{20,24},{24,20... | collective-permute-start | bytes 995336 | tf_op jit(solution)/shard_map/ppermute | solution.py:331
  15.9 0.0 copy-start.2
  15.9 1.8 %collective-permute-start.5 = (f32[3,3,72,128]{3,2,1,0:T(8,128)S(1)}, f32[3,3,72,128]{3,2,1,0:T(8,128)S(1)}, u32[]{:S(2)}, u32[]{:S(2)}) collective-permute-start(f32[3,3,72,128]{3,2,1,0:T(8,128)S(1)} %get-tuple-element.36), channel_id=1, source_target_pairs={{0,4},{4,0},{8,12},{12,8},{1,5},{5,1},{9,13},{13,9},{2,6},{6,2},{1... | collective-permute-start | bytes 995336 | tf_op jit(solution)/shard_map/ppermute | solution.py:331
  17.7 0.9 %shard_map.67.w_ref = bf16[6,3,2,128,384]{4,3,2,1,0:T(8,128)(2,1)S(1)} custom-call(f32[3,3,3,96,96]{4,3,2,1,0:T(8,128)S(1)} %copy-done.1), custom_call_target="tpu_custom_call" | custom-call | tf_op jit(solution)/shard_map/pallas_call | solution.py:342
  18.7 0.0 copy-start
  18.7 0.8 %shard_map.69.w2_ref = bf16[5,3,2,128,384]{4,3,2,1,0:T(8,128)(2,1)S(1)} custom-call(f32[3,3,3,96,96]{4,3,2,1,0:T(8,128)S(1)} %copy-done.2), custom_call_target="tpu_custom_call" | custom-call | tf_op jit(solution)/shard_map/pallas_call | solution.py:342
  19.5 0.5 %copy-done = f32[3,3,3,96,96]{4,3,2,1,0:T(8,128)S(1)} copy-done((f32[3,3,3,96,96]{4,3,2,1,0:T(8,128)S(1)}, f32[3,3,3,96,96]{4,3,2,1,0:T(8,128)}, u32[]{:S(2)}) %copy-start) | copy-done | bytes 995352
  20.0 0.6 %shard_map.70.w1_ref = bf16[4,3,2,128,384]{4,3,2,1,0:T(8,128)(2,1)S(1)} custom-call(f32[3,3,3,96,96]{4,3,2,1,0:T(8,128)S(1)} %copy-done), custom_call_target="tpu_custom_call" | custom-call | tf_op jit(solution)/shard_map/pallas_call | solution.py:342
  20.6 0.0 collective-permute-done.2.ra0
  20.6 3.3 %collective-permute-done.3.ra1 = f32[3,3,72,128]{3,2,1,0:T(8,128)S(1)} collective-permute-done((f32[3,3,72,128]{3,2,1,0:T(8,128)S(1)}, f32[3,3,72,128]{3,2,1,0:T(8,128)S(1)}, u32[]{:S(2)}, u32[]{:S(2)}) %collective-permute-start.3) | collective-permute-done | bytes 331808 | tf_op jit(solution)/shard_map/ppermute | solution.py:331
  23.9 5.7 %shard_map.68.g_ref = f32[4,8,72,128]{3,2,1,0:T(8,128)S(1)} custom-call(s32[2]{0:T(128)S(1)} %pad_add_fusion.par_ref, f32[4,4,72,128]{3,2,1,0:T(8,128)S(1)} %get-tuple-element.30.cp_ref, f32[3,3,72,128]{3,2,1,0:T(8,128)S(1)} %collective-permute-done.2.ra0, f32[3,3,72,128]{3,2,1,0:T(8,128)S(1)} %collective-permute-done.3.ra1, ...), custom_call_target="tpu_custom_call" | custom-call | tf_op jit(solution)/shard_map/pallas_call | solution.py:342
  29.6 0.5 %collective-permute-done.5.rb1 = f32[3,3,72,128]{3,2,1,0:T(8,128)S(1)} collective-permute-done((f32[3,3,72,128]{3,2,1,0:T(8,128)S(1)}, f32[3,3,72,128]{3,2,1,0:T(8,128)S(1)}, u32[]{:S(2)}, u32[]{:S(2)}) %collective-permute-start.5) | collective-permute-done | bytes 331808 | tf_op jit(solution)/shard_map/ppermute | solution.py:331
  30.0 9.2 %shard_map.71 = f32[4,4,64,96]{3,2,1,0:T(8,128)} custom-call(s32[2]{0:T(128)S(1)} %pad_add_fusion.par_ref, f32[4,8,72,128]{3,2,1,0:T(8,128)S(1)} %shard_map.68.g_ref, f32[4,4,72,128]{3,2,1,0:T(8,128)S(1)} %get-tuple-element.33.s2_ref, f32[4,4,72,128]{3,2,1,0:T(8,128)S(1)} %get-tuple-element.34.s1_ref, f32[3,3,72,128]{3,2,1,0:T(8,128)S(1)} %collective-permute-done.4.rb0, ...), custom_call_target="tpu_custom_call" | custom-call | tf_op jit(solution)/shard_map/pallas_call | solution.py:342
  (3 shorter events, 0.0 us)
Async XLA Ops:
  1.8 7.6 %collective-permute-start = (f32[4,4,8,128]{3,2,1,0:T(8,128)S(1)}, f32[4,4,8,128]{3,2,1,0:T(8,128)S(1)}, u32[]{:S(2)}, u32[]{:S(2)}) collective-permute-start(f32[4,4,8,128]{3,2,1,0:T(8,128)S(1)} %get-tuple-element.21), channel_id=1, source_target_pairs={{1,2},{2,1},{5,6},{6,5},{9,10},{10,9},{13,14},{14,13},{17,18},{18,... | collective-permute-start | bytes 196616 | tf_op jit(solution)/shard_map/ppermute | solution.py:331
  2.5 6.9 %collective-permute-start.1 = (f32[4,4,8,128]{3,2,1,0:T(8,128)S(1)}, f32[4,4,8,128]{3,2,1,0:T(8,128)S(1)}, u32[]{:S(2)}, u32[]{:S(2)}) collective-permute-start(f32[4,4,8,128]{3,2,1,0:T(8,128)S(1)} %get-tuple-element.22), channel_id=1, source_target_pairs={{0,1},{1,0},{2,3},{3,2},{4,5},{5,4},{6,7},{7,6},{8,9},{9,8},{10,11... | collective-permute-start | bytes 196616 | tf_op jit(solution)/shard_map/ppermute | solution.py:331
  9.4 8.3 %copy-start.1 = (f32[3,3,3,96,96]{4,3,2,1,0:T(8,128)S(1)}, f32[3,3,3,96,96]{4,3,2,1,0:T(8,128)}, u32[]{:S(2)}) copy-start(f32[3,3,3,96,96]{4,3,2,1,0:T(8,128)} %w_ref.3) | copy-start | bytes 2985988
  10.1 10.5 %collective-permute-start.2 = (f32[3,3,72,128]{3,2,1,0:T(8,128)S(1)}, f32[3,3,72,128]{3,2,1,0:T(8,128)S(1)}, u32[]{:S(2)}, u32[]{:S(2)}) collective-permute-start(f32[3,3,72,128]{3,2,1,0:T(8,128)S(1)} %get-tuple-element.31), channel_id=1, source_target_pairs={{4,8},{8,4},{5,9},{9,5},{6,10},{10,6},{7,11},{11,7},{20,24},{24,20... | collective-permute-start | bytes 995336 | tf_op jit(solution)/shard_map/ppermute | solution.py:331
  10.8 13.1 %collective-permute-start.3 = (f32[3,3,72,128]{3,2,1,0:T(8,128)S(1)}, f32[3,3,72,128]{3,2,1,0:T(8,128)S(1)}, u32[]{:S(2)}, u32[]{:S(2)}) collective-permute-start(f32[3,3,72,128]{3,2,1,0:T(8,128)S(1)} %get-tuple-element.32), channel_id=1, source_target_pairs={{0,4},{4,0},{8,12},{12,8},{1,5},{5,1},{9,13},{13,9},{2,6},{6,2},{1... | collective-permute-start | bytes 995336 | tf_op jit(solution)/shard_map/ppermute | solution.py:331
  15.2 14.3 %collective-permute-start.4 = (f32[3,3,72,128]{3,2,1,0:T(8,128)S(1)}, f32[3,3,72,128]{3,2,1,0:T(8,128)S(1)}, u32[]{:S(2)}, u32[]{:S(2)}) collective-permute-start(f32[3,3,72,128]{3,2,1,0:T(8,128)S(1)} %get-tuple-element.35), channel_id=1, source_target_pairs={{4,8},{8,4},{5,9},{9,5},{6,10},{10,6},{7,11},{11,7},{20,24},{24,20... | collective-permute-start | bytes 995336 | tf_op jit(solution)/shard_map/ppermute | solution.py:331
  15.9 2.7 %copy-start.2 = (f32[3,3,3,96,96]{4,3,2,1,0:T(8,128)S(1)}, f32[3,3,3,96,96]{4,3,2,1,0:T(8,128)}, u32[]{:S(2)}) copy-start(f32[3,3,3,96,96]{4,3,2,1,0:T(8,128)} %w_ref.4) | copy-start | bytes 2985988
  15.9 14.1 %collective-permute-start.5 = (f32[3,3,72,128]{3,2,1,0:T(8,128)S(1)}, f32[3,3,72,128]{3,2,1,0:T(8,128)S(1)}, u32[]{:S(2)}, u32[]{:S(2)}) collective-permute-start(f32[3,3,72,128]{3,2,1,0:T(8,128)S(1)} %get-tuple-element.36), channel_id=1, source_target_pairs={{0,4},{4,0},{8,12},{12,8},{1,5},{5,1},{9,13},{13,9},{2,6},{6,2},{1... | collective-permute-start | bytes 995336 | tf_op jit(solution)/shard_map/ppermute | solution.py:331
  18.7 1.3 %copy-start = (f32[3,3,3,96,96]{4,3,2,1,0:T(8,128)S(1)}, f32[3,3,3,96,96]{4,3,2,1,0:T(8,128)}, u32[]{:S(2)}) copy-start(f32[3,3,3,96,96]{4,3,2,1,0:T(8,128)} %w_ref.5) | copy-start | bytes 2985988

commit v4 on v3

--- a/solution.py
+++ b/solution.py
@@ -6,6 +6,7 @@
 from jax.experimental import pallas as pl
 from jax.experimental.pallas import tpu as pltpu
 from jax.sharding import PartitionSpec as P
+
 
 LANES = 128
 SUB = 8
@@ -53,59 +54,7 @@
     return frames + [jnp.where(lane < chans, fourth, 0.0)]
 
 
-def edge_kernel(par_ref, cot_hbm, sec_hbm, fst_hbm, wp0, wp1, raw_ref, pad_ref, sems):
-    frames, rows, cols, chans = cot_hbm.shape
-    copies = []
-    for a, src in enumerate((cot_hbm, sec_hbm, fst_hbm)):
-        for side, start in enumerate((0, cols - SUB)):
-            copies.append(
-                pltpu.make_async_copy(src.at[:, :, pl.ds(start, SUB), :], raw_ref.at[a, side], sems.at[a, side])
-            )
-            copies[-1].start()
-    pad_ref[...] = jnp.zeros(pad_ref.shape, F32)
-    for copy in copies:
-        copy.wait()
-    pad_ref[0, :, :, :, :, 0:chans] = raw_ref[0]
-    pad_ref[1:3, :, :, :, :, 0:chans] = silu_slope(raw_ref[1:3])
-
-    def cols_out(left, right):
-        sub = sub_of((SUB, LANES))
-        for t in range(frames):
-            for h in range(rows):
-                c0, a0, b0 = (pad_ref[a, 0, t, h] for a in range(3))
-                c7, a7, b7 = (pad_ref[a, 1, t, h] for a in range(3))
-                right[t, h] = jnp.where(
-                    sub >= 5, c7, jnp.where((sub == 2) | (sub == 3), roll(a7, 4, 0), jnp.where(sub == 1, roll(b7, 2, 0), 0.0))
-                )
-                left[t, h] = jnp.where(
-                    sub < 3, c0, jnp.where((sub == 4) | (sub == 5), roll(a0, 4, 0), jnp.where(sub == 6, roll(b0, 6, 0), 0.0))
-                )
-
-    @pl.when(par_ref[1] == 0)
-    def _():
-        cols_out(wp1, wp0)
-
-    @pl.when(par_ref[1] != 0)
-    def _():
-        cols_out(wp0, wp1)
-
-
-def put_rows(read_cot, read_s2, read_s1, rows, top_a, top_b, low_a, low_b, span, chans):
-    def put(read, h, dst, at):
-        for g, val in enumerate(group_frames([read(t, h) for t in range(4)], chans)):
-            dst[g, at, span] = val
-
-    for r in range(3):
-        put(read_cot, r, top_a, r)
-        put(read_cot, rows - 3 + r, low_a, r)
-    for r in range(2):
-        put(read_s2, r, top_b, r)
-        put(read_s2, rows - 2 + r, low_b, r)
-    put(read_s1, 0, top_b, 2)
-    put(read_s1, rows - 1, low_b, 2)
-
-
-def pack_kernel(par_ref, cot_hbm, sec_hbm, fst_hbm, ma0, ma1, mb0, mb1, cp_ref, s2_ref, s1_ref, raw_ref, sems):
+def pack_kernel(par_ref, cot_hbm, sec_hbm, fst_hbm, ma0, ma1, mb0, mb1, wp0, wp1, cp_ref, s2_ref, s1_ref, raw_ref, sems):
     frames, rows, cols, chans = cot_hbm.shape
     copies = [pltpu.make_async_copy(src, raw_ref.at[a], sems.at[a]) for a, src in enumerate((cot_hbm, sec_hbm, fst_hbm))]
     for copy in copies:
@@ -120,9 +69,19 @@
                 value = raw_ref[a, t, h]
                 ref[t, h, 0:cols, 0:chans] = silu_slope(value) if a else value
 
-    def rows_out(*dst):
-        reads = [lambda t, h, ref=ref: ref[t, h, 0:cols] for ref in outs]
-        put_rows(*reads, rows, *dst, slice(0, cols), chans)
+    def rows_out(top_a, top_b, low_a, low_b):
+        def put(src, h, dst, at):
+            for g, val in enumerate(group_frames([src[t, h, 0:cols] for t in range(frames)], chans)):
+                dst[g, at] = val
+
+        for r in range(3):
+            put(cp_ref, r, top_a, r)
+            put(cp_ref, rows - 3 + r, low_a, r)
+        for r in range(2):
+            put(s2_ref, r, top_b, r)
+            put(s2_ref, rows - 2 + r, low_b, r)
+        put(s1_ref, 0, top_b, 2)
+        put(s1_ref, rows - 1, low_b, 2)
 
     @pl.when(par_ref[0] == 0)
     def _():
@@ -132,10 +91,31 @@
     def _():
         rows_out(ma0, mb0, ma1, mb1)
 
-
-def corner_kernel(chans, par_ref, rw0, rw1, _a0, _a1, _b0, _b1, _c, _s2, _s1, ma0, ma1, mb0, mb1, cp_ref, s2_ref, s1_ref):
+    def cols_out(left, right):
+        sub = sub_of((SUB, LANES))
+        for t in range(frames):
+            for h in range(rows):
+                c0, a0, b0 = (ref[t, h, 0:SUB] for ref in outs)
+                c7, a7, b7 = (ref[t, h, cols - SUB : cols] for ref in outs)
+                right[t, h] = jnp.where(
+                    sub >= 5, c7, jnp.where((sub == 2) | (sub == 3), roll(a7, 4, 0), jnp.where(sub == 1, roll(b7, 2, 0), 0.0))
+                )
+                left[t, h] = jnp.where(
+                    sub < 3, c0, jnp.where((sub == 4) | (sub == 5), roll(a0, 4, 0), jnp.where(sub == 6, roll(b0, 6, 0), 0.0))
+                )
+
+    @pl.when(par_ref[1] == 0)
+    def _():
+        cols_out(wp1, wp0)
+
+    @pl.when(par_ref[1] != 0)
+    def _():
+        cols_out(wp0, wp1)
+
+
+def corner_kernel(chans, par_ref, rw0, rw1, _c, _s2, _s1, _b0, _b1, mc0, mc1, cp_ref, s2_ref, s1_ref, _mb0, _mb1):
     frames, rows = rw0.shape[:2]
-    cols = ma0.shape[2] - SUB
+    cols = cp_ref.shape[2] - SUB
     even = par_ref[1] == 0
     sub = sub_of((SUB, LANES))
     for t in range(frames):
@@ -146,17 +126,27 @@
             s2_ref[t, h, cols:] = jnp.where(sub < 2, roll(right, 4, 0), jnp.where(sub >= 6, roll(left, 4, 0), 0.0))
             s1_ref[t, h, cols:] = jnp.where(sub == 0, roll(right, 2, 0), jnp.where(sub == 7, roll(left, 6, 0), 0.0))
 
-    def rows_out(*dst):
-        reads = [lambda t, h, ref=ref: ref[t, h, cols:] for ref in (cp_ref, s2_ref, s1_ref)]
-        put_rows(*reads, rows, *dst, slice(cols, cols + SUB), chans)
+    def out(top, low):
+        def put(src, h, dst, at):
+            for g, val in enumerate(group_frames([src[t, h, cols:] for t in range(frames)], chans)):
+                dst[g, at] = val
+
+        for r in range(3):
+            put(cp_ref, r, top, r)
+            put(cp_ref, rows - 3 + r, low, r)
+        for r in range(2):
+            put(s2_ref, r, top, 3 + r)
+            put(s2_ref, rows - 2 + r, low, 3 + r)
+        put(s1_ref, 0, top, 5)
+        put(s1_ref, rows - 1, low, 5)
 
     @pl.when(par_ref[0] == 0)
     def _():
-        rows_out(ma1, mb1, ma0, mb0)
+        out(mc1, mc0)
 
     @pl.when(par_ref[0] != 0)
     def _():
-        rows_out(ma0, mb0, ma1, mb1)
+        out(mc0, mc1)
 
 
 def weight_kernel(wanted, w_ref, out_ref):
@@ -273,12 +263,15 @@
     return ungroup_frames([jnp.where(par == 0, from_even[g, r], from_odd[g, r]) for g in range(3)], chans)
 
 
-def third_kernel(chans, par_ref, cp_ref, ra0, ra1, w_ref, out_ref, x_ref, s_ref, y_ref):
+def third_kernel(chans, par_ref, cp_ref, ra0, ra1, rc0, rc1, w_ref, out_ref, x_ref, s_ref, y_ref):
     rows, width = cp_ref.shape[1:3]
+    cols = width - SUB
     for r in range(3):
-        for at, even, odd in ((r, ra1, ra0), (r + 3, ra0, ra1)):
+        for at, even, odd, ceven, codd in ((r, ra1, ra0, rc1, rc0), (r + 3, ra0, ra1, rc0, rc1)):
             for t, frame in enumerate(halo_rows(chans, par_ref[0], even, odd, r)):
-                x_ref[t, at] = frame
+                x_ref[t, at, 0:cols] = frame
+            for t, frame in enumerate(halo_rows(chans, par_ref[0], ceven, codd, r)):
+                x_ref[t, at, cols:] = frame
 
     def read(t, r, at):
         if 3 <= r < 3 + rows:
@@ -291,14 +284,16 @@
     conv(read, rows, width, s_ref, y_ref, w_ref, emit)
 
 
-def last_kernel(chans, par_ref, g_ref, s2_ref, s1_ref, rb0, rb1, w2_ref, w1_ref, out_hbm,
+def last_kernel(chans, par_ref, g_ref, s2_ref, s1_ref, rb0, rb1, rc0, rc1, w2_ref, w1_ref, out_hbm,
                 e_ref, x1_ref, s_ref, y_ref, stage_ref, sems):
     frames, rows, width, _ = s2_ref.shape
     cols = width - SUB
     for r in range(3):
-        for side, even, odd in ((0, rb1, rb0), (1, rb0, rb1)):
+        for side, even, odd, ceven, codd in ((0, rb1, rb0, rc1, rc0), (1, rb0, rb1, rc0, rc1)):
             for t, frame in enumerate(halo_rows(chans, par_ref[0], even, odd, r)):
-                e_ref[side, r, t] = frame
+                e_ref[side, r, t, 0:cols] = frame
+            for t, frame in enumerate(halo_rows(chans, par_ref[0], ceven, codd, 3 + r)):
+                e_ref[side, r, t, cols:] = frame
 
     def slope2(t, r, at):
         if 2 <= r < 2 + rows:
@@ -332,7 +327,9 @@
 
 
 def swaps(first, second, axis):
-    got = swap(first, axis, 0), swap(second, axis, 1)
+    got = []
+    for which, value in enumerate((first, second)):
+        got.append(swap(value, axis, which))
     return got
 
 
@@ -351,7 +348,7 @@
     )(*args)
 
 
-def local(cotangent, stored_first, stored_second, w_first, w_second, w_third):
+def program(cotangent, stored_first, stored_second, w_first, w_second, w_third):
     frames, rows, cols, chans = cotangent.shape
     width = cols + SUB
     par = jnp.stack([(lax.axis_index("ha") + 1) % 2, (lax.axis_index("wa") + 1) % 2]).astype(jnp.int32)
@@ -364,30 +361,25 @@
 
     edge = arr(frames, rows, SUB, LANES)
     own = arr(frames, rows, width, LANES)
-    message = arr(3, 3, width, LANES)
+    message = arr(3, 3, cols, LANES)
+    corner = arr(3, 6, SUB, LANES)
     fields = tuple(pltpu.with_memory_space_constraint(x, pltpu.HBM) for x in (cotangent, stored_second, stored_first))
-    wp0, wp1 = call(
-        edge_kernel,
-        (edge, edge),
-        (par,) + fields,
-        [vmem(3, 2, frames, rows, SUB, chans), vmem(3, 2, frames, rows, SUB, LANES), pltpu.SemaphoreType.DMA((3, 2))],
-        hbm=True,
-    )
-    rw0, rw1 = swaps(wp0, wp1, "wa")
-    packed = call(
+    ma0, ma1, mb0, mb1, wp0, wp1, *kept = call(
         pack_kernel,
-        (message,) * 4 + (own,) * 3,
+        (message,) * 4 + (edge,) * 2 + (own,) * 3,
         (par,) + fields,
         [vmem(3, frames, rows, cols, chans), pltpu.SemaphoreType.DMA((3,))],
         hbm=True,
     )
-    ma0, ma1, mb0, mb1, cp, s2, s1 = call(
+    ra0, ra1 = swaps(ma0, ma1, "ha")
+    rw0, rw1 = swaps(wp0, wp1, "wa")
+    mc0, mc1, cp, s2, s1, mb0, mb1 = call(
         functools.partial(corner_kernel, chans),
-        (message,) * 4 + (own,) * 3,
-        (par, rw0, rw1) + tuple(packed),
-        alias={n + 3: n for n in range(7)},
-    )
-    ra0, ra1 = swaps(ma0, ma1, "ha")
+        (corner,) * 2 + (own,) * 3 + (message,) * 2,
+        (par, rw0, rw1, *kept, mb0, mb1),
+        alias={n + 3: n + 2 for n in range(5)},
+    )
+    rc0, rc1 = swaps(mc0, mc1, "ha")
     rb0, rb1 = swaps(mb0, mb1, "ha")
 
     def prepare(w, size):
@@ -407,13 +399,13 @@
     grad = call(
         functools.partial(third_kernel, chans),
         arr(frames, rows + 4, width, LANES),
-        (par, cp, ra0, ra1, u3),
+        (par, cp, ra0, ra1, rc0, rc1, u3),
         [vmem(frames, 6, width, LANES)] + scratch(rows),
     )
     return call(
         functools.partial(last_kernel, chans),
         arr(frames, rows, cols, chans),
-        (par, grad, s2, s1, rb0, rb1, u2, u1),
+        (par, grad, s2, s1, rb0, rb1, rc0, rc1, u2, u1),
         [vmem(2, 3, frames, width, LANES), vmem(frames, rows + 2, width, LANES)]
         + scratch((rows + 2) // 2)
         + [vmem(frames, rows, cols, chans), pltpu.SemaphoreType.DMA((frames,))],
@@ -431,4 +423,4 @@
         P(),
     )
     out_specs = P("clip", "ha", "wa", None)
-    return jax.shard_map(local, mesh=mesh, in_specs=in_specs, out_specs=out_specs, check_vma=False)
+    return jax.shard_map(program, mesh=mesh, in_specs=in_specs, out_specs=out_specs, check_vma=False)

time: 39.5 us -> 46.2 us (1.17)
  starting transfers between devices: 12.6 us -> 24.7 us
  waiting for transfers between devices: 3.74 us -> 0.02 us
  Pallas kernels: 22.2 us -> 20.5 us
    ppermute x6 -> x8, starting transfers between devices: 12.6 us -> 24.7 us  [swap(): return lax.ppermute(value, axis, pairs)]
    ppermute x6 -> x8, waiting for transfers between devices: 3.74 us -> 0.02 us  [swap(): return lax.ppermute(value, axis, pairs)]
    pallas_call x8 -> x7, Pallas kernels: 22.2 us -> 20.5 us  [call(): pl.pallas_call(body, out_shape=out_shape, in_specs=[SMEM_SPEC if a.dtype...]
  transfers between devices with their start and end apart: 6 -> 8, of which waited for: 2 -> 0; matrix products, arithmetic and copies ran while one was open for 0% -> 0% of each run, Pallas kernels for 27% -> 19%
where the time goes in v4:
time: 46.2 us; the launch traced here: 46 us
  starting transfers between devices  24.7 us (53%)
  Pallas kernels  20.5 us (44%)
  local copies, waits for them, and re-layouts  0.52 us (1%)
    ppermute x8, starting transfers between devices, swap(): return lax.ppermute(value, axis, pairs)  24.7 us
    pallas_call x7, Pallas kernels, call(): pl.pallas_call(body, out_shape=out_shape, in_specs=[SMEM_SPEC if a.dtype...  20.5 us
  transfers between devices with their start and end apart: 8, of which 0 were waited for; matrix products, arithmetic and copies ran while one was open for 0% of the time, Pallas kernels for 19%

profile of v4, /device:TPU:0, one launch (start us, length us, event | category | flops | bytes accessed | tf_op | source)
XLA Modules:
  0.0 46.0 jit_solution(9646199992945386376)
XLA Ops:
  0.0 0.1 pad_add_fusion.par_ref
  0.1 2.5 %shard_map.64 = (f32[3,3,64,128]{3,2,1,0:T(8,128)S(1)}, f32[3,3,64,128]{3,2,1,0:T(8,128)S(1)}, f32[3,3,64,128]{3,2,1,0:T(8,128)S(1)}, f32[3,3,64,128]{3,2,1,0:T(...) custom-call(s32[2]{0:T(128)S(1)} %pad_add_fusion.par_ref, ...), custom_call_target="tpu_custom_call" | custom-call | tf_op jit(solution)/shard_map/pallas_call | solution.py:339
  2.6 0.0 copy-start.1
  2.6 0.8 %collective-permute-start = (f32[4,4,8,128]{3,2,1,0:T(8,128)S(1)}, f32[4,4,8,128]{3,2,1,0:T(8,128)S(1)}, u32[]{:S(2)}, u32[]{:S(2)}) collective-permute-start(f32[4,4,8,128]{3,2,1,0:T(8,128)S(1)} %get-tuple-element.21), channel_id=1, source_target_pairs={{1,2},{2,1},{5,6},{6,5},{9,10},{10,9},{13,14},{14,13},{17,18},{18,... | collective-permute-start | bytes 196616 | tf_op jit(solution)/shard_map/ppermute | solution.py:326
  3.4 4.4 %collective-permute-start.1 = (f32[4,4,8,128]{3,2,1,0:T(8,128)S(1)}, f32[4,4,8,128]{3,2,1,0:T(8,128)S(1)}, u32[]{:S(2)}, u32[]{:S(2)}) collective-permute-start(f32[4,4,8,128]{3,2,1,0:T(8,128)S(1)} %get-tuple-element.22), channel_id=1, source_target_pairs={{0,1},{1,0},{2,3},{3,2},{4,5},{5,4},{6,7},{7,6},{8,9},{9,8},{10,11... | collective-permute-start | bytes 196616 | tf_op jit(solution)/shard_map/ppermute | solution.py:326
  7.8 0.7 %collective-permute-start.2 = (f32[3,3,64,128]{3,2,1,0:T(8,128)S(1)}, f32[3,3,64,128]{3,2,1,0:T(8,128)S(1)}, u32[]{:S(2)}, u32[]{:S(2)}) collective-permute-start(f32[3,3,64,128]{3,2,1,0:T(8,128)S(1)} %get-tuple-element.29), channel_id=1, source_target_pairs={{4,8},{8,4},{5,9},{9,5},{6,10},{10,6},{7,11},{11,7},{20,24},{24,20... | collective-permute-start | bytes 884744 | tf_op jit(solution)/shard_map/ppermute | solution.py:326
  8.5 4.4 %collective-permute-start.3 = (f32[3,3,64,128]{3,2,1,0:T(8,128)S(1)}, f32[3,3,64,128]{3,2,1,0:T(8,128)S(1)}, u32[]{:S(2)}, u32[]{:S(2)}) collective-permute-start(f32[3,3,64,128]{3,2,1,0:T(8,128)S(1)} %get-tuple-element.30), channel_id=1, source_target_pairs={{0,4},{4,0},{8,12},{12,8},{1,5},{5,1},{9,13},{13,9},{2,6},{6,2},{1... | collective-permute-start | bytes 884744 | tf_op jit(solution)/shard_map/ppermute | solution.py:326
  12.9 0.0 collective-permute-done.rw0
  12.9 0.0 collective-permute-done.1.rw1
  12.9 0.7 %shard_map.65 = (f32[3,6,8,128]{3,2,1,0:T(8,128)S(1)}, f32[3,6,8,128]{3,2,1,0:T(8,128)S(1)}, f32[4,4,72,128]{3,2,1,0:T(8,128)S(1)}, f32[4,4,72,128]{3,2,1,0:T(8,...) custom-call(s32[2]{0:T(128)S(1)} %pad_add_fusion.par_ref, ...), custom_call_target="tpu_custom_call", output_to_operand_aliasing={{2}: (3, {}), {3}: (4, {}), {4}: (5, {}), {5}: (6, {}), {6}... | custom-call | tf_op jit(solution)/shard_map/pallas_call | solution.py:339
  13.6 0.7 %collective-permute-start.6 = (f32[3,3,64,128]{3,2,1,0:T(8,128)S(1)}, f32[3,3,64,128]{3,2,1,0:T(8,128)S(1)}, u32[]{:S(2)}, u32[]{:S(2)}) collective-permute-start(f32[3,3,64,128]{3,2,1,0:T(8,128)S(1)} %get-tuple-element.35), channel_id=1, source_target_pairs={{4,8},{8,4},{5,9},{9,5},{6,10},{10,6},{7,11},{11,7},{20,24},{24,20... | collective-permute-start | bytes 884744 | tf_op jit(solution)/shard_map/ppermute | solution.py:326
  14.3 1.8 %collective-permute-start.7 = (f32[3,3,64,128]{3,2,1,0:T(8,128)S(1)}, f32[3,3,64,128]{3,2,1,0:T(8,128)S(1)}, u32[]{:S(2)}, u32[]{:S(2)}) collective-permute-start(f32[3,3,64,128]{3,2,1,0:T(8,128)S(1)} %get-tuple-element.36), channel_id=1, source_target_pairs={{0,4},{4,0},{8,12},{12,8},{1,5},{5,1},{9,13},{13,9},{2,6},{6,2},{1... | collective-permute-start | bytes 884744 | tf_op jit(solution)/shard_map/ppermute | solution.py:326
  16.1 0.7 %collective-permute-start.4 = (f32[3,6,8,128]{3,2,1,0:T(8,128)S(1)}, f32[3,6,8,128]{3,2,1,0:T(8,128)S(1)}, u32[]{:S(2)}, u32[]{:S(2)}) collective-permute-start(f32[3,6,8,128]{3,2,1,0:T(8,128)S(1)} %get-tuple-element.31), channel_id=1, source_target_pairs={{4,8},{8,4},{5,9},{9,5},{6,10},{10,6},{7,11},{11,7},{20,24},{24,20... | collective-permute-start | bytes 221192 | tf_op jit(solution)/shard_map/ppermute | solution.py:326
  16.8 0.0 copy-start.2
  16.8 11.3 %collective-permute-start.5 = (f32[3,6,8,128]{3,2,1,0:T(8,128)S(1)}, f32[3,6,8,128]{3,2,1,0:T(8,128)S(1)}, u32[]{:S(2)}, u32[]{:S(2)}) collective-permute-start(f32[3,6,8,128]{3,2,1,0:T(8,128)S(1)} %get-tuple-element.32), channel_id=1, source_target_pairs={{0,4},{4,0},{8,12},{12,8},{1,5},{5,1},{9,13},{13,9},{2,6},{6,2},{1... | collective-permute-start | bytes 221192 | tf_op jit(solution)/shard_map/ppermute | solution.py:326
  28.1 0.9 %shard_map.66.w_ref = bf16[6,3,2,128,384]{4,3,2,1,0:T(8,128)(2,1)S(1)} custom-call(f32[3,3,3,96,96]{4,3,2,1,0:T(8,128)S(1)} %copy-done.1), custom_call_target="tpu_custom_call" | custom-call | tf_op jit(solution)/shard_map/pallas_call | solution.py:339
  29.1 0.0 copy-start
  29.1 0.8 %shard_map.68.w2_ref = bf16[5,3,2,128,384]{4,3,2,1,0:T(8,128)(2,1)S(1)} custom-call(f32[3,3,3,96,96]{4,3,2,1,0:T(8,128)S(1)} %copy-done.2), custom_call_target="tpu_custom_call" | custom-call | tf_op jit(solution)/shard_map/pallas_call | solution.py:339
  29.9 0.5 %copy-done = f32[3,3,3,96,96]{4,3,2,1,0:T(8,128)S(1)} copy-done((f32[3,3,3,96,96]{4,3,2,1,0:T(8,128)S(1)}, f32[3,3,3,96,96]{4,3,2,1,0:T(8,128)}, u32[]{:S(2)}) %copy-start) | copy-done | bytes 995352
  30.4 0.6 %shard_map.69.w1_ref = bf16[4,3,2,128,384]{4,3,2,1,0:T(8,128)(2,1)S(1)} custom-call(f32[3,3,3,96,96]{4,3,2,1,0:T(8,128)S(1)} %copy-done), custom_call_target="tpu_custom_call" | custom-call | tf_op jit(solution)/shard_map/pallas_call | solution.py:339
  31.0 0.0 collective-permute-done.5.rc1
  31.1 0.0 collective-permute-done.3.ra1
  31.1 5.7 %shard_map.67.g_ref = f32[4,8,72,128]{3,2,1,0:T(8,128)S(1)} custom-call(s32[2]{0:T(128)S(1)} %pad_add_fusion.par_ref, f32[4,4,72,128]{3,2,1,0:T(8,128)S(1)} %get-tuple-element.28.cp_ref, f32[3,3,64,128]{3,2,1,0:T(8,128)S(1)} %collective-permute-done.2.ra0, f32[3,3,64,128]{3,2,1,0:T(8,128)S(1)} %collective-permute-done.3.ra1, ...), custom_call_target="tpu_custom_call" | custom-call | tf_op jit(solution)/shard_map/pallas_call | solution.py:339
  36.8 9.2 %shard_map.70 = f32[4,4,64,96]{3,2,1,0:T(8,128)} custom-call(s32[2]{0:T(128)S(1)} %pad_add_fusion.par_ref, f32[4,8,72,128]{3,2,1,0:T(8,128)S(1)} %shard_map.67.g_ref, f32[4,4,72,128]{3,2,1,0:T(8,128)S(1)} %get-tuple-element.33.s2_ref, f32[4,4,72,128]{3,2,1,0:T(8,128)S(1)} %get-tuple-element.34.s1_ref, f32[3,3,64,128]{3,2,1,0:T(8,128)S(1)} %collective-permute-done.6.rb0, ...), custom_call_target="tpu_custom_call" | custom-call | tf_op jit(solution)/shard_map/pallas_call | solution.py:339
  (6 shorter events, 0.0 us)
Async XLA Ops:
  2.6 25.5 %copy-start.1 = (f32[3,3,3,96,96]{4,3,2,1,0:T(8,128)S(1)}, f32[3,3,3,96,96]{4,3,2,1,0:T(8,128)}, u32[]{:S(2)}) copy-start(f32[3,3,3,96,96]{4,3,2,1,0:T(8,128)} %w_ref.3) | copy-start | bytes 2985988
  2.6 10.3 %collective-permute-start = (f32[4,4,8,128]{3,2,1,0:T(8,128)S(1)}, f32[4,4,8,128]{3,2,1,0:T(8,128)S(1)}, u32[]{:S(2)}, u32[]{:S(2)}) collective-permute-start(f32[4,4,8,128]{3,2,1,0:T(8,128)S(1)} %get-tuple-element.21), channel_id=1, source_target_pairs={{1,2},{2,1},{5,6},{6,5},{9,10},{10,9},{13,14},{14,13},{17,18},{18,... | collective-permute-start | bytes 196616 | tf_op jit(solution)/shard_map/ppermute | solution.py:326
  3.4 9.5 %collective-permute-start.1 = (f32[4,4,8,128]{3,2,1,0:T(8,128)S(1)}, f32[4,4,8,128]{3,2,1,0:T(8,128)S(1)}, u32[]{:S(2)}, u32[]{:S(2)}) collective-permute-start(f32[4,4,8,128]{3,2,1,0:T(8,128)S(1)} %get-tuple-element.22), channel_id=1, source_target_pairs={{0,1},{1,0},{2,3},{3,2},{4,5},{5,4},{6,7},{7,6},{8,9},{9,8},{10,11... | collective-permute-start | bytes 196616 | tf_op jit(solution)/shard_map/ppermute | solution.py:326
  7.8 23.2 %collective-permute-start.2 = (f32[3,3,64,128]{3,2,1,0:T(8,128)S(1)}, f32[3,3,64,128]{3,2,1,0:T(8,128)S(1)}, u32[]{:S(2)}, u32[]{:S(2)}) collective-permute-start(f32[3,3,64,128]{3,2,1,0:T(8,128)S(1)} %get-tuple-element.29), channel_id=1, source_target_pairs={{4,8},{8,4},{5,9},{9,5},{6,10},{10,6},{7,11},{11,7},{20,24},{24,20... | collective-permute-start | bytes 884744 | tf_op jit(solution)/shard_map/ppermute | solution.py:326
  8.5 22.6 %collective-permute-start.3 = (f32[3,3,64,128]{3,2,1,0:T(8,128)S(1)}, f32[3,3,64,128]{3,2,1,0:T(8,128)S(1)}, u32[]{:S(2)}, u32[]{:S(2)}) collective-permute-start(f32[3,3,64,128]{3,2,1,0:T(8,128)S(1)} %get-tuple-element.30), channel_id=1, source_target_pairs={{0,4},{4,0},{8,12},{12,8},{1,5},{5,1},{9,13},{13,9},{2,6},{6,2},{1... | collective-permute-start | bytes 884744 | tf_op jit(solution)/shard_map/ppermute | solution.py:326
  13.6 23.1 %collective-permute-start.6 = (f32[3,3,64,128]{3,2,1,0:T(8,128)S(1)}, f32[3,3,64,128]{3,2,1,0:T(8,128)S(1)}, u32[]{:S(2)}, u32[]{:S(2)}) collective-permute-start(f32[3,3,64,128]{3,2,1,0:T(8,128)S(1)} %get-tuple-element.35), channel_id=1, source_target_pairs={{4,8},{8,4},{5,9},{9,5},{6,10},{10,6},{7,11},{11,7},{20,24},{24,20... | collective-permute-start | bytes 884744 | tf_op jit(solution)/shard_map/ppermute | solution.py:326
  14.3 22.5 %collective-permute-start.7 = (f32[3,3,64,128]{3,2,1,0:T(8,128)S(1)}, f32[3,3,64,128]{3,2,1,0:T(8,128)S(1)}, u32[]{:S(2)}, u32[]{:S(2)}) collective-permute-start(f32[3,3,64,128]{3,2,1,0:T(8,128)S(1)} %get-tuple-element.36), channel_id=1, source_target_pairs={{0,4},{4,0},{8,12},{12,8},{1,5},{5,1},{9,13},{13,9},{2,6},{6,2},{1... | collective-permute-start | bytes 884744 | tf_op jit(solution)/shard_map/ppermute | solution.py:326
  16.1 0.7 %collective-permute-start.4 = (f32[3,6,8,128]{3,2,1,0:T(8,128)S(1)}, f32[3,6,8,128]{3,2,1,0:T(8,128)S(1)}, u32[]{:S(2)}, u32[]{:S(2)}) collective-permute-start(f32[3,6,8,128]{3,2,1,0:T(8,128)S(1)} %get-tuple-element.31), channel_id=1, source_target_pairs={{4,8},{8,4},{5,9},{9,5},{6,10},{10,6},{7,11},{11,7},{20,24},{24,20... | collective-permute-start | bytes 221192 | tf_op jit(solution)/shard_map/ppermute | solution.py:326
  16.8 12.3 %copy-start.2 = (f32[3,3,3,96,96]{4,3,2,1,0:T(8,128)S(1)}, f32[3,3,3,96,96]{4,3,2,1,0:T(8,128)}, u32[]{:S(2)}) copy-start(f32[3,3,3,96,96]{4,3,2,1,0:T(8,128)} %w_ref.4) | copy-start | bytes 2985988
  16.8 14.3 %collective-permute-start.5 = (f32[3,6,8,128]{3,2,1,0:T(8,128)S(1)}, f32[3,6,8,128]{3,2,1,0:T(8,128)S(1)}, u32[]{:S(2)}, u32[]{:S(2)}) collective-permute-start(f32[3,6,8,128]{3,2,1,0:T(8,128)S(1)} %get-tuple-element.32), channel_id=1, source_target_pairs={{0,4},{4,0},{8,12},{12,8},{1,5},{5,1},{9,13},{13,9},{2,6},{6,2},{1... | collective-permute-start | bytes 221192 | tf_op jit(solution)/shard_map/ppermute | solution.py:326
  29.1 1.3 %copy-start = (f32[3,3,3,96,96]{4,3,2,1,0:T(8,128)S(1)}, f32[3,3,3,96,96]{4,3,2,1,0:T(8,128)}, u32[]{:S(2)}) copy-start(f32[3,3,3,96,96]{4,3,2,1,0:T(8,128)} %w_ref.5) | copy-start | bytes 2985988

commit v5 on v4

--- a/solution.py
+++ b/solution.py
@@ -54,49 +54,48 @@
     return frames + [jnp.where(lane < chans, fourth, 0.0)]
 
 
-def pack_kernel(par_ref, cot_hbm, sec_hbm, fst_hbm, ma0, ma1, mb0, mb1, wp0, wp1, cp_ref, s2_ref, s1_ref, raw_ref, sems):
+def group_row(src, h, cols, chans):
+    return group_frames([src[t, h, 0:cols] for t in range(4)], chans)
+
+
+def pack_kernel(par_ref, cot_hbm, sec_hbm, fst_hbm, ma0, ma1, wp0, wp1, cp_ref, sec_ref, fst_ref, raw_ref, edge_ref, sems):
     frames, rows, cols, chans = cot_hbm.shape
-    copies = [pltpu.make_async_copy(src, raw_ref.at[a], sems.at[a]) for a, src in enumerate((cot_hbm, sec_hbm, fst_hbm))]
+    copies = [
+        pltpu.make_async_copy(src, dst, sems.at[a])
+        for a, (src, dst) in enumerate(((cot_hbm, raw_ref), (sec_hbm, sec_ref), (fst_hbm, fst_ref)))
+    ]
     for copy in copies:
         copy.start()
-    outs = (cp_ref, s2_ref, s1_ref)
-    for ref in outs:
-        ref[...] = jnp.zeros(ref.shape, F32)
-    for a, ref in enumerate(outs):
-        copies[a].wait()
-        for t in range(frames):
-            for h in range(rows):
-                value = raw_ref[a, t, h]
-                ref[t, h, 0:cols, 0:chans] = silu_slope(value) if a else value
-
-    def rows_out(top_a, top_b, low_a, low_b):
-        def put(src, h, dst, at):
-            for g, val in enumerate(group_frames([src[t, h, 0:cols] for t in range(frames)], chans)):
-                dst[g, at] = val
-
+    cp_ref[...] = jnp.zeros(cp_ref.shape, F32)
+    edge_ref[...] = jnp.zeros(edge_ref.shape, F32)
+    copies[0].wait()
+    cp_ref[:, :, 0:cols, 0:chans] = raw_ref[...]
+
+    def rows_out(top, low):
         for r in range(3):
-            put(cp_ref, r, top_a, r)
-            put(cp_ref, rows - 3 + r, low_a, r)
-        for r in range(2):
-            put(s2_ref, r, top_b, r)
-            put(s2_ref, rows - 2 + r, low_b, r)
-        put(s1_ref, 0, top_b, 2)
-        put(s1_ref, rows - 1, low_b, 2)
+            for dst, h in ((top, r), (low, rows - 3 + r)):
+                for g, val in enumerate(group_row(cp_ref, h, cols, chans)):
+                    dst[g, r] = val
 
     @pl.when(par_ref[0] == 0)
     def _():
-        rows_out(ma1, mb1, ma0, mb0)
+        rows_out(ma1, ma0)
 
     @pl.when(par_ref[0] != 0)
     def _():
-        rows_out(ma0, mb0, ma1, mb1)
+        rows_out(ma0, ma1)
+
+    for a, ref in ((0, sec_ref), (1, fst_ref)):
+        copies[1 + a].wait()
+        for side, start in enumerate((0, cols - SUB)):
+            edge_ref[a, side, :, :, :, 0:chans] = silu_slope(ref[:, :, start : start + SUB])
 
     def cols_out(left, right):
         sub = sub_of((SUB, LANES))
         for t in range(frames):
             for h in range(rows):
-                c0, a0, b0 = (ref[t, h, 0:SUB] for ref in outs)
-                c7, a7, b7 = (ref[t, h, cols - SUB : cols] for ref in outs)
+                c0, a0, b0 = cp_ref[t, h, 0:SUB], edge_ref[0, 0, t, h], edge_ref[1, 0, t, h]
+                c7, a7, b7 = cp_ref[t, h, cols - SUB : cols], edge_ref[0, 1, t, h], edge_ref[1, 1, t, h]
                 right[t, h] = jnp.where(
                     sub >= 5, c7, jnp.where((sub == 2) | (sub == 3), roll(a7, 4, 0), jnp.where(sub == 1, roll(b7, 2, 0), 0.0))
                 )
@@ -111,6 +110,36 @@
     @pl.when(par_ref[1] != 0)
     def _():
         cols_out(wp0, wp1)
+
+
+def slope_kernel(par_ref, sec_ref, fst_ref, mb0, mb1, s2_ref, s1_ref):
+    frames, rows, cols, chans = sec_ref.shape
+    blank = jnp.zeros((cols, LANES), F32)
+    for src, ref in ((sec_ref, s2_ref), (fst_ref, s1_ref)):
+        for t in range(frames):
+            for h in range(rows):
+                ref[t, h, 0:cols] = blank
+                ref[t, h, 0:cols, 0:chans] = silu_slope(src[t, h])
+
+    def rows_out(top, low):
+        for src, h, dst, at in (
+            (s2_ref, 0, top, 0),
+            (s2_ref, 1, top, 1),
+            (s1_ref, 0, top, 2),
+            (s2_ref, rows - 2, low, 0),
+            (s2_ref, rows - 1, low, 1),
+            (s1_ref, rows - 1, low, 2),
+        ):
+            for g, val in enumerate(group_row(src, h, cols, chans)):
+                dst[g, at] = val
+
+    @pl.when(par_ref[0] == 0)
+    def _():
+        rows_out(mb1, mb0)
+
+    @pl.when(par_ref[0] != 0)
+    def _():
+        rows_out(mb0, mb1)
 
 
 def corner_kernel(chans, par_ref, rw0, rw1, _c, _s2, _s1, _b0, _b1, mc0, mc1, cp_ref, s2_ref, s1_ref, _mb0, _mb1):
@@ -149,21 +178,36 @@
         out(mc0, mc1)
 
 
-def weight_kernel(wanted, w_ref, out_ref):
+def prepare(w_ref, out_ref, wanted, k, i):
     chans = w_ref.shape[3]
-    out_ref[...] = jnp.zeros(out_ref.shape, BF16)
+    f0, f1, f2 = (w_ref[i, 2 - m, k] for m in range(3))
+    even, odd = (f0 + f2) * (1 / 6), f1 * (1 / 6)
+    far, odd2 = f0 * (1 / 24) + f2 * (1 / 6), f1 * (1 / 12)
+    points = (f0 * 0.25, -even - odd, odd - even, far + odd2, far - odd2, f2)
+    lanes = pl.ds((2 - i) * LANES, chans)
+    for n, p in enumerate(wanted):
+        high = points[p].astype(BF16)
+        out_ref[n, k, 0, 0:chans, lanes] = high
+        out_ref[n, k, 1, 0:chans, lanes] = (points[p] - high.astype(F32)).astype(BF16)
+
+
+def prepare_all(w_ref, out_ref, wanted):
+    steps = []
+    for n in range(len(wanted)):
+        for k in range(3):
+            def clear(n=n, k=k):
+                out_ref[n, k] = jnp.zeros(out_ref.shape[2:], BF16)
+
+            steps.append(clear)
     for k in range(3):
         for i in range(3):
-            f0, f1, f2 = (w_ref[i, 2 - m, k] for m in range(3))
-            even, odd = (f0 + f2) * (1 / 6), f1 * (1 / 6)
-            far, odd2 = f0 * (1 / 24) + f2 * (1 / 6), f1 * (1 / 12)
-            points = (f0 * 0.25, -even - odd, odd - even, far + odd2, far - odd2, f2)
-            lanes = pl.ds((2 - i) * LANES, chans)
-            for n, p in enumerate(wanted):
-                u = points[p]
-                high = u.astype(BF16)
-                out_ref[n, k, 0, 0:chans, lanes] = high
-                out_ref[n, k, 1, 0:chans, lanes] = (u - high.astype(F32)).astype(BF16)
+            steps.append(functools.partial(prepare, w_ref, out_ref, wanted, k, i))
+    return steps
+
+
+def weight_kernel(wanted, w_ref, out_ref):
+    for step in prepare_all(w_ref, out_ref, wanted):
+        step()
 
 
 POINTS = {2: (0, 1, 2, 5), 3: (0, 1, 2, 3, 5), 4: (0, 1, 2, 3, 4, 5)}
@@ -222,7 +266,7 @@
     return roll(taps[:, :two], -1, 0) + taps[:, two : 2 * two] + roll(taps[:, 2 * two :], 1, 0)
 
 
-def conv(read, size, width, s_ref, y_ref, w_ref, emit, done=None):
+def conv(read, size, width, s_ref, y_ref, w_ref, emit, done=None, beside=()):
     chunks = width // SUB
     points = len(POINTS[size])
 
@@ -248,6 +292,8 @@
         for n in range(2):
             y_ref[0, p, n] = shifted_sum((own[:, 0, n] + later[:, n]).reshape(width, 6 * LANES))
             y_ref[1, p, n] = shifted_sum(own[:, 1, n].reshape(width, 6 * LANES))
+        for step in beside[p * len(beside) // points : (p + 1) * len(beside) // points]:
+            step()
 
     for t in range(4):
         lanes = pl.ds(t % 2 * LANES, LANES)
@@ -263,7 +309,7 @@
     return ungroup_frames([jnp.where(par == 0, from_even[g, r], from_odd[g, r]) for g in range(3)], chans)
 
 
-def third_kernel(chans, par_ref, cp_ref, ra0, ra1, rc0, rc1, w_ref, out_ref, x_ref, s_ref, y_ref):
+def third_kernel(chans, par_ref, cp_ref, ra0, ra1, rc0, rc1, w_ref, w2_ref, w1_ref, out_ref, u2_ref, u1_ref, x_ref, s_ref, y_ref):
     rows, width = cp_ref.shape[1:3]
     cols = width - SUB
     for r in range(3):
@@ -281,7 +327,8 @@
     def emit(t, o, value):
         out_ref[t, o] = value
 
-    conv(read, rows, width, s_ref, y_ref, w_ref, emit)
+    beside = prepare_all(w2_ref, u2_ref, POINTS[(rows + 2) // 2]) + prepare_all(w1_ref, u1_ref, POINTS[rows // 2])
+    conv(read, rows, width, s_ref, y_ref, w_ref, emit, beside=beside)
 
 
 def last_kernel(chans, par_ref, g_ref, s2_ref, s1_ref, rb0, rb1, rc0, rc1, w2_ref, w1_ref, out_hbm,
@@ -364,30 +411,31 @@
     message = arr(3, 3, cols, LANES)
     corner = arr(3, 6, SUB, LANES)
     fields = tuple(pltpu.with_memory_space_constraint(x, pltpu.HBM) for x in (cotangent, stored_second, stored_first))
-    ma0, ma1, mb0, mb1, wp0, wp1, *kept = call(
+    raw = arr(frames, rows, cols, chans)
+    ma0, ma1, wp0, wp1, cp, sec, fst = call(
         pack_kernel,
-        (message,) * 4 + (edge,) * 2 + (own,) * 3,
+        (message,) * 2 + (edge,) * 2 + (own, raw, raw),
         (par,) + fields,
-        [vmem(3, frames, rows, cols, chans), pltpu.SemaphoreType.DMA((3,))],
+        [vmem(frames, rows, cols, chans), vmem(2, 2, frames, rows, SUB, LANES), pltpu.SemaphoreType.DMA((3,))],
         hbm=True,
     )
     ra0, ra1 = swaps(ma0, ma1, "ha")
     rw0, rw1 = swaps(wp0, wp1, "wa")
+    mb0, mb1, s2, s1 = call(slope_kernel, (message,) * 2 + (own,) * 2, (par, sec, fst))
     mc0, mc1, cp, s2, s1, mb0, mb1 = call(
         functools.partial(corner_kernel, chans),
         (corner,) * 2 + (own,) * 3 + (message,) * 2,
-        (par, rw0, rw1, *kept, mb0, mb1),
+        (par, rw0, rw1, cp, s2, s1, mb0, mb1),
         alias={n + 3: n + 2 for n in range(5)},
     )
     rc0, rc1 = swaps(mc0, mc1, "ha")
     rb0, rb1 = swaps(mb0, mb1, "ha")
 
-    def prepare(w, size):
-        points = POINTS[size]
-        shape = arr(len(points), 3, 2, LANES, 3 * LANES, dtype=BF16)
-        return call(functools.partial(weight_kernel, points), shape, (w,))
-
-    u3, u2, u1 = prepare(w_third, rows), prepare(w_second, (rows + 2) // 2), prepare(w_first, rows // 2)
+    def weights(size):
+        return arr(len(POINTS[size]), 3, 2, LANES, 3 * LANES, dtype=BF16)
+
+    size3, size2, size1 = rows, (rows + 2) // 2, rows // 2
+    u3 = call(functools.partial(weight_kernel, POINTS[size3]), weights(size3), (w_third,))
 
     def scratch(size):
         points = len(POINTS[size])
@@ -396,18 +444,18 @@
             vmem(2, points, 2, width, 2 * LANES),
         ]
 
-    grad = call(
+    grad, u2, u1 = call(
         functools.partial(third_kernel, chans),
-        arr(frames, rows + 4, width, LANES),
-        (par, cp, ra0, ra1, rc0, rc1, u3),
-        [vmem(frames, 6, width, LANES)] + scratch(rows),
+        (arr(frames, rows + 4, width, LANES), weights(size2), weights(size1)),
+        (par, cp, ra0, ra1, rc0, rc1, u3, w_second, w_first),
+        [vmem(frames, 6, width, LANES)] + scratch(size3),
     )
     return call(
         functools.partial(last_kernel, chans),
         arr(frames, rows, cols, chans),
         (par, grad, s2, s1, rb0, rb1, rc0, rc1, u2, u1),
         [vmem(2, 3, frames, width, LANES), vmem(frames, rows + 2, width, LANES)]
-        + scratch((rows + 2) // 2)
+        + scratch(size2)
         + [vmem(frames, rows, cols, chans), pltpu.SemaphoreType.DMA((frames,))],
         hbm_out=True,
     )

time: 46.2 us -> 46 us (level)
  waiting for transfers between devices: 0.02 us -> 1.39 us
  starting transfers between devices: 24.7 us -> 23.4 us
  local copies, waits for them, and re-layouts: 0.52 us -> 0.02 us
    ppermute x8, waiting for transfers between devices: 0.02 us -> 1.39 us  [swap(): return lax.ppermute(value, axis, pairs)]
    ppermute x8, starting transfers between devices: 24.7 us -> 23.4 us  [swap(): return lax.ppermute(value, axis, pairs)]
    unnamed x6, local copies, waits for them, and re-layouts: 0.52 us -> 0.02 us
    pallas_call x7 -> x6, Pallas kernels: 20.5 us -> 20.7 us  [call(): pl.pallas_call(body, out_shape=out_shape, in_specs=[SMEM_SPEC if a.dtype...]
  transfers between devices with their start and end apart: 8 -> 8, of which waited for: 0 -> 1; matrix products, arithmetic and copies ran while one was open for 0% -> 0% of each run, Pallas kernels for 19% -> 21%
where the time goes in v5:
time: 46 us; the launch traced here: 45.8 us
  starting transfers between devices  23.4 us (51%)
  Pallas kernels  20.7 us (45%)
  waiting for transfers between devices  1.39 us (3%)
    ppermute x8, starting transfers between devices, swap(): return lax.ppermute(value, axis, pairs)  23.4 us
    pallas_call x6, Pallas kernels, call(): pl.pallas_call(body, out_shape=out_shape, in_specs=[SMEM_SPEC if a.dtype...  20.7 us
    ppermute x8, waiting for transfers between devices, swap(): return lax.ppermute(value, axis, pairs)  1.39 us
  transfers between devices with their start and end apart: 8, of which 1 were waited for; matrix products, arithmetic and copies ran while one was open for 0% of the time, Pallas kernels for 21%

profile of v5, /device:TPU:0, one launch (start us, length us, event | category | flops | bytes accessed | tf_op | source)
XLA Modules:
  0.0 45.8 jit_solution(4086437316420910275)
XLA Ops:
  0.0 0.1 pad_add_fusion.par_ref
  0.1 2.0 %shard_map.64 = (f32[3,3,64,128]{3,2,1,0:T(8,128)S(1)}, f32[3,3,64,128]{3,2,1,0:T(8,128)S(1)}, f32[4,4,8,128]{3,2,1,0:T(8,128)S(1)}, f32[4,4,8,128]{3,2,1,0:T(8,...) custom-call(s32[2]{0:T(128)S(1)} %pad_add_fusion.par_ref, ...), custom_call_target="tpu_custom_call" | custom-call | tf_op jit(solution)/shard_map/pallas_call | solution.py:386
  2.1 0.7 %collective-permute-start = (f32[4,4,8,128]{3,2,1,0:T(8,128)S(1)}, f32[4,4,8,128]{3,2,1,0:T(8,128)S(1)}, u32[]{:S(2)}, u32[]{:S(2)}) collective-permute-start(f32[4,4,8,128]{3,2,1,0:T(8,128)S(1)} %get-tuple-element.26), channel_id=1, source_target_pairs={{1,2},{2,1},{5,6},{6,5},{9,10},{10,9},{13,14},{14,13},{17,18},{18,... | collective-permute-start | bytes 196616 | tf_op jit(solution)/shard_map/ppermute | solution.py:373
  2.8 4.4 %collective-permute-start.1 = (f32[4,4,8,128]{3,2,1,0:T(8,128)S(1)}, f32[4,4,8,128]{3,2,1,0:T(8,128)S(1)}, u32[]{:S(2)}, u32[]{:S(2)}) collective-permute-start(f32[4,4,8,128]{3,2,1,0:T(8,128)S(1)} %get-tuple-element.27), channel_id=1, source_target_pairs={{0,1},{1,0},{2,3},{3,2},{4,5},{5,4},{6,7},{7,6},{8,9},{9,8},{10,11... | collective-permute-start | bytes 196616 | tf_op jit(solution)/shard_map/ppermute | solution.py:373
  7.2 0.7 %collective-permute-start.2 = (f32[3,3,64,128]{3,2,1,0:T(8,128)S(1)}, f32[3,3,64,128]{3,2,1,0:T(8,128)S(1)}, u32[]{:S(2)}, u32[]{:S(2)}) collective-permute-start(f32[3,3,64,128]{3,2,1,0:T(8,128)S(1)} %get-tuple-element.36), channel_id=1, source_target_pairs={{4,8},{8,4},{5,9},{9,5},{6,10},{10,6},{7,11},{11,7},{20,24},{24,20... | collective-permute-start | bytes 884744 | tf_op jit(solution)/shard_map/ppermute | solution.py:373
  7.8 4.4 %collective-permute-start.3 = (f32[3,3,64,128]{3,2,1,0:T(8,128)S(1)}, f32[3,3,64,128]{3,2,1,0:T(8,128)S(1)}, u32[]{:S(2)}, u32[]{:S(2)}) collective-permute-start(f32[3,3,64,128]{3,2,1,0:T(8,128)S(1)} %get-tuple-element.37), channel_id=1, source_target_pairs={{0,4},{4,0},{8,12},{12,8},{1,5},{5,1},{9,13},{13,9},{2,6},{6,2},{1... | collective-permute-start | bytes 884744 | tf_op jit(solution)/shard_map/ppermute | solution.py:373
  12.3 1.2 %shard_map.65 = (f32[3,3,64,128]{3,2,1,0:T(8,128)S(1)}, f32[3,3,64,128]{3,2,1,0:T(8,128)S(1)}, f32[4,4,72,128]{3,2,1,0:T(8,128)S(1)}, f32[4,4,72,128]{3,2,1,0:T(8,128)S(1)}) custom-call(s32[2]{0:T(128)S(1)} %pad_add_fusion.par_ref, f32[4,4,64,96]{3,2,1,0:T(8,128)S(1)} %get-tuple-element.29.sec_ref, f32[4,4,64,96]{3,2,1,0:T(8,128)S(1)} %get-tuple-element.30.fst_ref), custom_call_target="tpu_custom_call" | custom-call | tf_op jit(solution)/shard_map/pallas_call | solution.py:386
  13.4 0.0 copy-start
  13.5 0.0 collective-permute-done.rw0
  13.5 0.0 collective-permute-done.1.rw1
  13.5 0.7 %shard_map.66 = (f32[3,6,8,128]{3,2,1,0:T(8,128)S(1)}, f32[3,6,8,128]{3,2,1,0:T(8,128)S(1)}, f32[4,4,72,128]{3,2,1,0:T(8,128)S(1)}, f32[4,4,72,128]{3,2,1,0:T(8,...) custom-call(s32[2]{0:T(128)S(1)} %pad_add_fusion.par_ref, ...), custom_call_target="tpu_custom_call", output_to_operand_aliasing={{2}: (3, {}), {3}: (4, {}), {4}: (5, {}), {5}: (6, {}), {6}... | custom-call | tf_op jit(solution)/shard_map/pallas_call | solution.py:386
  14.2 0.7 %collective-permute-start.6 = (f32[3,3,64,128]{3,2,1,0:T(8,128)S(1)}, f32[3,3,64,128]{3,2,1,0:T(8,128)S(1)}, u32[]{:S(2)}, u32[]{:S(2)}) collective-permute-start(f32[3,3,64,128]{3,2,1,0:T(8,128)S(1)} %get-tuple-element.43), channel_id=1, source_target_pairs={{4,8},{8,4},{5,9},{9,5},{6,10},{10,6},{7,11},{11,7},{20,24},{24,20... | collective-permute-start | bytes 884744 | tf_op jit(solution)/shard_map/ppermute | solution.py:373
  14.9 1.8 %collective-permute-start.7 = (f32[3,3,64,128]{3,2,1,0:T(8,128)S(1)}, f32[3,3,64,128]{3,2,1,0:T(8,128)S(1)}, u32[]{:S(2)}, u32[]{:S(2)}) collective-permute-start(f32[3,3,64,128]{3,2,1,0:T(8,128)S(1)} %get-tuple-element.44), channel_id=1, source_target_pairs={{0,4},{4,0},{8,12},{12,8},{1,5},{5,1},{9,13},{13,9},{2,6},{6,2},{1... | collective-permute-start | bytes 884744 | tf_op jit(solution)/shard_map/ppermute | solution.py:373
  16.6 0.7 %collective-permute-start.4 = (f32[3,6,8,128]{3,2,1,0:T(8,128)S(1)}, f32[3,6,8,128]{3,2,1,0:T(8,128)S(1)}, u32[]{:S(2)}, u32[]{:S(2)}) collective-permute-start(f32[3,6,8,128]{3,2,1,0:T(8,128)S(1)} %get-tuple-element.38), channel_id=1, source_target_pairs={{4,8},{8,4},{5,9},{9,5},{6,10},{10,6},{7,11},{11,7},{20,24},{24,20... | collective-permute-start | bytes 221192 | tf_op jit(solution)/shard_map/ppermute | solution.py:373
  17.3 0.0 copy-start.1
  17.3 0.0 copy-start.2
  17.3 10.1 %collective-permute-start.5 = (f32[3,6,8,128]{3,2,1,0:T(8,128)S(1)}, f32[3,6,8,128]{3,2,1,0:T(8,128)S(1)}, u32[]{:S(2)}, u32[]{:S(2)}) collective-permute-start(f32[3,6,8,128]{3,2,1,0:T(8,128)S(1)} %get-tuple-element.39), channel_id=1, source_target_pairs={{0,4},{4,0},{8,12},{12,8},{1,5},{5,1},{9,13},{13,9},{2,6},{6,2},{1... | collective-permute-start | bytes 221192 | tf_op jit(solution)/shard_map/ppermute | solution.py:373
  27.5 0.9 %shard_map.67.w_ref = bf16[6,3,2,128,384]{4,3,2,1,0:T(8,128)(2,1)S(1)} custom-call(f32[3,3,3,96,96]{4,3,2,1,0:T(8,128)S(1)} %copy-done), custom_call_target="tpu_custom_call" | custom-call | tf_op jit(solution)/shard_map/pallas_call | solution.py:386
  28.4 1.4 %collective-permute-done.5.rc1 = f32[3,6,8,128]{3,2,1,0:T(8,128)S(1)} collective-permute-done((f32[3,6,8,128]{3,2,1,0:T(8,128)S(1)}, f32[3,6,8,128]{3,2,1,0:T(8,128)S(1)}, u32[]{:S(2)}, u32[]{:S(2)}) %collective-permute-start.5) | collective-permute-done | bytes 73760 | tf_op jit(solution)/shard_map/ppermute | solution.py:373
  29.8 0.0 collective-permute-done.2.ra0
  29.8 0.0 collective-permute-done.3.ra1
  29.8 6.7 %shard_map.68 = (f32[4,8,72,128]{3,2,1,0:T(8,128)S(1)}, bf16[5,3,2,128,384]{4,3,2,1,0:T(8,128)(2,1)S(1)}, bf16[4,3,2,128,384]{4,3,2,1,0:T(8,128)(2,1)S(1)}) custom-call(s32[2]{0:T(128)S(1)} %pad_add_fusion.par_ref, f32[4,4,72,128]{3,2,1,0:T(8,128)S(1)} %get-tuple-element.35.cp_ref, f32[3,3,64,128]{3,2,1,0:T(8,128)S(1)} %collective-permute-done.2.ra0, ...), custom_call_target="tpu_custom_call" | custom-call | tf_op jit(solution)/shard_map/pallas_call | solution.py:386
  36.6 0.0 collective-permute-done.6.rb0
  36.6 9.2 %shard_map.69 = f32[4,4,64,96]{3,2,1,0:T(8,128)} custom-call(s32[2]{0:T(128)S(1)} %pad_add_fusion.par_ref, f32[4,8,72,128]{3,2,1,0:T(8,128)S(1)} %get-tuple-element.40.g_ref, f32[4,4,72,128]{3,2,1,0:T(8,128)S(1)} %get-tuple-element.41.s2_ref, f32[4,4,72,128]{3,2,1,0:T(8,128)S(1)} %get-tuple-element.42.s1_ref, ...), custom_call_target="tpu_custom_call" | custom-call | tf_op jit(solution)/shard_map/pallas_call | solution.py:386
  (5 shorter events, 0.0 us)
Async XLA Ops:
  2.1 11.4 %collective-permute-start = (f32[4,4,8,128]{3,2,1,0:T(8,128)S(1)}, f32[4,4,8,128]{3,2,1,0:T(8,128)S(1)}, u32[]{:S(2)}, u32[]{:S(2)}) collective-permute-start(f32[4,4,8,128]{3,2,1,0:T(8,128)S(1)} %get-tuple-element.26), channel_id=1, source_target_pairs={{1,2},{2,1},{5,6},{6,5},{9,10},{10,9},{13,14},{14,13},{17,18},{18,... | collective-permute-start | bytes 196616 | tf_op jit(solution)/shard_map/ppermute | solution.py:373
  2.8 10.7 %collective-permute-start.1 = (f32[4,4,8,128]{3,2,1,0:T(8,128)S(1)}, f32[4,4,8,128]{3,2,1,0:T(8,128)S(1)}, u32[]{:S(2)}, u32[]{:S(2)}) collective-permute-start(f32[4,4,8,128]{3,2,1,0:T(8,128)S(1)} %get-tuple-element.27), channel_id=1, source_target_pairs={{0,1},{1,0},{2,3},{3,2},{4,5},{5,4},{6,7},{7,6},{8,9},{9,8},{10,11... | collective-permute-start | bytes 196616 | tf_op jit(solution)/shard_map/ppermute | solution.py:373
  7.2 22.6 %collective-permute-start.2 = (f32[3,3,64,128]{3,2,1,0:T(8,128)S(1)}, f32[3,3,64,128]{3,2,1,0:T(8,128)S(1)}, u32[]{:S(2)}, u32[]{:S(2)}) collective-permute-start(f32[3,3,64,128]{3,2,1,0:T(8,128)S(1)} %get-tuple-element.36), channel_id=1, source_target_pairs={{4,8},{8,4},{5,9},{9,5},{6,10},{10,6},{7,11},{11,7},{20,24},{24,20... | collective-permute-start | bytes 884744 | tf_op jit(solution)/shard_map/ppermute | solution.py:373
  7.8 22.0 %collective-permute-start.3 = (f32[3,3,64,128]{3,2,1,0:T(8,128)S(1)}, f32[3,3,64,128]{3,2,1,0:T(8,128)S(1)}, u32[]{:S(2)}, u32[]{:S(2)}) collective-permute-start(f32[3,3,64,128]{3,2,1,0:T(8,128)S(1)} %get-tuple-element.37), channel_id=1, source_target_pairs={{0,4},{4,0},{8,12},{12,8},{1,5},{5,1},{9,13},{13,9},{2,6},{6,2},{1... | collective-permute-start | bytes 884744 | tf_op jit(solution)/shard_map/ppermute | solution.py:373
  13.4 14.0 %copy-start = (f32[3,3,3,96,96]{4,3,2,1,0:T(8,128)S(1)}, f32[3,3,3,96,96]{4,3,2,1,0:T(8,128)}, u32[]{:S(2)}) copy-start(f32[3,3,3,96,96]{4,3,2,1,0:T(8,128)} %w_ref.1) | copy-start | bytes 2985988
  14.2 22.4 %collective-permute-start.6 = (f32[3,3,64,128]{3,2,1,0:T(8,128)S(1)}, f32[3,3,64,128]{3,2,1,0:T(8,128)S(1)}, u32[]{:S(2)}, u32[]{:S(2)}) collective-permute-start(f32[3,3,64,128]{3,2,1,0:T(8,128)S(1)} %get-tuple-element.43), channel_id=1, source_target_pairs={{4,8},{8,4},{5,9},{9,5},{6,10},{10,6},{7,11},{11,7},{20,24},{24,20... | collective-permute-start | bytes 884744 | tf_op jit(solution)/shard_map/ppermute | solution.py:373
  14.9 21.7 %collective-permute-start.7 = (f32[3,3,64,128]{3,2,1,0:T(8,128)S(1)}, f32[3,3,64,128]{3,2,1,0:T(8,128)S(1)}, u32[]{:S(2)}, u32[]{:S(2)}) collective-permute-start(f32[3,3,64,128]{3,2,1,0:T(8,128)S(1)} %get-tuple-element.44), channel_id=1, source_target_pairs={{0,4},{4,0},{8,12},{12,8},{1,5},{5,1},{9,13},{13,9},{2,6},{6,2},{1... | collective-permute-start | bytes 884744 | tf_op jit(solution)/shard_map/ppermute | solution.py:373
  16.6 0.7 %collective-permute-start.4 = (f32[3,6,8,128]{3,2,1,0:T(8,128)S(1)}, f32[3,6,8,128]{3,2,1,0:T(8,128)S(1)}, u32[]{:S(2)}, u32[]{:S(2)}) collective-permute-start(f32[3,6,8,128]{3,2,1,0:T(8,128)S(1)} %get-tuple-element.38), channel_id=1, source_target_pairs={{4,8},{8,4},{5,9},{9,5},{6,10},{10,6},{7,11},{11,7},{20,24},{24,20... | collective-permute-start | bytes 221192 | tf_op jit(solution)/shard_map/ppermute | solution.py:373
  17.3 12.5 %copy-start.1 = (f32[3,3,3,96,96]{4,3,2,1,0:T(8,128)S(1)}, f32[3,3,3,96,96]{4,3,2,1,0:T(8,128)}, u32[]{:S(2)}) copy-start(f32[3,3,3,96,96]{4,3,2,1,0:T(8,128)} %w2_ref.1) | copy-start | bytes 2985988
  17.3 12.5 %copy-start.2 = (f32[3,3,3,96,96]{4,3,2,1,0:T(8,128)S(1)}, f32[3,3,3,96,96]{4,3,2,1,0:T(8,128)}, u32[]{:S(2)}) copy-start(f32[3,3,3,96,96]{4,3,2,1,0:T(8,128)} %w1_ref.1) | copy-start | bytes 2985988
  17.3 12.5 %collective-permute-start.5 = (f32[3,6,8,128]{3,2,1,0:T(8,128)S(1)}, f32[3,6,8,128]{3,2,1,0:T(8,128)S(1)}, u32[]{:S(2)}, u32[]{:S(2)}) collective-permute-start(f32[3,6,8,128]{3,2,1,0:T(8,128)S(1)} %get-tuple-element.39), channel_id=1, source_target_pairs={{0,4},{4,0},{8,12},{12,8},{1,5},{5,1},{9,13},{13,9},{2,6},{6,2},{1... | collective-permute-start | bytes 221192 | tf_op jit(solution)/shard_map/ppermute | solution.py:373

commit v6 on v5

--- a/solution.py
+++ b/solution.py
@@ -178,30 +178,38 @@
         out(mc0, mc1)
 
 
-def prepare(w_ref, out_ref, wanted, k, i):
+def prepare(w_ref, out_ref, wanted, k, i, which):
     chans = w_ref.shape[3]
-    f0, f1, f2 = (w_ref[i, 2 - m, k] for m in range(3))
-    even, odd = (f0 + f2) * (1 / 6), f1 * (1 / 6)
-    far, odd2 = f0 * (1 / 24) + f2 * (1 / 6), f1 * (1 / 12)
-    points = (f0 * 0.25, -even - odd, odd - even, far + odd2, far - odd2, f2)
-    lanes = pl.ds((2 - i) * LANES, chans)
-    for n, p in enumerate(wanted):
-        high = points[p].astype(BF16)
+    blank = jnp.zeros((chans, LANES - chans), F32)
+    f0, f1, f2 = (jnp.concatenate([w_ref[i, 2 - m, k], blank], 1) for m in range(3))
+    points = {
+        0: lambda: f0 * 0.25,
+        1: lambda: (f0 + f1 + f2) * (-1 / 6),
+        2: lambda: (f1 - f0 - f2) * (1 / 6),
+        3: lambda: f0 * (1 / 24) + f1 * (1 / 12) + f2 * (1 / 6),
+        4: lambda: f0 * (1 / 24) - f1 * (1 / 12) + f2 * (1 / 6),
+        5: lambda: f2,
+    }
+    lanes = pl.ds((2 - i) * LANES, LANES)
+    for n in which:
+        value = points[wanted[n]]()
+        high = value.astype(BF16)
         out_ref[n, k, 0, 0:chans, lanes] = high
-        out_ref[n, k, 1, 0:chans, lanes] = (points[p] - high.astype(F32)).astype(BF16)
+        out_ref[n, k, 1, 0:chans, lanes] = (value - high.astype(F32)).astype(BF16)
 
 
 def prepare_all(w_ref, out_ref, wanted):
+    chans = w_ref.shape[3]
+
+    def clear(n, k):
+        out_ref[n, k, :, chans:] = jnp.zeros((2, LANES - chans, 3 * LANES), BF16)
+
     steps = []
-    for n in range(len(wanted)):
-        for k in range(3):
-            def clear(n=n, k=k):
-                out_ref[n, k] = jnp.zeros(out_ref.shape[2:], BF16)
-
-            steps.append(clear)
     for k in range(3):
-        for i in range(3):
-            steps.append(functools.partial(prepare, w_ref, out_ref, wanted, k, i))
+        for n in range(len(wanted)):
+            steps.append(functools.partial(clear, n, k))
+            for i in range(3):
+                steps.append(functools.partial(prepare, w_ref, out_ref, wanted, k, i, (n,)))
     return steps
 
 
@@ -285,15 +293,21 @@
     lax.fori_loop(0, chunks, one, 0)
 
     wide = 4 * LANES
+    gap = 2 * points
+
+    def other_work(n):
+        for step in beside[n * len(beside) // gap : (n + 1) * len(beside) // gap]:
+            step()
+
     for p in range(points):
         near, far = right_operands(w_ref, p)
         own = product(s_ref[p].reshape(chunks * 4 * SUB, wide), near).reshape(chunks, 2, 2, SUB, 6 * LANES)
+        other_work(2 * p)
         later = product(s_ref[p, :, 1].reshape(chunks * 2 * SUB, wide), far).reshape(chunks, 2, SUB, 6 * LANES)
+        other_work(2 * p + 1)
         for n in range(2):
             y_ref[0, p, n] = shifted_sum((own[:, 0, n] + later[:, n]).reshape(width, 6 * LANES))
             y_ref[1, p, n] = shifted_sum(own[:, 1, n].reshape(width, 6 * LANES))
-        for step in beside[p * len(beside) // points : (p + 1) * len(beside) // points]:
-            step()
 
     for t in range(4):
         lanes = pl.ds(t % 2 * LANES, LANES)

time: 46 us -> 45.4 us (0.987)
  Pallas kernels: 20.7 us -> 20.1 us
    pallas_call x6, Pallas kernels: 20.7 us -> 20.1 us  [call(): pl.pallas_call(body, out_shape=out_shape, in_specs=[SMEM_SPEC if a.dtype...]
  transfers between devices with their start and end apart: 8 -> 8, of which waited for: 1 -> 1; matrix products, arithmetic and copies ran while one was open for 0% -> 0% of each run, Pallas kernels for 21% -> 20%
where the time goes in v6:
time: 45.4 us; the launch traced here: 45.2 us
  starting transfers between devices  23.4 us (52%)
  Pallas kernels  20.1 us (44%)
  waiting for transfers between devices  1.45 us (3%)
    ppermute x8, starting transfers between devices, swap(): return lax.ppermute(value, axis, pairs)  23.4 us
    pallas_call x6, Pallas kernels, call(): pl.pallas_call(body, out_shape=out_shape, in_specs=[SMEM_SPEC if a.dtype...  20.1 us
    ppermute x8, waiting for transfers between devices, swap(): return lax.ppermute(value, axis, pairs)  1.45 us
  transfers between devices with their start and end apart: 8, of which 1 were waited for; matrix products, arithmetic and copies ran while one was open for 0% of the time, Pallas kernels for 20%

profile of v6, /device:TPU:0, one launch (start us, length us, event | category | flops | bytes accessed | tf_op | source)
XLA Modules:
  0.0 45.2 jit_solution(17276357577577063001)
XLA Ops:
  0.0 0.1 pad_add_fusion.par_ref
  0.1 2.0 %shard_map.64 = (f32[3,3,64,128]{3,2,1,0:T(8,128)S(1)}, f32[3,3,64,128]{3,2,1,0:T(8,128)S(1)}, f32[4,4,8,128]{3,2,1,0:T(8,128)S(1)}, f32[4,4,8,128]{3,2,1,0:T(8,...) custom-call(s32[2]{0:T(128)S(1)} %pad_add_fusion.par_ref, ...), custom_call_target="tpu_custom_call" | custom-call | tf_op jit(solution)/shard_map/pallas_call | solution.py:400
  2.1 0.7 %collective-permute-start = (f32[4,4,8,128]{3,2,1,0:T(8,128)S(1)}, f32[4,4,8,128]{3,2,1,0:T(8,128)S(1)}, u32[]{:S(2)}, u32[]{:S(2)}) collective-permute-start(f32[4,4,8,128]{3,2,1,0:T(8,128)S(1)} %get-tuple-element.26), channel_id=1, source_target_pairs={{1,2},{2,1},{5,6},{6,5},{9,10},{10,9},{13,14},{14,13},{17,18},{18,... | collective-permute-start | bytes 196616 | tf_op jit(solution)/shard_map/ppermute | solution.py:387
  2.8 4.4 %collective-permute-start.1 = (f32[4,4,8,128]{3,2,1,0:T(8,128)S(1)}, f32[4,4,8,128]{3,2,1,0:T(8,128)S(1)}, u32[]{:S(2)}, u32[]{:S(2)}) collective-permute-start(f32[4,4,8,128]{3,2,1,0:T(8,128)S(1)} %get-tuple-element.27), channel_id=1, source_target_pairs={{0,1},{1,0},{2,3},{3,2},{4,5},{5,4},{6,7},{7,6},{8,9},{9,8},{10,11... | collective-permute-start | bytes 196616 | tf_op jit(solution)/shard_map/ppermute | solution.py:387
  7.2 0.7 %collective-permute-start.2 = (f32[3,3,64,128]{3,2,1,0:T(8,128)S(1)}, f32[3,3,64,128]{3,2,1,0:T(8,128)S(1)}, u32[]{:S(2)}, u32[]{:S(2)}) collective-permute-start(f32[3,3,64,128]{3,2,1,0:T(8,128)S(1)} %get-tuple-element.36), channel_id=1, source_target_pairs={{4,8},{8,4},{5,9},{9,5},{6,10},{10,6},{7,11},{11,7},{20,24},{24,20... | collective-permute-start | bytes 884744 | tf_op jit(solution)/shard_map/ppermute | solution.py:387
  7.8 4.4 %collective-permute-start.3 = (f32[3,3,64,128]{3,2,1,0:T(8,128)S(1)}, f32[3,3,64,128]{3,2,1,0:T(8,128)S(1)}, u32[]{:S(2)}, u32[]{:S(2)}) collective-permute-start(f32[3,3,64,128]{3,2,1,0:T(8,128)S(1)} %get-tuple-element.37), channel_id=1, source_target_pairs={{0,4},{4,0},{8,12},{12,8},{1,5},{5,1},{9,13},{13,9},{2,6},{6,2},{1... | collective-permute-start | bytes 884744 | tf_op jit(solution)/shard_map/ppermute | solution.py:387
  12.3 1.2 %shard_map.65 = (f32[3,3,64,128]{3,2,1,0:T(8,128)S(1)}, f32[3,3,64,128]{3,2,1,0:T(8,128)S(1)}, f32[4,4,72,128]{3,2,1,0:T(8,128)S(1)}, f32[4,4,72,128]{3,2,1,0:T(8,128)S(1)}) custom-call(s32[2]{0:T(128)S(1)} %pad_add_fusion.par_ref, f32[4,4,64,96]{3,2,1,0:T(8,128)S(1)} %get-tuple-element.29.sec_ref, f32[4,4,64,96]{3,2,1,0:T(8,128)S(1)} %get-tuple-element.30.fst_ref), custom_call_target="tpu_custom_call" | custom-call | tf_op jit(solution)/shard_map/pallas_call | solution.py:400
  13.4 0.0 copy-start
  13.5 0.0 collective-permute-done.rw0
  13.5 0.0 collective-permute-done.1.rw1
  13.5 0.7 %shard_map.66 = (f32[3,6,8,128]{3,2,1,0:T(8,128)S(1)}, f32[3,6,8,128]{3,2,1,0:T(8,128)S(1)}, f32[4,4,72,128]{3,2,1,0:T(8,128)S(1)}, f32[4,4,72,128]{3,2,1,0:T(8,...) custom-call(s32[2]{0:T(128)S(1)} %pad_add_fusion.par_ref, ...), custom_call_target="tpu_custom_call", output_to_operand_aliasing={{2}: (3, {}), {3}: (4, {}), {4}: (5, {}), {5}: (6, {}), {6}... | custom-call | tf_op jit(solution)/shard_map/pallas_call | solution.py:400
  14.2 0.7 %collective-permute-start.6 = (f32[3,3,64,128]{3,2,1,0:T(8,128)S(1)}, f32[3,3,64,128]{3,2,1,0:T(8,128)S(1)}, u32[]{:S(2)}, u32[]{:S(2)}) collective-permute-start(f32[3,3,64,128]{3,2,1,0:T(8,128)S(1)} %get-tuple-element.43), channel_id=1, source_target_pairs={{4,8},{8,4},{5,9},{9,5},{6,10},{10,6},{7,11},{11,7},{20,24},{24,20... | collective-permute-start | bytes 884744 | tf_op jit(solution)/shard_map/ppermute | solution.py:387
  14.9 1.8 %collective-permute-start.7 = (f32[3,3,64,128]{3,2,1,0:T(8,128)S(1)}, f32[3,3,64,128]{3,2,1,0:T(8,128)S(1)}, u32[]{:S(2)}, u32[]{:S(2)}) collective-permute-start(f32[3,3,64,128]{3,2,1,0:T(8,128)S(1)} %get-tuple-element.44), channel_id=1, source_target_pairs={{0,4},{4,0},{8,12},{12,8},{1,5},{5,1},{9,13},{13,9},{2,6},{6,2},{1... | collective-permute-start | bytes 884744 | tf_op jit(solution)/shard_map/ppermute | solution.py:387
  16.6 0.7 %collective-permute-start.4 = (f32[3,6,8,128]{3,2,1,0:T(8,128)S(1)}, f32[3,6,8,128]{3,2,1,0:T(8,128)S(1)}, u32[]{:S(2)}, u32[]{:S(2)}) collective-permute-start(f32[3,6,8,128]{3,2,1,0:T(8,128)S(1)} %get-tuple-element.38), channel_id=1, source_target_pairs={{4,8},{8,4},{5,9},{9,5},{6,10},{10,6},{7,11},{11,7},{20,24},{24,20... | collective-permute-start | bytes 221192 | tf_op jit(solution)/shard_map/ppermute | solution.py:387
  17.3 0.0 copy-start.1
  17.3 0.0 copy-start.2
  17.3 10.1 %collective-permute-start.5 = (f32[3,6,8,128]{3,2,1,0:T(8,128)S(1)}, f32[3,6,8,128]{3,2,1,0:T(8,128)S(1)}, u32[]{:S(2)}, u32[]{:S(2)}) collective-permute-start(f32[3,6,8,128]{3,2,1,0:T(8,128)S(1)} %get-tuple-element.39), channel_id=1, source_target_pairs={{0,4},{4,0},{8,12},{12,8},{1,5},{5,1},{9,13},{13,9},{2,6},{6,2},{1... | collective-permute-start | bytes 221192 | tf_op jit(solution)/shard_map/ppermute | solution.py:387
  27.5 0.9 %shard_map.67.w_ref = bf16[6,3,2,128,384]{4,3,2,1,0:T(8,128)(2,1)S(1)} custom-call(f32[3,3,3,96,96]{4,3,2,1,0:T(8,128)S(1)} %copy-done), custom_call_target="tpu_custom_call" | custom-call | tf_op jit(solution)/shard_map/pallas_call | solution.py:400
  28.4 1.4 %collective-permute-done.5.rc1 = f32[3,6,8,128]{3,2,1,0:T(8,128)S(1)} collective-permute-done((f32[3,6,8,128]{3,2,1,0:T(8,128)S(1)}, f32[3,6,8,128]{3,2,1,0:T(8,128)S(1)}, u32[]{:S(2)}, u32[]{:S(2)}) %collective-permute-start.5) | collective-permute-done | bytes 73760 | tf_op jit(solution)/shard_map/ppermute | solution.py:387
  29.8 0.0 collective-permute-done.2.ra0
  29.8 0.0 collective-permute-done.3.ra1
  29.8 6.2 %shard_map.68 = (f32[4,8,72,128]{3,2,1,0:T(8,128)S(1)}, bf16[5,3,2,128,384]{4,3,2,1,0:T(8,128)(2,1)S(1)}, bf16[4,3,2,128,384]{4,3,2,1,0:T(8,128)(2,1)S(1)}) custom-call(s32[2]{0:T(128)S(1)} %pad_add_fusion.par_ref, f32[4,4,72,128]{3,2,1,0:T(8,128)S(1)} %get-tuple-element.35.cp_ref, f32[3,3,64,128]{3,2,1,0:T(8,128)S(1)} %collective-permute-done.2.ra0, ...), custom_call_target="tpu_custom_call" | custom-call | tf_op jit(solution)/shard_map/pallas_call | solution.py:400
  36.0 0.0 collective-permute-done.6.rb0
  36.0 9.2 %shard_map.69 = f32[4,4,64,96]{3,2,1,0:T(8,128)} custom-call(s32[2]{0:T(128)S(1)} %pad_add_fusion.par_ref, f32[4,8,72,128]{3,2,1,0:T(8,128)S(1)} %get-tuple-element.40.g_ref, f32[4,4,72,128]{3,2,1,0:T(8,128)S(1)} %get-tuple-element.41.s2_ref, f32[4,4,72,128]{3,2,1,0:T(8,128)S(1)} %get-tuple-element.42.s1_ref, ...), custom_call_target="tpu_custom_call" | custom-call | tf_op jit(solution)/shard_map/pallas_call | solution.py:400
  (5 shorter events, 0.0 us)
Async XLA Ops:
  2.1 11.4 %collective-permute-start = (f32[4,4,8,128]{3,2,1,0:T(8,128)S(1)}, f32[4,4,8,128]{3,2,1,0:T(8,128)S(1)}, u32[]{:S(2)}, u32[]{:S(2)}) collective-permute-start(f32[4,4,8,128]{3,2,1,0:T(8,128)S(1)} %get-tuple-element.26), channel_id=1, source_target_pairs={{1,2},{2,1},{5,6},{6,5},{9,10},{10,9},{13,14},{14,13},{17,18},{18,... | collective-permute-start | bytes 196616 | tf_op jit(solution)/shard_map/ppermute | solution.py:387
  2.8 10.7 %collective-permute-start.1 = (f32[4,4,8,128]{3,2,1,0:T(8,128)S(1)}, f32[4,4,8,128]{3,2,1,0:T(8,128)S(1)}, u32[]{:S(2)}, u32[]{:S(2)}) collective-permute-start(f32[4,4,8,128]{3,2,1,0:T(8,128)S(1)} %get-tuple-element.27), channel_id=1, source_target_pairs={{0,1},{1,0},{2,3},{3,2},{4,5},{5,4},{6,7},{7,6},{8,9},{9,8},{10,11... | collective-permute-start | bytes 196616 | tf_op jit(solution)/shard_map/ppermute | solution.py:387
  7.2 22.6 %collective-permute-start.2 = (f32[3,3,64,128]{3,2,1,0:T(8,128)S(1)}, f32[3,3,64,128]{3,2,1,0:T(8,128)S(1)}, u32[]{:S(2)}, u32[]{:S(2)}) collective-permute-start(f32[3,3,64,128]{3,2,1,0:T(8,128)S(1)} %get-tuple-element.36), channel_id=1, source_target_pairs={{4,8},{8,4},{5,9},{9,5},{6,10},{10,6},{7,11},{11,7},{20,24},{24,20... | collective-permute-start | bytes 884744 | tf_op jit(solution)/shard_map/ppermute | solution.py:387
  7.8 22.0 %collective-permute-start.3 = (f32[3,3,64,128]{3,2,1,0:T(8,128)S(1)}, f32[3,3,64,128]{3,2,1,0:T(8,128)S(1)}, u32[]{:S(2)}, u32[]{:S(2)}) collective-permute-start(f32[3,3,64,128]{3,2,1,0:T(8,128)S(1)} %get-tuple-element.37), channel_id=1, source_target_pairs={{0,4},{4,0},{8,12},{12,8},{1,5},{5,1},{9,13},{13,9},{2,6},{6,2},{1... | collective-permute-start | bytes 884744 | tf_op jit(solution)/shard_map/ppermute | solution.py:387
  13.4 14.0 %copy-start = (f32[3,3,3,96,96]{4,3,2,1,0:T(8,128)S(1)}, f32[3,3,3,96,96]{4,3,2,1,0:T(8,128)}, u32[]{:S(2)}) copy-start(f32[3,3,3,96,96]{4,3,2,1,0:T(8,128)} %w_ref.1) | copy-start | bytes 2985988
  14.2 21.9 %collective-permute-start.6 = (f32[3,3,64,128]{3,2,1,0:T(8,128)S(1)}, f32[3,3,64,128]{3,2,1,0:T(8,128)S(1)}, u32[]{:S(2)}, u32[]{:S(2)}) collective-permute-start(f32[3,3,64,128]{3,2,1,0:T(8,128)S(1)} %get-tuple-element.43), channel_id=1, source_target_pairs={{4,8},{8,4},{5,9},{9,5},{6,10},{10,6},{7,11},{11,7},{20,24},{24,20... | collective-permute-start | bytes 884744 | tf_op jit(solution)/shard_map/ppermute | solution.py:387
  14.9 21.2 %collective-permute-start.7 = (f32[3,3,64,128]{3,2,1,0:T(8,128)S(1)}, f32[3,3,64,128]{3,2,1,0:T(8,128)S(1)}, u32[]{:S(2)}, u32[]{:S(2)}) collective-permute-start(f32[3,3,64,128]{3,2,1,0:T(8,128)S(1)} %get-tuple-element.44), channel_id=1, source_target_pairs={{0,4},{4,0},{8,12},{12,8},{1,5},{5,1},{9,13},{13,9},{2,6},{6,2},{1... | collective-permute-start | bytes 884744 | tf_op jit(solution)/shard_map/ppermute | solution.py:387
  16.6 0.7 %collective-permute-start.4 = (f32[3,6,8,128]{3,2,1,0:T(8,128)S(1)}, f32[3,6,8,128]{3,2,1,0:T(8,128)S(1)}, u32[]{:S(2)}, u32[]{:S(2)}) collective-permute-start(f32[3,6,8,128]{3,2,1,0:T(8,128)S(1)} %get-tuple-element.38), channel_id=1, source_target_pairs={{4,8},{8,4},{5,9},{9,5},{6,10},{10,6},{7,11},{11,7},{20,24},{24,20... | collective-permute-start | bytes 221192 | tf_op jit(solution)/shard_map/ppermute | solution.py:387
  17.3 12.5 %copy-start.1 = (f32[3,3,3,96,96]{4,3,2,1,0:T(8,128)S(1)}, f32[3,3,3,96,96]{4,3,2,1,0:T(8,128)}, u32[]{:S(2)}) copy-start(f32[3,3,3,96,96]{4,3,2,1,0:T(8,128)} %w2_ref.1) | copy-start | bytes 2985988
  17.3 12.5 %copy-start.2 = (f32[3,3,3,96,96]{4,3,2,1,0:T(8,128)S(1)}, f32[3,3,3,96,96]{4,3,2,1,0:T(8,128)}, u32[]{:S(2)}) copy-start(f32[3,3,3,96,96]{4,3,2,1,0:T(8,128)} %w1_ref.1) | copy-start | bytes 2985988
  17.3 12.5 %collective-permute-start.5 = (f32[3,6,8,128]{3,2,1,0:T(8,128)S(1)}, f32[3,6,8,128]{3,2,1,0:T(8,128)S(1)}, u32[]{:S(2)}, u32[]{:S(2)}) collective-permute-start(f32[3,6,8,128]{3,2,1,0:T(8,128)S(1)} %get-tuple-element.39), channel_id=1, source_target_pairs={{0,4},{4,0},{8,12},{12,8},{1,5},{5,1},{9,13},{13,9},{2,6},{6,2},{1... | collective-permute-start | bytes 221192 | tf_op jit(solution)/shard_map/ppermute | solution.py:387

commit v7 on v6

--- a/solution.py
+++ b/solution.py
@@ -218,6 +218,7 @@
         step()
 
 
+SLOTS = (0, 2, 1, 3)
 POINTS = {2: (0, 1, 2, 5), 3: (0, 1, 2, 3, 5), 4: (0, 1, 2, 3, 4, 5)}
 
 
@@ -250,28 +251,30 @@
 
 def right_operands(w_ref, p):
     zero = jnp.zeros((LANES, LANES), BF16)
-    near, far = [], []
-    for k in range(3):
-        parts = [w_ref[p, k, part] for part in range(2)]
-        own = [
-            jnp.concatenate([r[:, : 2 * LANES], jnp.concatenate([zero, r[:, :LANES]], 1)], 0) for r in parts
-        ]
-        later = [
-            jnp.concatenate([jnp.concatenate([r[:, 2 * LANES :], zero], 1), r[:, LANES:]], 0) for r in parts
-        ]
-        near.append(jnp.concatenate([own[0], own[0], own[1]], 1))
-        far.append(jnp.concatenate([later[0], later[0], later[1]], 1))
-    return jnp.concatenate(near, 0), jnp.concatenate(far, 0)
+    taps = [[w_ref[p, k, part] for k in range(3)] for part in range(2)]
+
+    def alone(at):
+        lanes = slice(at * LANES, (at + 1) * LANES)
+        high = [jnp.concatenate([r[:, lanes], r[:, lanes]], 1) for r in taps[0]]
+        return high + [jnp.concatenate([r[:, lanes], zero], 1) for r in taps[1]]
+
+    both = []
+    for lanes in (slice(LANES, 3 * LANES), slice(0, 2 * LANES)):
+        for high, low in zip(*taps):
+            both.append(jnp.concatenate([high[:, lanes], high[:, lanes], low[:, lanes]], 1))
+    return (
+        jnp.concatenate(alone(0), 0),
+        jnp.concatenate(alone(2) + alone(1) + alone(0), 0),
+        jnp.concatenate(both, 0),
+    )
 
 
 def product(left, right):
-    left = jnp.concatenate([left, left[:, : 2 * LANES]], 1)
     return lax.dot_general(left, right, (((1,), (1,)), ((), ())), preferred_element_type=F32)
 
 
 def shifted_sum(taps):
-    two = 2 * LANES
-    return roll(taps[:, :two], -1, 0) + taps[:, two : 2 * two] + roll(taps[:, 2 * two :], 1, 0)
+    return roll(taps[:, :LANES], -1, 0) + taps[:, LANES : 2 * LANES] + roll(taps[:, 2 * LANES :], 1, 0)
 
 
 def conv(read, size, width, s_ref, y_ref, w_ref, emit, done=None, beside=()):
@@ -281,38 +284,55 @@
     def one(c, carry):
         at = pl.ds(pl.multiple_of(c * SUB, SUB), SUB)
         for t in range(4):
-            pair, a = t // 2, t % 2
             x = [read(t, r, at) for r in range(2 * size + 2)]
             for p, pieces in enumerate(zip(transform(x[: size + 2], size), transform(x[size:], size))):
                 value = jnp.concatenate(pieces, 0)
                 high = value.astype(BF16)
-                s_ref[p, c, pair, :, a * LANES : (a + 1) * LANES] = high
-                s_ref[p, c, pair, :, (2 + a) * LANES : (3 + a) * LANES] = (value - high.astype(F32)).astype(BF16)
+                s_ref[p, c, SLOTS[t], :, 0:LANES] = high
+                s_ref[p, c, SLOTS[t], :, LANES:] = (value - high.astype(F32)).astype(BF16)
         return carry
 
     lax.fori_loop(0, chunks, one, 0)
 
-    wide = 4 * LANES
-    gap = 2 * points
+    gap = 3 * points
+    part = 3 * LANES
 
     def other_work(n):
         for step in beside[n * len(beside) // gap : (n + 1) * len(beside) // gap]:
             step()
 
+    def rows_of(out):
+        return out.reshape(chunks, -1, 2, SUB, out.shape[1])
+
+    def whole(out, at):
+        return out[..., 2 * at * part : (2 * at + 1) * part] + out[..., (2 * at + 1) * part : (2 * at + 2) * part]
+
     for p in range(points):
-        near, far = right_operands(w_ref, p)
-        own = product(s_ref[p].reshape(chunks * 4 * SUB, wide), near).reshape(chunks, 2, 2, SUB, 6 * LANES)
-        other_work(2 * p)
-        later = product(s_ref[p, :, 1].reshape(chunks * 2 * SUB, wide), far).reshape(chunks, 2, SUB, 6 * LANES)
-        other_work(2 * p + 1)
+        even, last, middle = right_operands(w_ref, p)
+        d_even = rows_of(product(s_ref[p, :, 0:2].reshape(chunks * 4 * SUB, 2 * LANES), even))
+        other_work(3 * p)
+        one_frame, two_frame = (s_ref[p, :, n].reshape(chunks * 2 * SUB, 2 * LANES) for n in (2, 1))
+        high = [f[:, :LANES] for f in (one_frame, two_frame)]
+        low = [f[:, LANES:] for f in (one_frame, two_frame)]
+        d_middle = rows_of(product(jnp.concatenate(high + low + high, 1), middle))
+        other_work(3 * p + 1)
+        d_last = rows_of(product(s_ref[p, :, 3].reshape(chunks * 2 * SUB, 2 * LANES), last))
+        other_work(3 * p + 2)
         for n in range(2):
-            y_ref[0, p, n] = shifted_sum((own[:, 0, n] + later[:, n]).reshape(width, 6 * LANES))
-            y_ref[1, p, n] = shifted_sum(own[:, 1, n].reshape(width, 6 * LANES))
+            first, third = whole(d_even[:, 0, n], 0), whole(d_even[:, 1, n], 0)
+            mid, end = d_middle[:, 0, n], d_last[:, 0, n]
+            frames = (
+                first + mid[..., :part],
+                mid[..., part:] + whole(end, 0),
+                third + whole(end, 1),
+                whole(end, 2),
+            )
+            for t, taps in enumerate(frames):
+                y_ref[t, p, n] = shifted_sum(taps.reshape(width, part))
 
     for t in range(4):
-        lanes = pl.ds(t % 2 * LANES, LANES)
         for tile in range(2):
-            rows = outputs([y_ref[t // 2, p, tile, :, lanes] for p in range(points)], size)
+            rows = outputs([y_ref[t, p, tile] for p in range(points)], size)
             for o, value in enumerate(rows):
                 emit(t, tile * size + o, value)
         if done is not None:
@@ -454,8 +474,8 @@
     def scratch(size):
         points = len(POINTS[size])
         return [
-            vmem(points, width // SUB, 2, 2 * SUB, 4 * LANES, dtype=BF16),
-            vmem(2, points, 2, width, 2 * LANES),
+            vmem(points, width // SUB, frames, 2 * SUB, 2 * LANES, dtype=BF16),
+            vmem(frames, points, 2, width, LANES),
         ]
 
     grad, u2, u1 = call(

time: 45.4 us -> 47.9 us (1.055)
  Pallas kernels: 20.1 us -> 22.4 us
    pallas_call x6, Pallas kernels: 20.1 us -> 22.4 us  [call(): pl.pallas_call(body, out_shape=out_shape, in_specs=[SMEM_SPEC if a.dtype...]
  transfers between devices with their start and end apart: 8 -> 8, of which waited for: 1 -> 1; matrix products, arithmetic and copies ran while one was open for 0% -> 0% of each run, Pallas kernels for 20% -> 21%
where the time goes in v7:
time: 47.9 us; the launch traced here: 47.7 us
  starting transfers between devices  23.4 us (49%)
  Pallas kernels  22.4 us (47%)
  waiting for transfers between devices  1.45 us (3%)
    ppermute x8, starting transfers between devices, swap(): return lax.ppermute(value, axis, pairs)  23.4 us
    pallas_call x6, Pallas kernels, call(): pl.pallas_call(body, out_shape=out_shape, in_specs=[SMEM_SPEC if a.dtype...  22.4 us
    ppermute x8, waiting for transfers between devices, swap(): return lax.ppermute(value, axis, pairs)  1.45 us
  transfers between devices with their start and end apart: 8, of which 1 were waited for; matrix products, arithmetic and copies ran while one was open for 0% of the time, Pallas kernels for 21%

profile of v7, /device:TPU:0, one launch (start us, length us, event | category | flops | bytes accessed | tf_op | source)
XLA Modules:
  0.0 47.7 jit_solution(7373284304951465146)
XLA Ops:
  0.0 0.1 pad_add_fusion.par_ref
  0.1 2.0 %shard_map.64 = (f32[3,3,64,128]{3,2,1,0:T(8,128)S(1)}, f32[3,3,64,128]{3,2,1,0:T(8,128)S(1)}, f32[4,4,8,128]{3,2,1,0:T(8,128)S(1)}, f32[4,4,8,128]{3,2,1,0:T(8,...) custom-call(s32[2]{0:T(128)S(1)} %pad_add_fusion.par_ref, ...), custom_call_target="tpu_custom_call" | custom-call | tf_op jit(solution)/shard_map/pallas_call | solution.py:420
  2.1 0.7 %collective-permute-start = (f32[4,4,8,128]{3,2,1,0:T(8,128)S(1)}, f32[4,4,8,128]{3,2,1,0:T(8,128)S(1)}, u32[]{:S(2)}, u32[]{:S(2)}) collective-permute-start(f32[4,4,8,128]{3,2,1,0:T(8,128)S(1)} %get-tuple-element.26), channel_id=1, source_target_pairs={{1,2},{2,1},{5,6},{6,5},{9,10},{10,9},{13,14},{14,13},{17,18},{18,... | collective-permute-start | bytes 196616 | tf_op jit(solution)/shard_map/ppermute | solution.py:407
  2.8 4.4 %collective-permute-start.1 = (f32[4,4,8,128]{3,2,1,0:T(8,128)S(1)}, f32[4,4,8,128]{3,2,1,0:T(8,128)S(1)}, u32[]{:S(2)}, u32[]{:S(2)}) collective-permute-start(f32[4,4,8,128]{3,2,1,0:T(8,128)S(1)} %get-tuple-element.27), channel_id=1, source_target_pairs={{0,1},{1,0},{2,3},{3,2},{4,5},{5,4},{6,7},{7,6},{8,9},{9,8},{10,11... | collective-permute-start | bytes 196616 | tf_op jit(solution)/shard_map/ppermute | solution.py:407
  7.2 0.7 %collective-permute-start.2 = (f32[3,3,64,128]{3,2,1,0:T(8,128)S(1)}, f32[3,3,64,128]{3,2,1,0:T(8,128)S(1)}, u32[]{:S(2)}, u32[]{:S(2)}) collective-permute-start(f32[3,3,64,128]{3,2,1,0:T(8,128)S(1)} %get-tuple-element.36), channel_id=1, source_target_pairs={{4,8},{8,4},{5,9},{9,5},{6,10},{10,6},{7,11},{11,7},{20,24},{24,20... | collective-permute-start | bytes 884744 | tf_op jit(solution)/shard_map/ppermute | solution.py:407
  7.8 4.4 %collective-permute-start.3 = (f32[3,3,64,128]{3,2,1,0:T(8,128)S(1)}, f32[3,3,64,128]{3,2,1,0:T(8,128)S(1)}, u32[]{:S(2)}, u32[]{:S(2)}) collective-permute-start(f32[3,3,64,128]{3,2,1,0:T(8,128)S(1)} %get-tuple-element.37), channel_id=1, source_target_pairs={{0,4},{4,0},{8,12},{12,8},{1,5},{5,1},{9,13},{13,9},{2,6},{6,2},{1... | collective-permute-start | bytes 884744 | tf_op jit(solution)/shard_map/ppermute | solution.py:407
  12.3 1.2 %shard_map.65 = (f32[3,3,64,128]{3,2,1,0:T(8,128)S(1)}, f32[3,3,64,128]{3,2,1,0:T(8,128)S(1)}, f32[4,4,72,128]{3,2,1,0:T(8,128)S(1)}, f32[4,4,72,128]{3,2,1,0:T(8,128)S(1)}) custom-call(s32[2]{0:T(128)S(1)} %pad_add_fusion.par_ref, f32[4,4,64,96]{3,2,1,0:T(8,128)S(1)} %get-tuple-element.29.sec_ref, f32[4,4,64,96]{3,2,1,0:T(8,128)S(1)} %get-tuple-element.30.fst_ref), custom_call_target="tpu_custom_call" | custom-call | tf_op jit(solution)/shard_map/pallas_call | solution.py:420
  13.4 0.0 copy-start
  13.5 0.0 collective-permute-done.rw0
  13.5 0.0 collective-permute-done.1.rw1
  13.5 0.7 %shard_map.66 = (f32[3,6,8,128]{3,2,1,0:T(8,128)S(1)}, f32[3,6,8,128]{3,2,1,0:T(8,128)S(1)}, f32[4,4,72,128]{3,2,1,0:T(8,128)S(1)}, f32[4,4,72,128]{3,2,1,0:T(8,...) custom-call(s32[2]{0:T(128)S(1)} %pad_add_fusion.par_ref, ...), custom_call_target="tpu_custom_call", output_to_operand_aliasing={{2}: (3, {}), {3}: (4, {}), {4}: (5, {}), {5}: (6, {}), {6}... | custom-call | tf_op jit(solution)/shard_map/pallas_call | solution.py:420
  14.2 0.7 %collective-permute-start.6 = (f32[3,3,64,128]{3,2,1,0:T(8,128)S(1)}, f32[3,3,64,128]{3,2,1,0:T(8,128)S(1)}, u32[]{:S(2)}, u32[]{:S(2)}) collective-permute-start(f32[3,3,64,128]{3,2,1,0:T(8,128)S(1)} %get-tuple-element.43), channel_id=1, source_target_pairs={{4,8},{8,4},{5,9},{9,5},{6,10},{10,6},{7,11},{11,7},{20,24},{24,20... | collective-permute-start | bytes 884744 | tf_op jit(solution)/shard_map/ppermute | solution.py:407
  14.9 1.8 %collective-permute-start.7 = (f32[3,3,64,128]{3,2,1,0:T(8,128)S(1)}, f32[3,3,64,128]{3,2,1,0:T(8,128)S(1)}, u32[]{:S(2)}, u32[]{:S(2)}) collective-permute-start(f32[3,3,64,128]{3,2,1,0:T(8,128)S(1)} %get-tuple-element.44), channel_id=1, source_target_pairs={{0,4},{4,0},{8,12},{12,8},{1,5},{5,1},{9,13},{13,9},{2,6},{6,2},{1... | collective-permute-start | bytes 884744 | tf_op jit(solution)/shard_map/ppermute | solution.py:407
  16.6 0.7 %collective-permute-start.4 = (f32[3,6,8,128]{3,2,1,0:T(8,128)S(1)}, f32[3,6,8,128]{3,2,1,0:T(8,128)S(1)}, u32[]{:S(2)}, u32[]{:S(2)}) collective-permute-start(f32[3,6,8,128]{3,2,1,0:T(8,128)S(1)} %get-tuple-element.38), channel_id=1, source_target_pairs={{4,8},{8,4},{5,9},{9,5},{6,10},{10,6},{7,11},{11,7},{20,24},{24,20... | collective-permute-start | bytes 221192 | tf_op jit(solution)/shard_map/ppermute | solution.py:407
  17.3 0.0 copy-start.1
  17.3 0.0 copy-start.2
  17.3 10.1 %collective-permute-start.5 = (f32[3,6,8,128]{3,2,1,0:T(8,128)S(1)}, f32[3,6,8,128]{3,2,1,0:T(8,128)S(1)}, u32[]{:S(2)}, u32[]{:S(2)}) collective-permute-start(f32[3,6,8,128]{3,2,1,0:T(8,128)S(1)} %get-tuple-element.39), channel_id=1, source_target_pairs={{0,4},{4,0},{8,12},{12,8},{1,5},{5,1},{9,13},{13,9},{2,6},{6,2},{1... | collective-permute-start | bytes 221192 | tf_op jit(solution)/shard_map/ppermute | solution.py:407
  27.5 0.9 %shard_map.67.w_ref = bf16[6,3,2,128,384]{4,3,2,1,0:T(8,128)(2,1)S(1)} custom-call(f32[3,3,3,96,96]{4,3,2,1,0:T(8,128)S(1)} %copy-done), custom_call_target="tpu_custom_call" | custom-call | tf_op jit(solution)/shard_map/pallas_call | solution.py:420
  28.4 1.4 %collective-permute-done.5.rc1 = f32[3,6,8,128]{3,2,1,0:T(8,128)S(1)} collective-permute-done((f32[3,6,8,128]{3,2,1,0:T(8,128)S(1)}, f32[3,6,8,128]{3,2,1,0:T(8,128)S(1)}, u32[]{:S(2)}, u32[]{:S(2)}) %collective-permute-start.5) | collective-permute-done | bytes 73760 | tf_op jit(solution)/shard_map/ppermute | solution.py:407
  29.8 0.0 collective-permute-done.2.ra0
  29.8 0.0 collective-permute-done.3.ra1
  29.8 7.1 %shard_map.68 = (f32[4,8,72,128]{3,2,1,0:T(8,128)S(1)}, bf16[5,3,2,128,384]{4,3,2,1,0:T(8,128)(2,1)S(1)}, bf16[4,3,2,128,384]{4,3,2,1,0:T(8,128)(2,1)S(1)}) custom-call(s32[2]{0:T(128)S(1)} %pad_add_fusion.par_ref, f32[4,4,72,128]{3,2,1,0:T(8,128)S(1)} %get-tuple-element.35.cp_ref, f32[3,3,64,128]{3,2,1,0:T(8,128)S(1)} %collective-permute-done.2.ra0, ...), custom_call_target="tpu_custom_call" | custom-call | tf_op jit(solution)/shard_map/pallas_call | solution.py:420
  36.9 0.0 collective-permute-done.6.rb0
  37.0 10.6 %shard_map.69 = f32[4,4,64,96]{3,2,1,0:T(8,128)} custom-call(s32[2]{0:T(128)S(1)} %pad_add_fusion.par_ref, f32[4,8,72,128]{3,2,1,0:T(8,128)S(1)} %get-tuple-element.40.g_ref, f32[4,4,72,128]{3,2,1,0:T(8,128)S(1)} %get-tuple-element.41.s2_ref, f32[4,4,72,128]{3,2,1,0:T(8,128)S(1)} %get-tuple-element.42.s1_ref, ...), custom_call_target="tpu_custom_call" | custom-call | tf_op jit(solution)/shard_map/pallas_call | solution.py:420
  (5 shorter events, 0.0 us)
Async XLA Ops:
  2.1 11.4 %collective-permute-start = (f32[4,4,8,128]{3,2,1,0:T(8,128)S(1)}, f32[4,4,8,128]{3,2,1,0:T(8,128)S(1)}, u32[]{:S(2)}, u32[]{:S(2)}) collective-permute-start(f32[4,4,8,128]{3,2,1,0:T(8,128)S(1)} %get-tuple-element.26), channel_id=1, source_target_pairs={{1,2},{2,1},{5,6},{6,5},{9,10},{10,9},{13,14},{14,13},{17,18},{18,... | collective-permute-start | bytes 196616 | tf_op jit(solution)/shard_map/ppermute | solution.py:407
  2.8 10.7 %collective-permute-start.1 = (f32[4,4,8,128]{3,2,1,0:T(8,128)S(1)}, f32[4,4,8,128]{3,2,1,0:T(8,128)S(1)}, u32[]{:S(2)}, u32[]{:S(2)}) collective-permute-start(f32[4,4,8,128]{3,2,1,0:T(8,128)S(1)} %get-tuple-element.27), channel_id=1, source_target_pairs={{0,1},{1,0},{2,3},{3,2},{4,5},{5,4},{6,7},{7,6},{8,9},{9,8},{10,11... | collective-permute-start | bytes 196616 | tf_op jit(solution)/shard_map/ppermute | solution.py:407
  7.2 22.6 %collective-permute-start.2 = (f32[3,3,64,128]{3,2,1,0:T(8,128)S(1)}, f32[3,3,64,128]{3,2,1,0:T(8,128)S(1)}, u32[]{:S(2)}, u32[]{:S(2)}) collective-permute-start(f32[3,3,64,128]{3,2,1,0:T(8,128)S(1)} %get-tuple-element.36), channel_id=1, source_target_pairs={{4,8},{8,4},{5,9},{9,5},{6,10},{10,6},{7,11},{11,7},{20,24},{24,20... | collective-permute-start | bytes 884744 | tf_op jit(solution)/shard_map/ppermute | solution.py:407
  7.8 22.0 %collective-permute-start.3 = (f32[3,3,64,128]{3,2,1,0:T(8,128)S(1)}, f32[3,3,64,128]{3,2,1,0:T(8,128)S(1)}, u32[]{:S(2)}, u32[]{:S(2)}) collective-permute-start(f32[3,3,64,128]{3,2,1,0:T(8,128)S(1)} %get-tuple-element.37), channel_id=1, source_target_pairs={{0,4},{4,0},{8,12},{12,8},{1,5},{5,1},{9,13},{13,9},{2,6},{6,2},{1... | collective-permute-start | bytes 884744 | tf_op jit(solution)/shard_map/ppermute | solution.py:407
  13.4 14.0 %copy-start = (f32[3,3,3,96,96]{4,3,2,1,0:T(8,128)S(1)}, f32[3,3,3,96,96]{4,3,2,1,0:T(8,128)}, u32[]{:S(2)}) copy-start(f32[3,3,3,96,96]{4,3,2,1,0:T(8,128)} %w_ref.1) | copy-start | bytes 2985988
  14.2 22.8 %collective-permute-start.6 = (f32[3,3,64,128]{3,2,1,0:T(8,128)S(1)}, f32[3,3,64,128]{3,2,1,0:T(8,128)S(1)}, u32[]{:S(2)}, u32[]{:S(2)}) collective-permute-start(f32[3,3,64,128]{3,2,1,0:T(8,128)S(1)} %get-tuple-element.43), channel_id=1, source_target_pairs={{4,8},{8,4},{5,9},{9,5},{6,10},{10,6},{7,11},{11,7},{20,24},{24,20... | collective-permute-start | bytes 884744 | tf_op jit(solution)/shard_map/ppermute | solution.py:407
  14.9 22.1 %collective-permute-start.7 = (f32[3,3,64,128]{3,2,1,0:T(8,128)S(1)}, f32[3,3,64,128]{3,2,1,0:T(8,128)S(1)}, u32[]{:S(2)}, u32[]{:S(2)}) collective-permute-start(f32[3,3,64,128]{3,2,1,0:T(8,128)S(1)} %get-tuple-element.44), channel_id=1, source_target_pairs={{0,4},{4,0},{8,12},{12,8},{1,5},{5,1},{9,13},{13,9},{2,6},{6,2},{1... | collective-permute-start | bytes 884744 | tf_op jit(solution)/shard_map/ppermute | solution.py:407
  16.6 0.7 %collective-permute-start.4 = (f32[3,6,8,128]{3,2,1,0:T(8,128)S(1)}, f32[3,6,8,128]{3,2,1,0:T(8,128)S(1)}, u32[]{:S(2)}, u32[]{:S(2)}) collective-permute-start(f32[3,6,8,128]{3,2,1,0:T(8,128)S(1)} %get-tuple-element.38), channel_id=1, source_target_pairs={{4,8},{8,4},{5,9},{9,5},{6,10},{10,6},{7,11},{11,7},{20,24},{24,20... | collective-permute-start | bytes 221192 | tf_op jit(solution)/shard_map/ppermute | solution.py:407
  17.3 12.5 %copy-start.1 = (f32[3,3,3,96,96]{4,3,2,1,0:T(8,128)S(1)}, f32[3,3,3,96,96]{4,3,2,1,0:T(8,128)}, u32[]{:S(2)}) copy-start(f32[3,3,3,96,96]{4,3,2,1,0:T(8,128)} %w2_ref.1) | copy-start | bytes 2985988
  17.3 12.5 %copy-start.2 = (f32[3,3,3,96,96]{4,3,2,1,0:T(8,128)S(1)}, f32[3,3,3,96,96]{4,3,2,1,0:T(8,128)}, u32[]{:S(2)}) copy-start(f32[3,3,3,96,96]{4,3,2,1,0:T(8,128)} %w1_ref.1) | copy-start | bytes 2985988
  17.3 12.5 %collective-permute-start.5 = (f32[3,6,8,128]{3,2,1,0:T(8,128)S(1)}, f32[3,6,8,128]{3,2,1,0:T(8,128)S(1)}, u32[]{:S(2)}, u32[]{:S(2)}) collective-permute-start(f32[3,6,8,128]{3,2,1,0:T(8,128)S(1)} %get-tuple-element.39), channel_id=1, source_target_pairs={{0,4},{4,0},{8,12},{12,8},{1,5},{5,1},{9,13},{13,9},{2,6},{6,2},{1... | collective-permute-start | bytes 221192 | tf_op jit(solution)/shard_map/ppermute | solution.py:407

commit v8 on v6

--- a/solution.py
+++ b/solution.py
@@ -13,7 +13,11 @@
 F32 = jnp.float32
 BF16 = jnp.bfloat16
 VMEM_SPEC = pl.BlockSpec(memory_space=pltpu.VMEM)
-SMEM_SPEC = pl.BlockSpec(memory_space=pltpu.SMEM)
+HBM_SPEC = pl.BlockSpec(memory_space=pltpu.HBM)
+
+
+def parity(axis):
+    return (lax.axis_index(axis) + 1) % 2
 
 
 def silu_slope(value):
@@ -58,7 +62,7 @@
     return group_frames([src[t, h, 0:cols] for t in range(4)], chans)
 
 
-def pack_kernel(par_ref, cot_hbm, sec_hbm, fst_hbm, ma0, ma1, wp0, wp1, cp_ref, sec_ref, fst_ref, raw_ref, edge_ref, sems):
+def pack_kernel(cot_hbm, sec_hbm, fst_hbm, ma0, ma1, wp0, wp1, cp_ref, sec_ref, fst_ref, raw_ref, edge_ref, sems):
     frames, rows, cols, chans = cot_hbm.shape
     copies = [
         pltpu.make_async_copy(src, dst, sems.at[a])
@@ -77,11 +81,11 @@
                 for g, val in enumerate(group_row(cp_ref, h, cols, chans)):
                     dst[g, r] = val
 
-    @pl.when(par_ref[0] == 0)
+    @pl.when(parity("ha") == 0)
     def _():
         rows_out(ma1, ma0)
 
-    @pl.when(par_ref[0] != 0)
+    @pl.when(parity("ha") != 0)
     def _():
         rows_out(ma0, ma1)
 
@@ -103,17 +107,19 @@
                     sub < 3, c0, jnp.where((sub == 4) | (sub == 5), roll(a0, 4, 0), jnp.where(sub == 6, roll(b0, 6, 0), 0.0))
                 )
 
-    @pl.when(par_ref[1] == 0)
+    @pl.when(parity("wa") == 0)
     def _():
         cols_out(wp1, wp0)
 
-    @pl.when(par_ref[1] != 0)
+    @pl.when(parity("wa") != 0)
     def _():
         cols_out(wp0, wp1)
 
 
-def slope_kernel(par_ref, sec_ref, fst_ref, mb0, mb1, s2_ref, s1_ref):
+def slope_kernel(wanted, sec_ref, fst_ref, w_hbm, mb0, mb1, s2_ref, s1_ref, u_ref, w_ref, sem):
     frames, rows, cols, chans = sec_ref.shape
+    load = pltpu.make_async_copy(w_hbm, w_ref, sem)
+    load.start()
     blank = jnp.zeros((cols, LANES), F32)
     for src, ref in ((sec_ref, s2_ref), (fst_ref, s1_ref)):
         for t in range(frames):
@@ -133,19 +139,23 @@
             for g, val in enumerate(group_row(src, h, cols, chans)):
                 dst[g, at] = val
 
-    @pl.when(par_ref[0] == 0)
+    @pl.when(parity("ha") == 0)
     def _():
         rows_out(mb1, mb0)
 
-    @pl.when(par_ref[0] != 0)
+    @pl.when(parity("ha") != 0)
     def _():
         rows_out(mb0, mb1)
 
-
-def corner_kernel(chans, par_ref, rw0, rw1, _c, _s2, _s1, _b0, _b1, mc0, mc1, cp_ref, s2_ref, s1_ref, _mb0, _mb1):
+    load.wait()
+    for step in prepare_all(w_ref, u_ref, wanted):
+        step()
+
+
+def corner_kernel(chans, rw0, rw1, _c, _s2, _s1, _b0, _b1, mc0, mc1, cp_ref, s2_ref, s1_ref, _mb0, _mb1):
     frames, rows = rw0.shape[:2]
     cols = cp_ref.shape[2] - SUB
-    even = par_ref[1] == 0
+    even = parity("wa") == 0
     sub = sub_of((SUB, LANES))
     for t in range(frames):
         for h in range(rows):
@@ -169,11 +179,11 @@
         put(s1_ref, 0, top, 5)
         put(s1_ref, rows - 1, low, 5)
 
-    @pl.when(par_ref[0] == 0)
+    @pl.when(parity("ha") == 0)
     def _():
         out(mc1, mc0)
 
-    @pl.when(par_ref[0] != 0)
+    @pl.when(parity("ha") != 0)
     def _():
         out(mc0, mc1)
 
@@ -213,11 +223,6 @@
     return steps
 
 
-def weight_kernel(wanted, w_ref, out_ref):
-    for step in prepare_all(w_ref, out_ref, wanted):
-        step()
-
-
 POINTS = {2: (0, 1, 2, 5), 3: (0, 1, 2, 3, 5), 4: (0, 1, 2, 3, 4, 5)}
 
 
@@ -274,7 +279,7 @@
     return roll(taps[:, :two], -1, 0) + taps[:, two : 2 * two] + roll(taps[:, 2 * two :], 1, 0)
 
 
-def conv(read, size, width, s_ref, y_ref, w_ref, emit, done=None, beside=()):
+def conv(read, size, width, s_ref, y_ref, w_ref, emit, done=None, beside=(), ready=()):
     chunks = width // SUB
     points = len(POINTS[size])
 
@@ -291,6 +296,8 @@
         return carry
 
     lax.fori_loop(0, chunks, one, 0)
+    for load in ready:
+        load.wait()
 
     wide = 4 * LANES
     gap = 2 * points
@@ -319,18 +326,22 @@
             done(t)
 
 
-def halo_rows(chans, par, from_even, from_odd, r):
-    return ungroup_frames([jnp.where(par == 0, from_even[g, r], from_odd[g, r]) for g in range(3)], chans)
-
-
-def third_kernel(chans, par_ref, cp_ref, ra0, ra1, rc0, rc1, w_ref, w2_ref, w1_ref, out_ref, u2_ref, u1_ref, x_ref, s_ref, y_ref):
+def halo_rows(chans, from_even, from_odd, r):
+    return ungroup_frames([jnp.where(parity("ha") == 0, from_even[g, r], from_odd[g, r]) for g in range(3)], chans)
+
+
+def third_kernel(chans, cp_ref, ra0, ra1, rc0, rc1, w_ref, w2_hbm, w1_hbm, out_ref, u2_ref, u1_ref, x_ref, s_ref, y_ref,
+                 w2_ref, w1_ref, sems):
+    loads = [pltpu.make_async_copy(a, b, sems.at[n]) for n, (a, b) in enumerate(((w2_hbm, w2_ref), (w1_hbm, w1_ref)))]
+    for load in loads:
+        load.start()
     rows, width = cp_ref.shape[1:3]
     cols = width - SUB
     for r in range(3):
         for at, even, odd, ceven, codd in ((r, ra1, ra0, rc1, rc0), (r + 3, ra0, ra1, rc0, rc1)):
-            for t, frame in enumerate(halo_rows(chans, par_ref[0], even, odd, r)):
+            for t, frame in enumerate(halo_rows(chans, even, odd, r)):
                 x_ref[t, at, 0:cols] = frame
-            for t, frame in enumerate(halo_rows(chans, par_ref[0], ceven, codd, r)):
+            for t, frame in enumerate(halo_rows(chans, ceven, codd, r)):
                 x_ref[t, at, cols:] = frame
 
     def read(t, r, at):
@@ -342,18 +353,18 @@
         out_ref[t, o] = value
 
     beside = prepare_all(w2_ref, u2_ref, POINTS[(rows + 2) // 2]) + prepare_all(w1_ref, u1_ref, POINTS[rows // 2])
-    conv(read, rows, width, s_ref, y_ref, w_ref, emit, beside=beside)
-
-
-def last_kernel(chans, par_ref, g_ref, s2_ref, s1_ref, rb0, rb1, rc0, rc1, w2_ref, w1_ref, out_hbm,
+    conv(read, rows, width, s_ref, y_ref, w_ref, emit, beside=beside, ready=loads)
+
+
+def last_kernel(chans, g_ref, s2_ref, s1_ref, rb0, rb1, rc0, rc1, w2_ref, w1_ref, out_hbm,
                 e_ref, x1_ref, s_ref, y_ref, stage_ref, sems):
     frames, rows, width, _ = s2_ref.shape
     cols = width - SUB
     for r in range(3):
         for side, even, odd, ceven, codd in ((0, rb1, rb0, rc1, rc0), (1, rb0, rb1, rc0, rc1)):
-            for t, frame in enumerate(halo_rows(chans, par_ref[0], even, odd, r)):
+            for t, frame in enumerate(halo_rows(chans, even, odd, r)):
                 e_ref[side, r, t, 0:cols] = frame
-            for t, frame in enumerate(halo_rows(chans, par_ref[0], ceven, codd, 3 + r)):
+            for t, frame in enumerate(halo_rows(chans, ceven, codd, 3 + r)):
                 e_ref[side, r, t, cols:] = frame
 
     def slope2(t, r, at):
@@ -394,25 +405,22 @@
     return got
 
 
-def call(body, out_shape, args, scratch=(), hbm=False, hbm_out=False, alias=None, vmem=40 << 20, flops=0, cost=0):
-    hbm_spec = pl.BlockSpec(memory_space=pltpu.HBM)
-    where, out = hbm_spec if hbm else VMEM_SPEC, hbm_spec if hbm_out else VMEM_SPEC
+def call(body, out_shape, args, scratch=(), hbm=(), hbm_out=False, alias=None, vmem=40 << 20):
+    out = HBM_SPEC if hbm_out else VMEM_SPEC
     return pl.pallas_call(
         body,
         out_shape=out_shape,
-        in_specs=[SMEM_SPEC if a.dtype == jnp.int32 else where for a in args],
+        in_specs=[HBM_SPEC if n in hbm else VMEM_SPEC for n in range(len(args))],
         out_specs=jax.tree.map(lambda _: out, out_shape),
         scratch_shapes=list(scratch),
         input_output_aliases=alias or {},
         compiler_params=pltpu.CompilerParams(vmem_limit_bytes=vmem),
-        cost_estimate=pl.CostEstimate(flops=flops, bytes_accessed=cost, transcendentals=0),
     )(*args)
 
 
 def program(cotangent, stored_first, stored_second, w_first, w_second, w_third):
     frames, rows, cols, chans = cotangent.shape
     width = cols + SUB
-    par = jnp.stack([(lax.axis_index("ha") + 1) % 2, (lax.axis_index("wa") + 1) % 2]).astype(jnp.int32)
 
     def arr(*shape, dtype=F32):
         return jax.ShapeDtypeStruct(shape, dtype)
@@ -424,32 +432,40 @@
     own = arr(frames, rows, width, LANES)
     message = arr(3, 3, cols, LANES)
     corner = arr(3, 6, SUB, LANES)
-    fields = tuple(pltpu.with_memory_space_constraint(x, pltpu.HBM) for x in (cotangent, stored_second, stored_first))
+    *fields, third, second, first = (
+        pltpu.with_memory_space_constraint(x, pltpu.HBM)
+        for x in (cotangent, stored_second, stored_first, w_third, w_second, w_first)
+    )
     raw = arr(frames, rows, cols, chans)
     ma0, ma1, wp0, wp1, cp, sec, fst = call(
         pack_kernel,
         (message,) * 2 + (edge,) * 2 + (own, raw, raw),
-        (par,) + fields,
+        tuple(fields),
         [vmem(frames, rows, cols, chans), vmem(2, 2, frames, rows, SUB, LANES), pltpu.SemaphoreType.DMA((3,))],
-        hbm=True,
+        hbm=(0, 1, 2),
     )
     ra0, ra1 = swaps(ma0, ma1, "ha")
     rw0, rw1 = swaps(wp0, wp1, "wa")
-    mb0, mb1, s2, s1 = call(slope_kernel, (message,) * 2 + (own,) * 2, (par, sec, fst))
+
+    def weights(size):
+        return arr(len(POINTS[size]), 3, 2, LANES, 3 * LANES, dtype=BF16)
+
+    size3, size2, size1 = rows, (rows + 2) // 2, rows // 2
+    mb0, mb1, s2, s1, u3 = call(
+        functools.partial(slope_kernel, POINTS[size3]),
+        (message,) * 2 + (own,) * 2 + (weights(size3),),
+        (sec, fst, third),
+        [vmem(*third.shape), pltpu.SemaphoreType.DMA],
+        hbm=(2,),
+    )
     mc0, mc1, cp, s2, s1, mb0, mb1 = call(
         functools.partial(corner_kernel, chans),
         (corner,) * 2 + (own,) * 3 + (message,) * 2,
-        (par, rw0, rw1, cp, s2, s1, mb0, mb1),
-        alias={n + 3: n + 2 for n in range(5)},
+        (rw0, rw1, cp, s2, s1, mb0, mb1),
+        alias={n + 2: n + 2 for n in range(5)},
     )
     rc0, rc1 = swaps(mc0, mc1, "ha")
     rb0, rb1 = swaps(mb0, mb1, "ha")
-
-    def weights(size):
-        return arr(len(POINTS[size]), 3, 2, LANES, 3 * LANES, dtype=BF16)
-
-    size3, size2, size1 = rows, (rows + 2) // 2, rows // 2
-    u3 = call(functools.partial(weight_kernel, POINTS[size3]), weights(size3), (w_third,))
 
     def scratch(size):
         points = len(POINTS[size])
@@ -461,13 +477,16 @@
     grad, u2, u1 = call(
         functools.partial(third_kernel, chans),
         (arr(frames, rows + 4, width, LANES), weights(size2), weights(size1)),
-        (par, cp, ra0, ra1, rc0, rc1, u3, w_second, w_first),
-        [vmem(frames, 6, width, LANES)] + scratch(size3),
+        (cp, ra0, ra1, rc0, rc1, u3, second, first),
+        [vmem(frames, 6, width, LANES)]
+        + scratch(size3)
+        + [vmem(*second.shape), vmem(*first.shape), pltpu.SemaphoreType.DMA((2,))],
+        hbm=(6, 7),
     )
     return call(
         functools.partial(last_kernel, chans),
         arr(frames, rows, cols, chans),
-        (par, grad, s2, s1, rb0, rb1, rc0, rc1, u2, u1),
+        (grad, s2, s1, rb0, rb1, rc0, rc1, u2, u1),
         [vmem(2, 3, frames, width, LANES), vmem(frames, rows + 2, width, LANES)]
         + scratch(size2)
         + [vmem(frames, rows, cols, chans), pltpu.SemaphoreType.DMA((frames,))],

time: 45.4 us -> 45.1 us (level)
  waiting for transfers between devices: 1.45 us -> 2.35 us
  Pallas kernels: 20.1 us -> 19.3 us
  starting transfers between devices: 23.4 us -> 22.9 us
    ppermute x8, waiting for transfers between devices: 1.45 us -> 2.35 us  [swap(): return lax.ppermute(value, axis, pairs)]
    pallas_call x6 -> x5, Pallas kernels: 20.1 us -> 19.3 us  [call(): pl.pallas_call(body, out_shape=out_shape, in_specs=[HBM_SPEC if n in hbm...]
    ppermute x8, starting transfers between devices: 23.4 us -> 22.9 us  [swap(): return lax.ppermute(value, axis, pairs)]
  transfers between devices with their start and end apart: 8 -> 8, of which waited for: 1 -> 1; matrix products, arithmetic and copies ran while one was open for 0% -> 0% of each run, Pallas kernels for 20% -> 21%
where the time goes in v8:
time: 45.1 us; the launch traced here: 44.8 us
  starting transfers between devices  22.9 us (51%)
  Pallas kernels  19.3 us (43%)
  waiting for transfers between devices  2.35 us (5%)
    ppermute x8, starting transfers between devices, swap(): return lax.ppermute(value, axis, pairs)  22.9 us
    pallas_call x5, Pallas kernels, call(): pl.pallas_call(body, out_shape=out_shape, in_specs=[HBM_SPEC if n in hbm...  19.3 us
    ppermute x8, waiting for transfers between devices, swap(): return lax.ppermute(value, axis, pairs)  2.35 us
  transfers between devices with their start and end apart: 8, of which 1 were waited for; matrix products, arithmetic and copies ran while one was open for 0% of the time, Pallas kernels for 21%

profile of v8, /device:TPU:0, one launch (start us, length us, event | category | flops | bytes accessed | tf_op | source)
XLA Modules:
  0.0 44.8 jit_solution(9264169639636157679)
XLA Ops:
  0.0 1.5 %shard_map.64 = (f32[3,3,64,128]{3,2,1,0:T(8,128)S(1)}, f32[3,3,64,128]{3,2,1,0:T(8,128)S(1)}, f32[4,4,8,128]{3,2,1,0:T(8,128)S(1)}, f32[4,4,8,128]{3,2,1,0:T(8,...) custom-call(f32[4,4,64,96]{3,2,1,0:T(8,128)} %cot_hbm.1, ...), custom_call_target="tpu_custom_call" | custom-call | tf_op jit(solution)/shard_map/pallas_call | solution.py:410
  1.5 0.7 %collective-permute-start = (f32[4,4,8,128]{3,2,1,0:T(8,128)S(1)}, f32[4,4,8,128]{3,2,1,0:T(8,128)S(1)}, u32[]{:S(2)}, u32[]{:S(2)}) collective-permute-start(f32[4,4,8,128]{3,2,1,0:T(8,128)S(1)} %get-tuple-element.27), channel_id=1, source_target_pairs={{1,2},{2,1},{5,6},{6,5},{9,10},{10,9},{13,14},{14,13},{17,18},{18,... | collective-permute-start | bytes 196616 | tf_op jit(solution)/shard_map/ppermute | solution.py:398
  2.1 4.4 %collective-permute-start.1 = (f32[4,4,8,128]{3,2,1,0:T(8,128)S(1)}, f32[4,4,8,128]{3,2,1,0:T(8,128)S(1)}, u32[]{:S(2)}, u32[]{:S(2)}) collective-permute-start(f32[4,4,8,128]{3,2,1,0:T(8,128)S(1)} %get-tuple-element.28), channel_id=1, source_target_pairs={{0,1},{1,0},{2,3},{3,2},{4,5},{5,4},{6,7},{7,6},{8,9},{9,8},{10,11... | collective-permute-start | bytes 196616 | tf_op jit(solution)/shard_map/ppermute | solution.py:398
  6.5 0.7 %collective-permute-start.2 = (f32[3,3,64,128]{3,2,1,0:T(8,128)S(1)}, f32[3,3,64,128]{3,2,1,0:T(8,128)S(1)}, u32[]{:S(2)}, u32[]{:S(2)}) collective-permute-start(f32[3,3,64,128]{3,2,1,0:T(8,128)S(1)} %get-tuple-element.37), channel_id=1, source_target_pairs={{4,8},{8,4},{5,9},{9,5},{6,10},{10,6},{7,11},{11,7},{20,24},{24,20... | collective-permute-start | bytes 884744 | tf_op jit(solution)/shard_map/ppermute | solution.py:398
  7.2 4.4 %collective-permute-start.3 = (f32[3,3,64,128]{3,2,1,0:T(8,128)S(1)}, f32[3,3,64,128]{3,2,1,0:T(8,128)S(1)}, u32[]{:S(2)}, u32[]{:S(2)}) collective-permute-start(f32[3,3,64,128]{3,2,1,0:T(8,128)S(1)} %get-tuple-element.38), channel_id=1, source_target_pairs={{0,4},{4,0},{8,12},{12,8},{1,5},{5,1},{9,13},{13,9},{2,6},{6,2},{1... | collective-permute-start | bytes 884744 | tf_op jit(solution)/shard_map/ppermute | solution.py:398
  11.7 2.2 %shard_map.65 = (f32[3,3,64,128]{3,2,1,0:T(8,128)S(1)}, f32[3,3,64,128]{3,2,1,0:T(8,128)S(1)}, f32[4,4,72,128]{3,2,1,0:T(8,128)S(1)}, f32[4,4,72,128]{3,2,1,0:T(8,128)S(1)}, bf16[6,3,2,128,384]{4,3,2,1,0:T(8,128)(2,1)S(1)}) custom-call(f32[4,4,64,96]{3,2,1,0:T(8,128)S(1)} %get-tuple-element.30.sec_ref, f32[4,4,64,96]{3,2,1,0:T(8,128)S(1)} %get-tuple-element.31.fst_ref, ...), custom_call_target="tpu_custom_call" | custom-call | tf_op jit(solution)/shard_map/pallas_call | solution.py:410
  13.9 0.0 collective-permute-done.rw0
  13.9 0.0 collective-permute-done.1.rw1
  13.9 0.1 shard_map.66
  14.1 0.7 %collective-permute-start.6 = (f32[3,3,64,128]{3,2,1,0:T(8,128)S(1)}, f32[3,3,64,128]{3,2,1,0:T(8,128)S(1)}, u32[]{:S(2)}, u32[]{:S(2)}) collective-permute-start(f32[3,3,64,128]{3,2,1,0:T(8,128)S(1)} %get-tuple-element.45), channel_id=1, source_target_pairs={{4,8},{8,4},{5,9},{9,5},{6,10},{10,6},{7,11},{11,7},{20,24},{24,20... | collective-permute-start | bytes 884744 | tf_op jit(solution)/shard_map/ppermute | solution.py:398
  14.8 1.8 %collective-permute-start.7 = (f32[3,3,64,128]{3,2,1,0:T(8,128)S(1)}, f32[3,3,64,128]{3,2,1,0:T(8,128)S(1)}, u32[]{:S(2)}, u32[]{:S(2)}) collective-permute-start(f32[3,3,64,128]{3,2,1,0:T(8,128)S(1)} %get-tuple-element.46), channel_id=1, source_target_pairs={{0,4},{4,0},{8,12},{12,8},{1,5},{5,1},{9,13},{13,9},{2,6},{6,2},{1... | collective-permute-start | bytes 884744 | tf_op jit(solution)/shard_map/ppermute | solution.py:398
  16.5 0.8 %collective-permute-start.4 = (f32[3,6,8,128]{3,2,1,0:T(8,128)S(1)}, f32[3,6,8,128]{3,2,1,0:T(8,128)S(1)}, u32[]{:S(2)}, u32[]{:S(2)}) collective-permute-start(f32[3,6,8,128]{3,2,1,0:T(8,128)S(1)} %get-tuple-element.39), channel_id=1, source_target_pairs={{4,8},{8,4},{5,9},{9,5},{6,10},{10,6},{7,11},{11,7},{20,24},{24,20... | collective-permute-start | bytes 221192 | tf_op jit(solution)/shard_map/ppermute | solution.py:398
  17.4 0.0 collective-permute-done.4.rc0
  17.4 9.5 %collective-permute-start.5 = (f32[3,6,8,128]{3,2,1,0:T(8,128)S(1)}, f32[3,6,8,128]{3,2,1,0:T(8,128)S(1)}, u32[]{:S(2)}, u32[]{:S(2)}) collective-permute-start(f32[3,6,8,128]{3,2,1,0:T(8,128)S(1)} %get-tuple-element.40), channel_id=1, source_target_pairs={{0,4},{4,0},{8,12},{12,8},{1,5},{5,1},{9,13},{13,9},{2,6},{6,2},{1... | collective-permute-start | bytes 221192 | tf_op jit(solution)/shard_map/ppermute | solution.py:398
  26.8 2.3 %collective-permute-done.5.rc1 = f32[3,6,8,128]{3,2,1,0:T(8,128)S(1)} collective-permute-done((f32[3,6,8,128]{3,2,1,0:T(8,128)S(1)}, f32[3,6,8,128]{3,2,1,0:T(8,128)S(1)}, u32[]{:S(2)}, u32[]{:S(2)}) %collective-permute-start.5) | collective-permute-done | bytes 73760 | tf_op jit(solution)/shard_map/ppermute | solution.py:398
  29.2 0.0 collective-permute-done.2.ra0
  29.2 0.0 collective-permute-done.3.ra1
  29.2 7.0 %shard_map.67 = (f32[4,8,72,128]{3,2,1,0:T(8,128)S(1)}, bf16[5,3,2,128,384]{4,3,2,1,0:T(8,128)(2,1)S(1)}, bf16[4,3,2,128,384]{4,3,2,1,0:T(8,128)(2,1)S(1)}) custom-call(f32[4,4,72,128]{3,2,1,0:T(8,128)S(1)} %get-tuple-element.36.cp_ref, f32[3,3,64,128]{3,2,1,0:T(8,128)S(1)} %collective-permute-done.2.ra0, f32[3,3,64,128]{3,2,1,0:T(8,128)S(1)} %collective-permute-done.3.ra1, ...), custom_call_target="tpu_custom_call" | custom-call | tf_op jit(solution)/shard_map/pallas_call | solution.py:410
  36.2 0.0 collective-permute-done.6.rb0
  36.2 0.0 collective-permute-done.7.rb1
  36.2 8.5 %shard_map.68 = f32[4,4,64,96]{3,2,1,0:T(8,128)} custom-call(f32[4,8,72,128]{3,2,1,0:T(8,128)S(1)} %get-tuple-element.42.g_ref, f32[4,4,72,128]{3,2,1,0:T(8,128)S(1)} %get-tuple-element.43.s2_ref, f32[4,4,72,128]{3,2,1,0:T(8,128)S(1)} %get-tuple-element.44.s1_ref, f32[3,3,64,128]{3,2,1,0:T(8,128)S(1)} %collective-permute-done.6.rb0, ...), custom_call_target="tpu_custom_call" | custom-call | tf_op jit(solution)/shard_map/pallas_call | solution.py:410
Async XLA Ops:
  1.5 12.4 %collective-permute-start = (f32[4,4,8,128]{3,2,1,0:T(8,128)S(1)}, f32[4,4,8,128]{3,2,1,0:T(8,128)S(1)}, u32[]{:S(2)}, u32[]{:S(2)}) collective-permute-start(f32[4,4,8,128]{3,2,1,0:T(8,128)S(1)} %get-tuple-element.27), channel_id=1, source_target_pairs={{1,2},{2,1},{5,6},{6,5},{9,10},{10,9},{13,14},{14,13},{17,18},{18,... | collective-permute-start | bytes 196616 | tf_op jit(solution)/shard_map/ppermute | solution.py:398
  2.1 11.8 %collective-permute-start.1 = (f32[4,4,8,128]{3,2,1,0:T(8,128)S(1)}, f32[4,4,8,128]{3,2,1,0:T(8,128)S(1)}, u32[]{:S(2)}, u32[]{:S(2)}) collective-permute-start(f32[4,4,8,128]{3,2,1,0:T(8,128)S(1)} %get-tuple-element.28), channel_id=1, source_target_pairs={{0,1},{1,0},{2,3},{3,2},{4,5},{5,4},{6,7},{7,6},{8,9},{9,8},{10,11... | collective-permute-start | bytes 196616 | tf_op jit(solution)/shard_map/ppermute | solution.py:398
  6.5 22.6 %collective-permute-start.2 = (f32[3,3,64,128]{3,2,1,0:T(8,128)S(1)}, f32[3,3,64,128]{3,2,1,0:T(8,128)S(1)}, u32[]{:S(2)}, u32[]{:S(2)}) collective-permute-start(f32[3,3,64,128]{3,2,1,0:T(8,128)S(1)} %get-tuple-element.37), channel_id=1, source_target_pairs={{4,8},{8,4},{5,9},{9,5},{6,10},{10,6},{7,11},{11,7},{20,24},{24,20... | collective-permute-start | bytes 884744 | tf_op jit(solution)/shard_map/ppermute | solution.py:398
  7.2 22.0 %collective-permute-start.3 = (f32[3,3,64,128]{3,2,1,0:T(8,128)S(1)}, f32[3,3,64,128]{3,2,1,0:T(8,128)S(1)}, u32[]{:S(2)}, u32[]{:S(2)}) collective-permute-start(f32[3,3,64,128]{3,2,1,0:T(8,128)S(1)} %get-tuple-element.38), channel_id=1, source_target_pairs={{0,4},{4,0},{8,12},{12,8},{1,5},{5,1},{9,13},{13,9},{2,6},{6,2},{1... | collective-permute-start | bytes 884744 | tf_op jit(solution)/shard_map/ppermute | solution.py:398
  14.1 22.1 %collective-permute-start.6 = (f32[3,3,64,128]{3,2,1,0:T(8,128)S(1)}, f32[3,3,64,128]{3,2,1,0:T(8,128)S(1)}, u32[]{:S(2)}, u32[]{:S(2)}) collective-permute-start(f32[3,3,64,128]{3,2,1,0:T(8,128)S(1)} %get-tuple-element.45), channel_id=1, source_target_pairs={{4,8},{8,4},{5,9},{9,5},{6,10},{10,6},{7,11},{11,7},{20,24},{24,20... | collective-permute-start | bytes 884744 | tf_op jit(solution)/shard_map/ppermute | solution.py:398
  14.8 21.4 %collective-permute-start.7 = (f32[3,3,64,128]{3,2,1,0:T(8,128)S(1)}, f32[3,3,64,128]{3,2,1,0:T(8,128)S(1)}, u32[]{:S(2)}, u32[]{:S(2)}) collective-permute-start(f32[3,3,64,128]{3,2,1,0:T(8,128)S(1)} %get-tuple-element.46), channel_id=1, source_target_pairs={{0,4},{4,0},{8,12},{12,8},{1,5},{5,1},{9,13},{13,9},{2,6},{6,2},{1... | collective-permute-start | bytes 884744 | tf_op jit(solution)/shard_map/ppermute | solution.py:398
  16.5 0.8 %collective-permute-start.4 = (f32[3,6,8,128]{3,2,1,0:T(8,128)S(1)}, f32[3,6,8,128]{3,2,1,0:T(8,128)S(1)}, u32[]{:S(2)}, u32[]{:S(2)}) collective-permute-start(f32[3,6,8,128]{3,2,1,0:T(8,128)S(1)} %get-tuple-element.39), channel_id=1, source_target_pairs={{4,8},{8,4},{5,9},{9,5},{6,10},{10,6},{7,11},{11,7},{20,24},{24,20... | collective-permute-start | bytes 221192 | tf_op jit(solution)/shard_map/ppermute | solution.py:398
  17.4 11.8 %collective-permute-start.5 = (f32[3,6,8,128]{3,2,1,0:T(8,128)S(1)}, f32[3,6,8,128]{3,2,1,0:T(8,128)S(1)}, u32[]{:S(2)}, u32[]{:S(2)}) collective-permute-start(f32[3,6,8,128]{3,2,1,0:T(8,128)S(1)} %get-tuple-element.40), channel_id=1, source_target_pairs={{0,4},{4,0},{8,12},{12,8},{1,5},{5,1},{9,13},{13,9},{2,6},{6,2},{1... | collective-permute-start | bytes 221192 | tf_op jit(solution)/shard_map/ppermute | solution.py:398

commit v9 on v8

--- a/solution.py
+++ b/solution.py
@@ -62,7 +62,7 @@
     return group_frames([src[t, h, 0:cols] for t in range(4)], chans)
 
 
-def pack_kernel(cot_hbm, sec_hbm, fst_hbm, ma0, ma1, wp0, wp1, cp_ref, sec_ref, fst_ref, raw_ref, edge_ref, sems):
+def pack_kernel(cot_hbm, sec_hbm, fst_hbm, ma0, ma1, wp0, wp1, cp_ref, sec_ref, fst_ref, raw_ref, edge_ref, row_ref, sems):
     frames, rows, cols, chans = cot_hbm.shape
     copies = [
         pltpu.make_async_copy(src, dst, sems.at[a])
@@ -75,11 +75,20 @@
     copies[0].wait()
     cp_ref[:, :, 0:cols, 0:chans] = raw_ref[...]
 
+    row_ref[...] = jnp.zeros(row_ref.shape, F32)
+    for copy in copies[1:]:
+        copy.wait()
+    for at, h in enumerate((0, rows - 1)):
+        row_ref[:, at, :, 0:chans] = silu_slope(fst_ref[:, h])
+
     def rows_out(top, low):
         for r in range(3):
             for dst, h in ((top, r), (low, rows - 3 + r)):
                 for g, val in enumerate(group_row(cp_ref, h, cols, chans)):
                     dst[g, r] = val
+        for at, dst in enumerate((top, low)):
+            for g, val in enumerate(group_row(row_ref, at, cols, chans)):
+                dst[g, 3] = val
 
     @pl.when(parity("ha") == 0)
     def _():
@@ -90,7 +99,6 @@
         rows_out(ma0, ma1)
 
     for a, ref in ((0, sec_ref), (1, fst_ref)):
-        copies[1 + a].wait()
         for side, start in enumerate((0, cols - SUB)):
             edge_ref[a, side, :, :, :, 0:chans] = silu_slope(ref[:, :, start : start + SUB])
 
@@ -116,7 +124,7 @@
         cols_out(wp0, wp1)
 
 
-def slope_kernel(wanted, sec_ref, fst_ref, w_hbm, mb0, mb1, s2_ref, s1_ref, u_ref, w_ref, sem):
+def slope_kernel(sec_ref, fst_ref, w_hbm, mb0, mb1, s2_ref, s1_ref, w_ref, sem):
     frames, rows, cols, chans = sec_ref.shape
     load = pltpu.make_async_copy(w_hbm, w_ref, sem)
     load.start()
@@ -131,10 +139,8 @@
         for src, h, dst, at in (
             (s2_ref, 0, top, 0),
             (s2_ref, 1, top, 1),
-            (s1_ref, 0, top, 2),
             (s2_ref, rows - 2, low, 0),
             (s2_ref, rows - 1, low, 1),
-            (s1_ref, rows - 1, low, 2),
         ):
             for g, val in enumerate(group_row(src, h, cols, chans)):
                 dst[g, at] = val
@@ -148,8 +154,6 @@
         rows_out(mb0, mb1)
 
     load.wait()
-    for step in prepare_all(w_ref, u_ref, wanted):
-        step()
 
 
 def corner_kernel(chans, rw0, rw1, _c, _s2, _s1, _b0, _b1, mc0, mc1, cp_ref, s2_ref, s1_ref, _mb0, _mb1):
@@ -208,19 +212,22 @@
         out_ref[n, k, 1, 0:chans, lanes] = (value - high.astype(F32)).astype(BF16)
 
 
-def prepare_all(w_ref, out_ref, wanted):
+def prepare_point(w_ref, out_ref, wanted, n):
     chans = w_ref.shape[3]
 
-    def clear(n, k):
+    def clear(k):
         out_ref[n, k, :, chans:] = jnp.zeros((2, LANES - chans, 3 * LANES), BF16)
 
     steps = []
     for k in range(3):
-        for n in range(len(wanted)):
-            steps.append(functools.partial(clear, n, k))
-            for i in range(3):
-                steps.append(functools.partial(prepare, w_ref, out_ref, wanted, k, i, (n,)))
+        steps.append(functools.partial(clear, k))
+        for i in range(3):
+            steps.append(functools.partial(prepare, w_ref, out_ref, wanted, k, i, (n,)))
     return steps
+
+
+def spread(steps, slots):
+    return [steps[n * len(steps) // slots : (n + 1) * len(steps) // slots] for n in range(slots)]
 
 
 POINTS = {2: (0, 1, 2, 5), 3: (0, 1, 2, 3, 5), 4: (0, 1, 2, 3, 4, 5)}
@@ -279,7 +286,7 @@
     return roll(taps[:, :two], -1, 0) + taps[:, two : 2 * two] + roll(taps[:, 2 * two :], 1, 0)
 
 
-def conv(read, size, width, s_ref, y_ref, w_ref, emit, done=None, beside=(), ready=()):
+def conv(read, size, width, s_ref, y_ref, w_ref, emit, done=None, beside=None):
     chunks = width // SUB
     points = len(POINTS[size])
 
@@ -296,14 +303,10 @@
         return carry
 
     lax.fori_loop(0, chunks, one, 0)
-    for load in ready:
-        load.wait()
-
     wide = 4 * LANES
-    gap = 2 * points
 
     def other_work(n):
-        for step in beside[n * len(beside) // gap : (n + 1) * len(beside) // gap]:
+        for step in beside[n] if beside else ():
             step()
 
     for p in range(points):
@@ -330,11 +333,9 @@
     return ungroup_frames([jnp.where(parity("ha") == 0, from_even[g, r], from_odd[g, r]) for g in range(3)], chans)
 
 
-def third_kernel(chans, cp_ref, ra0, ra1, rc0, rc1, w_ref, w2_hbm, w1_hbm, out_ref, u2_ref, u1_ref, x_ref, s_ref, y_ref,
-                 w2_ref, w1_ref, sems):
-    loads = [pltpu.make_async_copy(a, b, sems.at[n]) for n, (a, b) in enumerate(((w2_hbm, w2_ref), (w1_hbm, w1_ref)))]
-    for load in loads:
-        load.start()
+def third_kernel(chans, cp_ref, ra0, ra1, rc0, rc1, w3_ref, w2_hbm, out_ref, u2_ref, x_ref, u3_ref, s_ref, y_ref, w2_ref, sem):
+    load = pltpu.make_async_copy(w2_hbm, w2_ref, sem)
+    load.start()
     rows, width = cp_ref.shape[1:3]
     cols = width - SUB
     for r in range(3):
@@ -352,19 +353,35 @@
     def emit(t, o, value):
         out_ref[t, o] = value
 
-    beside = prepare_all(w2_ref, u2_ref, POINTS[(rows + 2) // 2]) + prepare_all(w1_ref, u1_ref, POINTS[rows // 2])
-    conv(read, rows, width, s_ref, y_ref, w_ref, emit, beside=beside, ready=loads)
-
-
-def last_kernel(chans, g_ref, s2_ref, s1_ref, rb0, rb1, rc0, rc1, w2_ref, w1_ref, out_hbm,
-                e_ref, x1_ref, s_ref, y_ref, stage_ref, sems):
+    own, later = POINTS[rows], POINTS[(rows + 2) // 2]
+    for step in prepare_point(w3_ref, u3_ref, own, 0):
+        step()
+    slots = len(own) * 2
+    beside = [[] for _ in range(slots)]
+    for p in range(1, len(own)):
+        for n, steps in enumerate(spread(prepare_point(w3_ref, u3_ref, own, p), 2)):
+            beside[2 * p - 2 + n] += steps
+    steps = [load.wait]
+    for n in range(len(later)):
+        steps += prepare_point(w2_ref, u2_ref, later, n)
+    for n, some in enumerate(spread(steps, slots - 2)):
+        beside[n + 2] += some
+    conv(read, rows, width, s_ref, y_ref, u3_ref, emit, beside=beside)
+
+
+def last_kernel(chans, g_ref, s2_ref, s1_ref, ra0, ra1, rb0, rb1, rc0, rc1, u2_ref, w1_hbm, out_hbm,
+                e_ref, x1_ref, u1_ref, s_ref, y_ref, w1_ref, stage_ref, load_sem, sems):
+    load = pltpu.make_async_copy(w1_hbm, w1_ref, load_sem)
+    load.start()
     frames, rows, width, _ = s2_ref.shape
     cols = width - SUB
-    for r in range(3):
-        for side, even, odd, ceven, codd in ((0, rb1, rb0, rc1, rc0), (1, rb0, rb1, rc0, rc1)):
-            for t, frame in enumerate(halo_rows(chans, even, odd, r)):
+    for side, (even, odd) in enumerate(((1, 0), (0, 1))):
+        for r in range(3):
+            main, at = ((rb0, rb1), r) if r < 2 else ((ra0, ra1), 3)
+            for t, frame in enumerate(halo_rows(chans, main[even], main[odd], at)):
                 e_ref[side, r, t, 0:cols] = frame
-            for t, frame in enumerate(halo_rows(chans, ceven, codd, 3 + r)):
+            corners = (rc0, rc1)
+            for t, frame in enumerate(halo_rows(chans, corners[even], corners[odd], 3 + r)):
                 e_ref[side, r, t, cols:] = frame
 
     def slope2(t, r, at):
@@ -382,10 +399,13 @@
     def copy_out(t):
         return pltpu.make_async_copy(stage_ref.at[t], out_hbm.at[t], sems.at[t])
 
-    conv(lambda t, r, at: g_ref[t, r, at] * slope2(t, r, at), (rows + 2) // 2, width, s_ref, y_ref, w2_ref, emit2)
-    conv(
-        lambda t, r, at: x1_ref[t, r, at], rows // 2, width, s_ref, y_ref, w1_ref, emit1, lambda t: copy_out(t).start()
-    )
+    size2, size1 = (rows + 2) // 2, rows // 2
+    steps = [load.wait]
+    for n in range(len(POINTS[size1])):
+        steps += prepare_point(w1_ref, u1_ref, POINTS[size1], n)
+    beside = [[], []] + spread(steps, 2 * len(POINTS[size2]) - 2)
+    conv(lambda t, r, at: g_ref[t, r, at] * slope2(t, r, at), size2, width, s_ref, y_ref, u2_ref, emit2, beside=beside)
+    conv(lambda t, r, at: x1_ref[t, r, at], size1, width, s_ref, y_ref, u1_ref, emit1, lambda t: copy_out(t).start())
     for t in range(frames):
         copy_out(t).wait()
 
@@ -430,7 +450,7 @@
 
     edge = arr(frames, rows, SUB, LANES)
     own = arr(frames, rows, width, LANES)
-    message = arr(3, 3, cols, LANES)
+    rows_a, rows_b = arr(3, 4, cols, LANES), arr(3, 2, cols, LANES)
     corner = arr(3, 6, SUB, LANES)
     *fields, third, second, first = (
         pltpu.with_memory_space_constraint(x, pltpu.HBM)
@@ -439,9 +459,9 @@
     raw = arr(frames, rows, cols, chans)
     ma0, ma1, wp0, wp1, cp, sec, fst = call(
         pack_kernel,
-        (message,) * 2 + (edge,) * 2 + (own, raw, raw),
+        (rows_a,) * 2 + (edge,) * 2 + (own, raw, raw),
         tuple(fields),
-        [vmem(frames, rows, cols, chans), vmem(2, 2, frames, rows, SUB, LANES), pltpu.SemaphoreType.DMA((3,))],
+        [vmem(frames, rows, cols, chans), vmem(2, 2, frames, rows, SUB, LANES), vmem(frames, 2, cols, LANES), pltpu.SemaphoreType.DMA((3,))],
         hbm=(0, 1, 2),
     )
     ra0, ra1 = swaps(ma0, ma1, "ha")
@@ -451,16 +471,16 @@
         return arr(len(POINTS[size]), 3, 2, LANES, 3 * LANES, dtype=BF16)
 
     size3, size2, size1 = rows, (rows + 2) // 2, rows // 2
-    mb0, mb1, s2, s1, u3 = call(
-        functools.partial(slope_kernel, POINTS[size3]),
-        (message,) * 2 + (own,) * 2 + (weights(size3),),
+    mb0, mb1, s2, s1, third = call(
+        slope_kernel,
+        (rows_b,) * 2 + (own,) * 2 + (arr(*third.shape),),
         (sec, fst, third),
-        [vmem(*third.shape), pltpu.SemaphoreType.DMA],
+        [pltpu.SemaphoreType.DMA],
         hbm=(2,),
     )
     mc0, mc1, cp, s2, s1, mb0, mb1 = call(
         functools.partial(corner_kernel, chans),
-        (corner,) * 2 + (own,) * 3 + (message,) * 2,
+        (corner,) * 2 + (own,) * 3 + (rows_b,) * 2,
         (rw0, rw1, cp, s2, s1, mb0, mb1),
         alias={n + 2: n + 2 for n in range(5)},
     )
@@ -474,22 +494,32 @@
             vmem(2, points, 2, width, 2 * LANES),
         ]
 
-    grad, u2, u1 = call(
+    grad, u2 = call(
         functools.partial(third_kernel, chans),
-        (arr(frames, rows + 4, width, LANES), weights(size2), weights(size1)),
-        (cp, ra0, ra1, rc0, rc1, u3, second, first),
-        [vmem(frames, 6, width, LANES)]
+        (arr(frames, rows + 4, width, LANES), weights(size2)),
+        (cp, ra0, ra1, rc0, rc1, third, second),
+        [vmem(frames, 6, width, LANES), vmem(*weights(size3).shape, dtype=BF16)]
         + scratch(size3)
-        + [vmem(*second.shape), vmem(*first.shape), pltpu.SemaphoreType.DMA((2,))],
-        hbm=(6, 7),
+        + [vmem(*second.shape), pltpu.SemaphoreType.DMA],
+        hbm=(6,),
     )
     return call(
         functools.partial(last_kernel, chans),
         arr(frames, rows, cols, chans),
-        (grad, s2, s1, rb0, rb1, rc0, rc1, u2, u1),
-        [vmem(2, 3, frames, width, LANES), vmem(frames, rows + 2, width, LANES)]
+        (grad, s2, s1, ra0, ra1, rb0, rb1, rc0, rc1, u2, first),
+        [
+            vmem(2, 3, frames, width, LANES),
+            vmem(frames, rows + 2, width, LANES),
+            vmem(*weights(size1).shape, dtype=BF16),
+        ]
         + scratch(size2)
-        + [vmem(frames, rows, cols, chans), pltpu.SemaphoreType.DMA((frames,))],
+        + [
+            vmem(*first.shape),
+            vmem(frames, rows, cols, chans),
+            pltpu.SemaphoreType.DMA,
+            pltpu.SemaphoreType.DMA((frames,)),
+        ],
+        hbm=(10,),
         hbm_out=True,
     )
 

time: 45.1 us -> 42.5 us (0.942)
  starting transfers between devices: 22.9 us -> 21.2 us
  Pallas kernels: 19.3 us -> 18.5 us
    ppermute x8, starting transfers between devices: 22.9 us -> 21.2 us  [swap(): return lax.ppermute(value, axis, pairs)]
    pallas_call x5, Pallas kernels: 19.3 us -> 18.5 us  [call(): pl.pallas_call(body, out_shape=out_shape, in_specs=[HBM_SPEC if n in hbm...]
  transfers between devices with their start and end apart: 8 -> 8, of which waited for: 1 -> 1; matrix products, arithmetic and copies ran while one was open for 0% -> 0% of each run, Pallas kernels for 21% -> 18%
where the time goes in v9:
time: 42.5 us; the launch traced here: 42.3 us
  starting transfers between devices  21.2 us (50%)
  Pallas kernels  18.5 us (44%)
  waiting for transfers between devices  2.38 us (6%)
    ppermute x8, starting transfers between devices, swap(): return lax.ppermute(value, axis, pairs)  21.2 us
    pallas_call x5, Pallas kernels, call(): pl.pallas_call(body, out_shape=out_shape, in_specs=[HBM_SPEC if n in hbm...  18.5 us
    ppermute x8, waiting for transfers between devices, swap(): return lax.ppermute(value, axis, pairs)  2.38 us
  transfers between devices with their start and end apart: 8, of which 1 were waited for; matrix products, arithmetic and copies ran while one was open for 0% of the time, Pallas kernels for 18%

profile of v9, /device:TPU:0, one launch (start us, length us, event | category | flops | bytes accessed | tf_op | source)
XLA Modules:
  0.0 42.3 jit_solution(6298885836138397514)
XLA Ops:
  0.0 1.9 %shard_map.64 = (f32[3,4,64,128]{3,2,1,0:T(8,128)S(1)}, f32[3,4,64,128]{3,2,1,0:T(8,128)S(1)}, f32[4,4,8,128]{3,2,1,0:T(8,128)S(1)}, f32[4,4,8,128]{3,2,1,0:T(8,...) custom-call(f32[4,4,64,96]{3,2,1,0:T(8,128)} %cot_hbm.1, ...), custom_call_target="tpu_custom_call" | custom-call | tf_op jit(solution)/shard_map/pallas_call | solution.py:430
  1.9 0.7 %collective-permute-start.2 = (f32[3,4,64,128]{3,2,1,0:T(8,128)S(1)}, f32[3,4,64,128]{3,2,1,0:T(8,128)S(1)}, u32[]{:S(2)}, u32[]{:S(2)}) collective-permute-start(f32[3,4,64,128]{3,2,1,0:T(8,128)S(1)} %get-tuple-element.36), channel_id=1, source_target_pairs={{4,8},{8,4},{5,9},{9,5},{6,10},{10,6},{7,11},{11,7},{20,24},{24,20... | collective-permute-start | bytes 1179656 | tf_op jit(solution)/shard_map/ppermute | solution.py:418
  2.6 5.9 %collective-permute-start.3 = (f32[3,4,64,128]{3,2,1,0:T(8,128)S(1)}, f32[3,4,64,128]{3,2,1,0:T(8,128)S(1)}, u32[]{:S(2)}, u32[]{:S(2)}) collective-permute-start(f32[3,4,64,128]{3,2,1,0:T(8,128)S(1)} %get-tuple-element.37), channel_id=1, source_target_pairs={{0,4},{4,0},{8,12},{12,8},{1,5},{5,1},{9,13},{13,9},{2,6},{6,2},{1... | collective-permute-start | bytes 1179656 | tf_op jit(solution)/shard_map/ppermute | solution.py:418
  8.5 0.7 %collective-permute-start = (f32[4,4,8,128]{3,2,1,0:T(8,128)S(1)}, f32[4,4,8,128]{3,2,1,0:T(8,128)S(1)}, u32[]{:S(2)}, u32[]{:S(2)}) collective-permute-start(f32[4,4,8,128]{3,2,1,0:T(8,128)S(1)} %get-tuple-element.26), channel_id=1, source_target_pairs={{1,2},{2,1},{5,6},{6,5},{9,10},{10,9},{13,14},{14,13},{17,18},{18,... | collective-permute-start | bytes 196616 | tf_op jit(solution)/shard_map/ppermute | solution.py:418
  9.1 2.9 %collective-permute-start.1 = (f32[4,4,8,128]{3,2,1,0:T(8,128)S(1)}, f32[4,4,8,128]{3,2,1,0:T(8,128)S(1)}, u32[]{:S(2)}, u32[]{:S(2)}) collective-permute-start(f32[4,4,8,128]{3,2,1,0:T(8,128)S(1)} %get-tuple-element.27), channel_id=1, source_target_pairs={{0,1},{1,0},{2,3},{3,2},{4,5},{5,4},{6,7},{7,6},{8,9},{9,8},{10,11... | collective-permute-start | bytes 196616 | tf_op jit(solution)/shard_map/ppermute | solution.py:418
  12.1 1.3 %shard_map.65 = (f32[3,2,64,128]{3,2,1,0:T(8,128)S(1)}, f32[3,2,64,128]{3,2,1,0:T(8,128)S(1)}, f32[4,4,72,128]{3,2,1,0:T(8,128)S(1)}, f32[4,4,72,128]{3,2,1,0:T(8,128)S(1)}, f32[3,3,3,96,96]{4,3,2,1,0:T(8,128)S(1)}) custom-call(f32[4,4,64,96]{3,2,1,0:T(8,128)S(1)} %get-tuple-element.29.sec_ref, f32[4,4,64,96]{3,2,1,0:T(8,128)S(1)} %get-tuple-element.30.fst_ref, ...), custom_call_target="tpu_custom_call" | custom-call | tf_op jit(solution)/shard_map/pallas_call | solution.py:430
  13.4 0.0 collective-permute-done.rw0
  13.4 0.0 collective-permute-done.1.rw1
  13.4 0.1 shard_map.66
  13.6 0.7 %collective-permute-start.6 = (f32[3,2,64,128]{3,2,1,0:T(8,128)S(1)}, f32[3,2,64,128]{3,2,1,0:T(8,128)S(1)}, u32[]{:S(2)}, u32[]{:S(2)}) collective-permute-start(f32[3,2,64,128]{3,2,1,0:T(8,128)S(1)} %get-tuple-element.44), channel_id=1, source_target_pairs={{4,8},{8,4},{5,9},{9,5},{6,10},{10,6},{7,11},{11,7},{20,24},{24,20... | collective-permute-start | bytes 589832 | tf_op jit(solution)/shard_map/ppermute | solution.py:418
  14.3 1.8 %collective-permute-start.7 = (f32[3,2,64,128]{3,2,1,0:T(8,128)S(1)}, f32[3,2,64,128]{3,2,1,0:T(8,128)S(1)}, u32[]{:S(2)}, u32[]{:S(2)}) collective-permute-start(f32[3,2,64,128]{3,2,1,0:T(8,128)S(1)} %get-tuple-element.45), channel_id=1, source_target_pairs={{0,4},{4,0},{8,12},{12,8},{1,5},{5,1},{9,13},{13,9},{2,6},{6,2},{1... | collective-permute-start | bytes 589832 | tf_op jit(solution)/shard_map/ppermute | solution.py:418
  16.0 0.7 %collective-permute-start.4 = (f32[3,6,8,128]{3,2,1,0:T(8,128)S(1)}, f32[3,6,8,128]{3,2,1,0:T(8,128)S(1)}, u32[]{:S(2)}, u32[]{:S(2)}) collective-permute-start(f32[3,6,8,128]{3,2,1,0:T(8,128)S(1)} %get-tuple-element.38), channel_id=1, source_target_pairs={{4,8},{8,4},{5,9},{9,5},{6,10},{10,6},{7,11},{11,7},{20,24},{24,20... | collective-permute-start | bytes 221192 | tf_op jit(solution)/shard_map/ppermute | solution.py:418
  16.7 0.0 collective-permute-done.4.rc0
  16.7 8.0 %collective-permute-start.5 = (f32[3,6,8,128]{3,2,1,0:T(8,128)S(1)}, f32[3,6,8,128]{3,2,1,0:T(8,128)S(1)}, u32[]{:S(2)}, u32[]{:S(2)}) collective-permute-start(f32[3,6,8,128]{3,2,1,0:T(8,128)S(1)} %get-tuple-element.39), channel_id=1, source_target_pairs={{0,4},{4,0},{8,12},{12,8},{1,5},{5,1},{9,13},{13,9},{2,6},{6,2},{1... | collective-permute-start | bytes 221192 | tf_op jit(solution)/shard_map/ppermute | solution.py:418
  24.7 2.4 %collective-permute-done.5.rc1 = f32[3,6,8,128]{3,2,1,0:T(8,128)S(1)} collective-permute-done((f32[3,6,8,128]{3,2,1,0:T(8,128)S(1)}, f32[3,6,8,128]{3,2,1,0:T(8,128)S(1)}, u32[]{:S(2)}, u32[]{:S(2)}) %collective-permute-start.5) | collective-permute-done | bytes 73760 | tf_op jit(solution)/shard_map/ppermute | solution.py:418
  27.0 0.0 collective-permute-done.2.ra0
  27.0 0.0 collective-permute-done.3.ra1
  27.1 6.1 %shard_map.67 = (f32[4,8,72,128]{3,2,1,0:T(8,128)S(1)}, bf16[5,3,2,128,384]{4,3,2,1,0:T(8,128)(2,1)S(1)}) custom-call(f32[4,4,72,128]{3,2,1,0:T(8,128)S(1)} %get-tuple-element.35.cp_ref, f32[3,4,64,128]{3,2,1,0:T(8,128)S(1)} %collective-permute-done.2.ra0, f32[3,4,64,128]{3,2,1,0:T(8,128)S(1)} %collective-permute-done.3.ra1, ...), custom_call_target="tpu_custom_call" | custom-call | tf_op jit(solution)/shard_map/pallas_call | solution.py:430
  33.1 0.0 collective-permute-done.6.rb0
  33.2 0.0 collective-permute-done.7.rb1
  33.2 9.1 %shard_map.68 = f32[4,4,64,96]{3,2,1,0:T(8,128)} custom-call(f32[4,8,72,128]{3,2,1,0:T(8,128)S(1)} %get-tuple-element.41.g_ref, f32[4,4,72,128]{3,2,1,0:T(8,128)S(1)} %get-tuple-element.42.s2_ref, f32[4,4,72,128]{3,2,1,0:T(8,128)S(1)} %get-tuple-element.43.s1_ref, f32[3,4,64,128]{3,2,1,0:T(8,128)S(1)} %collective-permute-done.2.ra0, ...), custom_call_target="tpu_custom_call" | custom-call | tf_op jit(solution)/shard_map/pallas_call | solution.py:430
Async XLA Ops:
  1.9 25.2 %collective-permute-start.2 = (f32[3,4,64,128]{3,2,1,0:T(8,128)S(1)}, f32[3,4,64,128]{3,2,1,0:T(8,128)S(1)}, u32[]{:S(2)}, u32[]{:S(2)}) collective-permute-start(f32[3,4,64,128]{3,2,1,0:T(8,128)S(1)} %get-tuple-element.36), channel_id=1, source_target_pairs={{4,8},{8,4},{5,9},{9,5},{6,10},{10,6},{7,11},{11,7},{20,24},{24,20... | collective-permute-start | bytes 1179656 | tf_op jit(solution)/shard_map/ppermute | solution.py:418
  2.6 24.5 %collective-permute-start.3 = (f32[3,4,64,128]{3,2,1,0:T(8,128)S(1)}, f32[3,4,64,128]{3,2,1,0:T(8,128)S(1)}, u32[]{:S(2)}, u32[]{:S(2)}) collective-permute-start(f32[3,4,64,128]{3,2,1,0:T(8,128)S(1)} %get-tuple-element.37), channel_id=1, source_target_pairs={{0,4},{4,0},{8,12},{12,8},{1,5},{5,1},{9,13},{13,9},{2,6},{6,2},{1... | collective-permute-start | bytes 1179656 | tf_op jit(solution)/shard_map/ppermute | solution.py:418
  8.5 4.9 %collective-permute-start = (f32[4,4,8,128]{3,2,1,0:T(8,128)S(1)}, f32[4,4,8,128]{3,2,1,0:T(8,128)S(1)}, u32[]{:S(2)}, u32[]{:S(2)}) collective-permute-start(f32[4,4,8,128]{3,2,1,0:T(8,128)S(1)} %get-tuple-element.26), channel_id=1, source_target_pairs={{1,2},{2,1},{5,6},{6,5},{9,10},{10,9},{13,14},{14,13},{17,18},{18,... | collective-permute-start | bytes 196616 | tf_op jit(solution)/shard_map/ppermute | solution.py:418
  9.1 4.3 %collective-permute-start.1 = (f32[4,4,8,128]{3,2,1,0:T(8,128)S(1)}, f32[4,4,8,128]{3,2,1,0:T(8,128)S(1)}, u32[]{:S(2)}, u32[]{:S(2)}) collective-permute-start(f32[4,4,8,128]{3,2,1,0:T(8,128)S(1)} %get-tuple-element.27), channel_id=1, source_target_pairs={{0,1},{1,0},{2,3},{3,2},{4,5},{5,4},{6,7},{7,6},{8,9},{9,8},{10,11... | collective-permute-start | bytes 196616 | tf_op jit(solution)/shard_map/ppermute | solution.py:418
  13.6 19.6 %collective-permute-start.6 = (f32[3,2,64,128]{3,2,1,0:T(8,128)S(1)}, f32[3,2,64,128]{3,2,1,0:T(8,128)S(1)}, u32[]{:S(2)}, u32[]{:S(2)}) collective-permute-start(f32[3,2,64,128]{3,2,1,0:T(8,128)S(1)} %get-tuple-element.44), channel_id=1, source_target_pairs={{4,8},{8,4},{5,9},{9,5},{6,10},{10,6},{7,11},{11,7},{20,24},{24,20... | collective-permute-start | bytes 589832 | tf_op jit(solution)/shard_map/ppermute | solution.py:418
  14.3 18.9 %collective-permute-start.7 = (f32[3,2,64,128]{3,2,1,0:T(8,128)S(1)}, f32[3,2,64,128]{3,2,1,0:T(8,128)S(1)}, u32[]{:S(2)}, u32[]{:S(2)}) collective-permute-start(f32[3,2,64,128]{3,2,1,0:T(8,128)S(1)} %get-tuple-element.45), channel_id=1, source_target_pairs={{0,4},{4,0},{8,12},{12,8},{1,5},{5,1},{9,13},{13,9},{2,6},{6,2},{1... | collective-permute-start | bytes 589832 | tf_op jit(solution)/shard_map/ppermute | solution.py:418
  16.0 0.7 %collective-permute-start.4 = (f32[3,6,8,128]{3,2,1,0:T(8,128)S(1)}, f32[3,6,8,128]{3,2,1,0:T(8,128)S(1)}, u32[]{:S(2)}, u32[]{:S(2)}) collective-permute-start(f32[3,6,8,128]{3,2,1,0:T(8,128)S(1)} %get-tuple-element.38), channel_id=1, source_target_pairs={{4,8},{8,4},{5,9},{9,5},{6,10},{10,6},{7,11},{11,7},{20,24},{24,20... | collective-permute-start | bytes 221192 | tf_op jit(solution)/shard_map/ppermute | solution.py:418
  16.7 10.3 %collective-permute-start.5 = (f32[3,6,8,128]{3,2,1,0:T(8,128)S(1)}, f32[3,6,8,128]{3,2,1,0:T(8,128)S(1)}, u32[]{:S(2)}, u32[]{:S(2)}) collective-permute-start(f32[3,6,8,128]{3,2,1,0:T(8,128)S(1)} %get-tuple-element.39), channel_id=1, source_target_pairs={{0,4},{4,0},{8,12},{12,8},{1,5},{5,1},{9,13},{13,9},{2,6},{6,2},{1... | collective-permute-start | bytes 221192 | tf_op jit(solution)/shard_map/ppermute | solution.py:418

commit v10 on v9

--- a/solution.py
+++ b/solution.py
@@ -124,10 +124,14 @@
         cols_out(wp0, wp1)
 
 
-def slope_kernel(sec_ref, fst_ref, w_hbm, mb0, mb1, s2_ref, s1_ref, w_ref, sem):
+def slope_kernel(wanted, sec_ref, fst_ref, w3_hbm, w2_hbm, w1_hbm, mb0, mb1, s2_ref, s1_ref, u_ref, w2_ref, w1_ref, w_ref, sems):
     frames, rows, cols, chans = sec_ref.shape
-    load = pltpu.make_async_copy(w_hbm, w_ref, sem)
-    load.start()
+    loads = [
+        pltpu.make_async_copy(src, dst, sems.at[n])
+        for n, (src, dst) in enumerate(((w3_hbm, w_ref), (w2_hbm, w2_ref), (w1_hbm, w1_ref)))
+    ]
+    for load in loads:
+        load.start()
     blank = jnp.zeros((cols, LANES), F32)
     for src, ref in ((sec_ref, s2_ref), (fst_ref, s1_ref)):
         for t in range(frames):
@@ -153,7 +157,12 @@
     def _():
         rows_out(mb0, mb1)
 
-    load.wait()
+    loads[0].wait()
+    for k in range(3):
+        for step in prepare(w_ref, u_ref, wanted, k):
+            step()
+    for load in loads[1:]:
+        load.wait()
 
 
 def corner_kernel(chans, rw0, rw1, _c, _s2, _s1, _b0, _b1, mc0, mc1, cp_ref, s2_ref, s1_ref, _mb0, _mb1):
@@ -192,38 +201,26 @@
         out(mc0, mc1)
 
 
-def prepare(w_ref, out_ref, wanted, k, i, which):
+def prepare(w_ref, out_ref, wanted, k):
     chans = w_ref.shape[3]
-    blank = jnp.zeros((chans, LANES - chans), F32)
-    f0, f1, f2 = (jnp.concatenate([w_ref[i, 2 - m, k], blank], 1) for m in range(3))
-    points = {
-        0: lambda: f0 * 0.25,
-        1: lambda: (f0 + f1 + f2) * (-1 / 6),
-        2: lambda: (f1 - f0 - f2) * (1 / 6),
-        3: lambda: f0 * (1 / 24) + f1 * (1 / 12) + f2 * (1 / 6),
-        4: lambda: f0 * (1 / 24) - f1 * (1 / 12) + f2 * (1 / 6),
-        5: lambda: f2,
-    }
-    lanes = pl.ds((2 - i) * LANES, LANES)
-    for n in which:
-        value = points[wanted[n]]()
-        high = value.astype(BF16)
-        out_ref[n, k, 0, 0:chans, lanes] = high
-        out_ref[n, k, 1, 0:chans, lanes] = (value - high.astype(F32)).astype(BF16)
-
-
-def prepare_point(w_ref, out_ref, wanted, n):
-    chans = w_ref.shape[3]
-
-    def clear(k):
-        out_ref[n, k, :, chans:] = jnp.zeros((2, LANES - chans, 3 * LANES), BF16)
-
-    steps = []
-    for k in range(3):
-        steps.append(functools.partial(clear, k))
-        for i in range(3):
-            steps.append(functools.partial(prepare, w_ref, out_ref, wanted, k, i, (n,)))
-    return steps
+
+    def clear():
+        for n in range(len(wanted)):
+            out_ref[n, k, :, chans:] = jnp.zeros((2, LANES - chans, 3 * LANES), BF16)
+
+    def time_tap(i):
+        blank = jnp.zeros((chans, LANES - chans), F32)
+        f0, f1, f2 = (jnp.concatenate([w_ref[i, 2 - m, k], blank], 1) for m in range(3))
+        even, odd = (f0 + f2) * (1 / 6), f1 * (1 / 6)
+        far, odd2 = f0 * (1 / 24) + f2 * (1 / 6), f1 * (1 / 12)
+        points = (f0 * 0.25, -even - odd, odd - even, far + odd2, far - odd2, f2)
+        lanes = pl.ds((2 - i) * LANES, LANES)
+        for n, p in enumerate(wanted):
+            high = points[p].astype(BF16)
+            out_ref[n, k, 0, 0:chans, lanes] = high
+            out_ref[n, k, 1, 0:chans, lanes] = (points[p] - high.astype(F32)).astype(BF16)
+
+    return [clear] + [functools.partial(time_tap, i) for i in range(3)]
 
 
 def spread(steps, slots):
@@ -333,9 +330,7 @@
     return ungroup_frames([jnp.where(parity("ha") == 0, from_even[g, r], from_odd[g, r]) for g in range(3)], chans)
 
 
-def third_kernel(chans, cp_ref, ra0, ra1, rc0, rc1, w3_ref, w2_hbm, out_ref, u2_ref, x_ref, u3_ref, s_ref, y_ref, w2_ref, sem):
-    load = pltpu.make_async_copy(w2_hbm, w2_ref, sem)
-    load.start()
+def third_kernel(chans, cp_ref, ra0, ra1, rc0, rc1, u3_ref, w2_ref, w1_ref, out_ref, u2_ref, u1_ref, x_ref, s_ref, y_ref):
     rows, width = cp_ref.shape[1:3]
     cols = width - SUB
     for r in range(3):
@@ -353,26 +348,15 @@
     def emit(t, o, value):
         out_ref[t, o] = value
 
-    own, later = POINTS[rows], POINTS[(rows + 2) // 2]
-    for step in prepare_point(w3_ref, u3_ref, own, 0):
-        step()
-    slots = len(own) * 2
-    beside = [[] for _ in range(slots)]
-    for p in range(1, len(own)):
-        for n, steps in enumerate(spread(prepare_point(w3_ref, u3_ref, own, p), 2)):
-            beside[2 * p - 2 + n] += steps
-    steps = [load.wait]
-    for n in range(len(later)):
-        steps += prepare_point(w2_ref, u2_ref, later, n)
-    for n, some in enumerate(spread(steps, slots - 2)):
-        beside[n + 2] += some
+    steps = []
+    for k in range(3):
+        steps += prepare(w2_ref, u2_ref, POINTS[(rows + 2) // 2], k) + prepare(w1_ref, u1_ref, POINTS[rows // 2], k)
+    beside = spread(steps, 2 * len(POINTS[rows]))
     conv(read, rows, width, s_ref, y_ref, u3_ref, emit, beside=beside)
 
 
-def last_kernel(chans, g_ref, s2_ref, s1_ref, ra0, ra1, rb0, rb1, rc0, rc1, u2_ref, w1_hbm, out_hbm,
-                e_ref, x1_ref, u1_ref, s_ref, y_ref, w1_ref, stage_ref, load_sem, sems):
-    load = pltpu.make_async_copy(w1_hbm, w1_ref, load_sem)
-    load.start()
+def last_kernel(chans, g_ref, s2_ref, s1_ref, ra0, ra1, rb0, rb1, rc0, rc1, u2_ref, u1_ref, out_hbm,
+                e_ref, x1_ref, s_ref, y_ref, stage_ref, sems):
     frames, rows, width, _ = s2_ref.shape
     cols = width - SUB
     for side, (even, odd) in enumerate(((1, 0), (0, 1))):
@@ -400,11 +384,7 @@
         return pltpu.make_async_copy(stage_ref.at[t], out_hbm.at[t], sems.at[t])
 
     size2, size1 = (rows + 2) // 2, rows // 2
-    steps = [load.wait]
-    for n in range(len(POINTS[size1])):
-        steps += prepare_point(w1_ref, u1_ref, POINTS[size1], n)
-    beside = [[], []] + spread(steps, 2 * len(POINTS[size2]) - 2)
-    conv(lambda t, r, at: g_ref[t, r, at] * slope2(t, r, at), size2, width, s_ref, y_ref, u2_ref, emit2, beside=beside)
+    conv(lambda t, r, at: g_ref[t, r, at] * slope2(t, r, at), size2, width, s_ref, y_ref, u2_ref, emit2)
     conv(lambda t, r, at: x1_ref[t, r, at], size1, width, s_ref, y_ref, u1_ref, emit1, lambda t: copy_out(t).start())
     for t in range(frames):
         copy_out(t).wait()
@@ -471,12 +451,12 @@
         return arr(len(POINTS[size]), 3, 2, LANES, 3 * LANES, dtype=BF16)
 
     size3, size2, size1 = rows, (rows + 2) // 2, rows // 2
-    mb0, mb1, s2, s1, third = call(
-        slope_kernel,
-        (rows_b,) * 2 + (own,) * 2 + (arr(*third.shape),),
-        (sec, fst, third),
-        [pltpu.SemaphoreType.DMA],
-        hbm=(2,),
+    mb0, mb1, s2, s1, u3, second, first = call(
+        functools.partial(slope_kernel, POINTS[size3]),
+        (rows_b,) * 2 + (own,) * 2 + (weights(size3), arr(*second.shape), arr(*first.shape)),
+        (sec, fst, third, second, first),
+        [vmem(*third.shape), pltpu.SemaphoreType.DMA((3,))],
+        hbm=(2, 3, 4),
     )
     mc0, mc1, cp, s2, s1, mb0, mb1 = call(
         functools.partial(corner_kernel, chans),
@@ -494,32 +474,19 @@
             vmem(2, points, 2, width, 2 * LANES),
         ]
 
-    grad, u2 = call(
+    grad, u2, u1 = call(
         functools.partial(third_kernel, chans),
-        (arr(frames, rows + 4, width, LANES), weights(size2)),
-        (cp, ra0, ra1, rc0, rc1, third, second),
-        [vmem(frames, 6, width, LANES), vmem(*weights(size3).shape, dtype=BF16)]
-        + scratch(size3)
-        + [vmem(*second.shape), pltpu.SemaphoreType.DMA],
-        hbm=(6,),
+        (arr(frames, rows + 4, width, LANES), weights(size2), weights(size1)),
+        (cp, ra0, ra1, rc0, rc1, u3, second, first),
+        [vmem(frames, 6, width, LANES)] + scratch(size3),
     )
     return call(
         functools.partial(last_kernel, chans),
         arr(frames, rows, cols, chans),
-        (grad, s2, s1, ra0, ra1, rb0, rb1, rc0, rc1, u2, first),
-        [
-            vmem(2, 3, frames, width, LANES),
-            vmem(frames, rows + 2, width, LANES),
-            vmem(*weights(size1).shape, dtype=BF16),
-        ]
+        (grad, s2, s1, ra0, ra1, rb0, rb1, rc0, rc1, u2, u1),
+        [vmem(2, 3, frames, width, LANES), vmem(frames, rows + 2, width, LANES)]
         + scratch(size2)
-        + [
-            vmem(*first.shape),
-            vmem(frames, rows, cols, chans),
-            pltpu.SemaphoreType.DMA,
-            pltpu.SemaphoreType.DMA((frames,)),
-        ],
-        hbm=(10,),
+        + [vmem(frames, rows, cols, chans), pltpu.SemaphoreType.DMA((frames,))],
         hbm_out=True,
     )
 

time: 42.5 us -> 41.4 us (0.974)
  starting transfers between devices: 21.2 us -> 20.5 us
    ppermute x8, starting transfers between devices: 21.2 us -> 20.5 us  [swap(): return lax.ppermute(value, axis, pairs)]
  transfers between devices with their start and end apart: 8 -> 8, of which waited for: 1 -> 1; matrix products, arithmetic and copies ran while one was open for 0% -> 0% of each run, Pallas kernels for 18% -> 19%
where the time goes in v10:
time: 41.4 us; the launch traced here: 41.2 us
  starting transfers between devices  20.5 us (50%)
  Pallas kernels  18.1 us (44%)
  waiting for transfers between devices  2.35 us (6%)
    ppermute x8, starting transfers between devices, swap(): return lax.ppermute(value, axis, pairs)  20.5 us
    pallas_call x5, Pallas kernels, call(): pl.pallas_call(body, out_shape=out_shape, in_specs=[HBM_SPEC if n in hbm...  18.1 us
    ppermute x8, waiting for transfers between devices, swap(): return lax.ppermute(value, axis, pairs)  2.35 us
  transfers between devices with their start and end apart: 8, of which 1 were waited for; matrix products, arithmetic and copies ran while one was open for 0% of the time, Pallas kernels for 19%

profile of v10, /device:TPU:0, one launch (start us, length us, event | category | flops | bytes accessed | tf_op | source)
XLA Modules:
  0.0 41.2 jit_solution(5974524366634209468)
XLA Ops:
  0.0 1.9 %shard_map.64 = (f32[3,4,64,128]{3,2,1,0:T(8,128)S(1)}, f32[3,4,64,128]{3,2,1,0:T(8,128)S(1)}, f32[4,4,8,128]{3,2,1,0:T(8,128)S(1)}, f32[4,4,8,128]{3,2,1,0:T(8,...) custom-call(f32[4,4,64,96]{3,2,1,0:T(8,128)} %cot_hbm.1, ...), custom_call_target="tpu_custom_call" | custom-call | tf_op jit(solution)/shard_map/pallas_call | solution.py:410
  1.9 0.7 %collective-permute-start.2 = (f32[3,4,64,128]{3,2,1,0:T(8,128)S(1)}, f32[3,4,64,128]{3,2,1,0:T(8,128)S(1)}, u32[]{:S(2)}, u32[]{:S(2)}) collective-permute-start(f32[3,4,64,128]{3,2,1,0:T(8,128)S(1)} %get-tuple-element.39), channel_id=1, source_target_pairs={{4,8},{8,4},{5,9},{9,5},{6,10},{10,6},{7,11},{11,7},{20,24},{24,20... | collective-permute-start | bytes 1179656 | tf_op jit(solution)/shard_map/ppermute | solution.py:398
  2.6 5.9 %collective-permute-start.3 = (f32[3,4,64,128]{3,2,1,0:T(8,128)S(1)}, f32[3,4,64,128]{3,2,1,0:T(8,128)S(1)}, u32[]{:S(2)}, u32[]{:S(2)}) collective-permute-start(f32[3,4,64,128]{3,2,1,0:T(8,128)S(1)} %get-tuple-element.40), channel_id=1, source_target_pairs={{0,4},{4,0},{8,12},{12,8},{1,5},{5,1},{9,13},{13,9},{2,6},{6,2},{1... | collective-permute-start | bytes 1179656 | tf_op jit(solution)/shard_map/ppermute | solution.py:398
  8.5 0.7 %collective-permute-start = (f32[4,4,8,128]{3,2,1,0:T(8,128)S(1)}, f32[4,4,8,128]{3,2,1,0:T(8,128)S(1)}, u32[]{:S(2)}, u32[]{:S(2)}) collective-permute-start(f32[4,4,8,128]{3,2,1,0:T(8,128)S(1)} %get-tuple-element.29), channel_id=1, source_target_pairs={{1,2},{2,1},{5,6},{6,5},{9,10},{10,9},{13,14},{14,13},{17,18},{18,... | collective-permute-start | bytes 196616 | tf_op jit(solution)/shard_map/ppermute | solution.py:398
  9.1 2.9 %collective-permute-start.1 = (f32[4,4,8,128]{3,2,1,0:T(8,128)S(1)}, f32[4,4,8,128]{3,2,1,0:T(8,128)S(1)}, u32[]{:S(2)}, u32[]{:S(2)}) collective-permute-start(f32[4,4,8,128]{3,2,1,0:T(8,128)S(1)} %get-tuple-element.30), channel_id=1, source_target_pairs={{0,1},{1,0},{2,3},{3,2},{4,5},{5,4},{6,7},{7,6},{8,9},{9,8},{10,11... | collective-permute-start | bytes 196616 | tf_op jit(solution)/shard_map/ppermute | solution.py:398
  12.1 2.1 %shard_map.65 = (f32[3,2,64,128]{3,2,1,0:T(8,128)S(1)}, f32[3,2,64,128]{3,2,1,0:T(8,128)S(1)}, f32[4,4,72,128]{3,2,1,0:T(8,128)S(1)}, f32[4,4,72,128]{3,2,1,0:T(...) custom-call(f32[4,4,64,96]{3,2,1,0:T(8,128)S(1)} %get-tuple-element., ...), custom_call_target="tpu_custom_call" | custom-call | tf_op jit(solution)/shard_map/pallas_call | solution.py:410
  14.2 0.0 collective-permute-done.rw0
  14.2 0.0 collective-permute-done.1.rw1
  14.2 0.1 shard_map.66
  14.4 0.7 %collective-permute-start.6 = (f32[3,2,64,128]{3,2,1,0:T(8,128)S(1)}, f32[3,2,64,128]{3,2,1,0:T(8,128)S(1)}, u32[]{:S(2)}, u32[]{:S(2)}) collective-permute-start(f32[3,2,64,128]{3,2,1,0:T(8,128)S(1)} %get-tuple-element.49), channel_id=1, source_target_pairs={{4,8},{8,4},{5,9},{9,5},{6,10},{10,6},{7,11},{11,7},{20,24},{24,20... | collective-permute-start | bytes 589832 | tf_op jit(solution)/shard_map/ppermute | solution.py:398
  15.1 1.8 %collective-permute-start.7 = (f32[3,2,64,128]{3,2,1,0:T(8,128)S(1)}, f32[3,2,64,128]{3,2,1,0:T(8,128)S(1)}, u32[]{:S(2)}, u32[]{:S(2)}) collective-permute-start(f32[3,2,64,128]{3,2,1,0:T(8,128)S(1)} %get-tuple-element.50), channel_id=1, source_target_pairs={{0,4},{4,0},{8,12},{12,8},{1,5},{5,1},{9,13},{13,9},{2,6},{6,2},{1... | collective-permute-start | bytes 589832 | tf_op jit(solution)/shard_map/ppermute | solution.py:398
  16.8 0.8 %collective-permute-start.4 = (f32[3,6,8,128]{3,2,1,0:T(8,128)S(1)}, f32[3,6,8,128]{3,2,1,0:T(8,128)S(1)}, u32[]{:S(2)}, u32[]{:S(2)}) collective-permute-start(f32[3,6,8,128]{3,2,1,0:T(8,128)S(1)} %get-tuple-element.41), channel_id=1, source_target_pairs={{4,8},{8,4},{5,9},{9,5},{6,10},{10,6},{7,11},{11,7},{20,24},{24,20... | collective-permute-start | bytes 221192 | tf_op jit(solution)/shard_map/ppermute | solution.py:398
  17.7 0.0 collective-permute-done.4.rc0
  17.7 7.0 %collective-permute-start.5 = (f32[3,6,8,128]{3,2,1,0:T(8,128)S(1)}, f32[3,6,8,128]{3,2,1,0:T(8,128)S(1)}, u32[]{:S(2)}, u32[]{:S(2)}) collective-permute-start(f32[3,6,8,128]{3,2,1,0:T(8,128)S(1)} %get-tuple-element.42), channel_id=1, source_target_pairs={{0,4},{4,0},{8,12},{12,8},{1,5},{5,1},{9,13},{13,9},{2,6},{6,2},{1... | collective-permute-start | bytes 221192 | tf_op jit(solution)/shard_map/ppermute | solution.py:398
  24.7 2.3 %collective-permute-done.5.rc1 = f32[3,6,8,128]{3,2,1,0:T(8,128)S(1)} collective-permute-done((f32[3,6,8,128]{3,2,1,0:T(8,128)S(1)}, f32[3,6,8,128]{3,2,1,0:T(8,128)S(1)}, u32[]{:S(2)}, u32[]{:S(2)}) %collective-permute-start.5) | collective-permute-done | bytes 73760 | tf_op jit(solution)/shard_map/ppermute | solution.py:398
  27.0 0.0 collective-permute-done.2.ra0
  27.1 0.0 collective-permute-done.3.ra1
  27.1 5.5 %shard_map.67 = (f32[4,8,72,128]{3,2,1,0:T(8,128)S(1)}, bf16[5,3,2,128,384]{4,3,2,1,0:T(8,128)(2,1)S(1)}, bf16[4,3,2,128,384]{4,3,2,1,0:T(8,128)(2,1)S(1)}) custom-call(f32[4,4,72,128]{3,2,1,0:T(8,128)S(1)} %get-tuple-element.38.cp_ref, f32[3,4,64,128]{3,2,1,0:T(8,128)S(1)} %collective-permute-done.2.ra0, f32[3,4,64,128]{3,2,1,0:T(8,128)S(1)} %collective-permute-done.3.ra1, ...), custom_call_target="tpu_custom_call" | custom-call | tf_op jit(solution)/shard_map/pallas_call | solution.py:410
  32.6 0.0 collective-permute-done.6.rb0
  32.6 0.0 collective-permute-done.7.rb1
  32.6 8.4 %shard_map.68 = f32[4,4,64,96]{3,2,1,0:T(8,128)} custom-call(f32[4,8,72,128]{3,2,1,0:T(8,128)S(1)} %get-tuple-element.46.g_ref, f32[4,4,72,128]{3,2,1,0:T(8,128)S(1)} %get-tuple-element.47.s2_ref, f32[4,4,72,128]{3,2,1,0:T(8,128)S(1)} %get-tuple-element.48.s1_ref, f32[3,4,64,128]{3,2,1,0:T(8,128)S(1)} %collective-permute-done.2.ra0, ...), custom_call_target="tpu_custom_call" | custom-call | tf_op jit(solution)/shard_map/pallas_call | solution.py:410
Async XLA Ops:
  1.9 25.2 %collective-permute-start.2 = (f32[3,4,64,128]{3,2,1,0:T(8,128)S(1)}, f32[3,4,64,128]{3,2,1,0:T(8,128)S(1)}, u32[]{:S(2)}, u32[]{:S(2)}) collective-permute-start(f32[3,4,64,128]{3,2,1,0:T(8,128)S(1)} %get-tuple-element.39), channel_id=1, source_target_pairs={{4,8},{8,4},{5,9},{9,5},{6,10},{10,6},{7,11},{11,7},{20,24},{24,20... | collective-permute-start | bytes 1179656 | tf_op jit(solution)/shard_map/ppermute | solution.py:398
  2.6 24.5 %collective-permute-start.3 = (f32[3,4,64,128]{3,2,1,0:T(8,128)S(1)}, f32[3,4,64,128]{3,2,1,0:T(8,128)S(1)}, u32[]{:S(2)}, u32[]{:S(2)}) collective-permute-start(f32[3,4,64,128]{3,2,1,0:T(8,128)S(1)} %get-tuple-element.40), channel_id=1, source_target_pairs={{0,4},{4,0},{8,12},{12,8},{1,5},{5,1},{9,13},{13,9},{2,6},{6,2},{1... | collective-permute-start | bytes 1179656 | tf_op jit(solution)/shard_map/ppermute | solution.py:398
  8.5 5.7 %collective-permute-start = (f32[4,4,8,128]{3,2,1,0:T(8,128)S(1)}, f32[4,4,8,128]{3,2,1,0:T(8,128)S(1)}, u32[]{:S(2)}, u32[]{:S(2)}) collective-permute-start(f32[4,4,8,128]{3,2,1,0:T(8,128)S(1)} %get-tuple-element.29), channel_id=1, source_target_pairs={{1,2},{2,1},{5,6},{6,5},{9,10},{10,9},{13,14},{14,13},{17,18},{18,... | collective-permute-start | bytes 196616 | tf_op jit(solution)/shard_map/ppermute | solution.py:398
  9.1 5.1 %collective-permute-start.1 = (f32[4,4,8,128]{3,2,1,0:T(8,128)S(1)}, f32[4,4,8,128]{3,2,1,0:T(8,128)S(1)}, u32[]{:S(2)}, u32[]{:S(2)}) collective-permute-start(f32[4,4,8,128]{3,2,1,0:T(8,128)S(1)} %get-tuple-element.30), channel_id=1, source_target_pairs={{0,1},{1,0},{2,3},{3,2},{4,5},{5,4},{6,7},{7,6},{8,9},{9,8},{10,11... | collective-permute-start | bytes 196616 | tf_op jit(solution)/shard_map/ppermute | solution.py:398
  14.4 18.2 %collective-permute-start.6 = (f32[3,2,64,128]{3,2,1,0:T(8,128)S(1)}, f32[3,2,64,128]{3,2,1,0:T(8,128)S(1)}, u32[]{:S(2)}, u32[]{:S(2)}) collective-permute-start(f32[3,2,64,128]{3,2,1,0:T(8,128)S(1)} %get-tuple-element.49), channel_id=1, source_target_pairs={{4,8},{8,4},{5,9},{9,5},{6,10},{10,6},{7,11},{11,7},{20,24},{24,20... | collective-permute-start | bytes 589832 | tf_op jit(solution)/shard_map/ppermute | solution.py:398
  15.1 17.5 %collective-permute-start.7 = (f32[3,2,64,128]{3,2,1,0:T(8,128)S(1)}, f32[3,2,64,128]{3,2,1,0:T(8,128)S(1)}, u32[]{:S(2)}, u32[]{:S(2)}) collective-permute-start(f32[3,2,64,128]{3,2,1,0:T(8,128)S(1)} %get-tuple-element.50), channel_id=1, source_target_pairs={{0,4},{4,0},{8,12},{12,8},{1,5},{5,1},{9,13},{13,9},{2,6},{6,2},{1... | collective-permute-start | bytes 589832 | tf_op jit(solution)/shard_map/ppermute | solution.py:398
  16.8 0.8 %collective-permute-start.4 = (f32[3,6,8,128]{3,2,1,0:T(8,128)S(1)}, f32[3,6,8,128]{3,2,1,0:T(8,128)S(1)}, u32[]{:S(2)}, u32[]{:S(2)}) collective-permute-start(f32[3,6,8,128]{3,2,1,0:T(8,128)S(1)} %get-tuple-element.41), channel_id=1, source_target_pairs={{4,8},{8,4},{5,9},{9,5},{6,10},{10,6},{7,11},{11,7},{20,24},{24,20... | collective-permute-start | bytes 221192 | tf_op jit(solution)/shard_map/ppermute | solution.py:398
  17.7 9.4 %collective-permute-start.5 = (f32[3,6,8,128]{3,2,1,0:T(8,128)S(1)}, f32[3,6,8,128]{3,2,1,0:T(8,128)S(1)}, u32[]{:S(2)}, u32[]{:S(2)}) collective-permute-start(f32[3,6,8,128]{3,2,1,0:T(8,128)S(1)} %get-tuple-element.42), channel_id=1, source_target_pairs={{0,4},{4,0},{8,12},{12,8},{1,5},{5,1},{9,13},{13,9},{2,6},{6,2},{1... | collective-permute-start | bytes 221192 | tf_op jit(solution)/shard_map/ppermute | solution.py:398

commit v11 on v10

--- a/solution.py
+++ b/solution.py
@@ -230,21 +230,30 @@
 POINTS = {2: (0, 1, 2, 5), 3: (0, 1, 2, 3, 5), 4: (0, 1, 2, 3, 4, 5)}
 
 
-def transform(x, size):
+def transform(x, size, p):
     if size == 2:
-        return 4.0 * (x[0] - x[2]), -3.0 * (x[1] + x[2]), 3.0 * (x[1] - x[2]), x[3] - x[1]
+        return (
+            lambda: 4.0 * (x(0) - x(2)),
+            lambda: -3.0 * (x(1) + x(2)),
+            lambda: 3.0 * (x(1) - x(2)),
+            lambda: x(3) - x(1),
+        )[p]()
     if size == 3:
-        a, b = x[3] - x[1], x[3] - 2.0 * x[1]
         return (
-            4.0 * (x[0] - x[2]) + 2.0 * a,
-            3.0 * (b - x[2]),
-            2.0 * x[1] - 3.0 * x[2] + x[3],
-            4.0 * a,
-            x[4] - x[2] - 2.0 * a,
-        )
-    a, b = x[4] - 4.0 * x[2], x[3] - 4.0 * x[1]
-    c, e = x[4] - x[2], 2.0 * (x[3] - x[1])
-    return 4.0 * x[0] - 5.0 * x[2] + x[4], a + b, a - b, c + e, c - e, 4.0 * x[1] - 5.0 * x[3] + x[5]
+            lambda: 4.0 * (x(0) - x(2)) + 2.0 * (x(3) - x(1)),
+            lambda: 3.0 * (x(3) - 2.0 * x(1) - x(2)),
+            lambda: 2.0 * x(1) - 3.0 * x(2) + x(3),
+            lambda: 4.0 * (x(3) - x(1)),
+            lambda: x(4) - x(2) - 2.0 * (x(3) - x(1)),
+        )[p]()
+    return (
+        lambda: 4.0 * x(0) - 5.0 * x(2) + x(4),
+        lambda: x(4) - 4.0 * x(2) + (x(3) - 4.0 * x(1)),
+        lambda: x(4) - 4.0 * x(2) - (x(3) - 4.0 * x(1)),
+        lambda: x(4) - x(2) + 2.0 * (x(3) - x(1)),
+        lambda: x(4) - x(2) - 2.0 * (x(3) - x(1)),
+        lambda: 4.0 * x(1) - 5.0 * x(3) + x(5),
+    )[p]()
 
 
 def outputs(y, size):
@@ -287,19 +296,24 @@
     chunks = width // SUB
     points = len(POINTS[size])
 
-    def one(c, carry):
-        at = pl.ds(pl.multiple_of(c * SUB, SUB), SUB)
+    def fill(p, at, blocks):
         for t in range(4):
             pair, a = t // 2, t % 2
-            x = [read(t, r, at) for r in range(2 * size + 2)]
-            for p, pieces in enumerate(zip(transform(x[: size + 2], size), transform(x[size:], size))):
-                value = jnp.concatenate(pieces, 0)
-                high = value.astype(BF16)
-                s_ref[p, c, pair, :, a * LANES : (a + 1) * LANES] = high
-                s_ref[p, c, pair, :, (2 + a) * LANES : (3 + a) * LANES] = (value - high.astype(F32)).astype(BF16)
+            tiles = []
+            for base in (0, size):
+                value = transform(lambda r: read(t, base + r, at), size, p)
+                tiles.append(value.reshape(-1, 1, SUB, LANES))
+            value = jnp.concatenate(tiles, 1).reshape(-1, 2 * SUB, LANES)
+            high = value.astype(BF16)
+            s_ref[p, blocks, pair, :, a * LANES : (a + 1) * LANES] = high
+            s_ref[p, blocks, pair, :, (2 + a) * LANES : (3 + a) * LANES] = (value - high.astype(F32)).astype(BF16)
+
+    def first(c, carry):
+        fill(0, pl.ds(pl.multiple_of(c * SUB, SUB), SUB), pl.ds(c, 1))
         return carry
 
-    lax.fori_loop(0, chunks, one, 0)
+    lax.fori_loop(0, chunks, first, 0)
+
     wide = 4 * LANES
 
     def other_work(n):
@@ -309,6 +323,8 @@
     for p in range(points):
         near, far = right_operands(w_ref, p)
         own = product(s_ref[p].reshape(chunks * 4 * SUB, wide), near).reshape(chunks, 2, 2, SUB, 6 * LANES)
+        if p + 1 < points:
+            fill(p + 1, slice(0, width), slice(0, chunks))
         other_work(2 * p)
         later = product(s_ref[p, :, 1].reshape(chunks * 2 * SUB, wide), far).reshape(chunks, 2, SUB, 6 * LANES)
         other_work(2 * p + 1)
@@ -330,7 +346,7 @@
     return ungroup_frames([jnp.where(parity("ha") == 0, from_even[g, r], from_odd[g, r]) for g in range(3)], chans)
 
 
-def third_kernel(chans, cp_ref, ra0, ra1, rc0, rc1, u3_ref, w2_ref, w1_ref, out_ref, u2_ref, u1_ref, x_ref, s_ref, y_ref):
+def third_kernel(chans, cp_ref, s2_ref, ra0, ra1, rc0, rc1, u3_ref, w2_ref, w1_ref, out_ref, u2_ref, u1_ref, x_ref, s_ref, y_ref):
     rows, width = cp_ref.shape[1:3]
     cols = width - SUB
     for r in range(3):
@@ -346,7 +362,7 @@
         return x_ref[t, r if r < 3 else r - rows, at]
 
     def emit(t, o, value):
-        out_ref[t, o] = value
+        out_ref[t, o] = value * s2_ref[t, o - 2] if 2 <= o < 2 + rows else value
 
     steps = []
     for k in range(3):
@@ -355,9 +371,9 @@
     conv(read, rows, width, s_ref, y_ref, u3_ref, emit, beside=beside)
 
 
-def last_kernel(chans, g_ref, s2_ref, s1_ref, ra0, ra1, rb0, rb1, rc0, rc1, u2_ref, u1_ref, out_hbm,
+def last_kernel(chans, g_ref, s1_ref, ra0, ra1, rb0, rb1, rc0, rc1, u2_ref, u1_ref, out_hbm,
                 e_ref, x1_ref, s_ref, y_ref, stage_ref, sems):
-    frames, rows, width, _ = s2_ref.shape
+    frames, rows, width, _ = s1_ref.shape
     cols = width - SUB
     for side, (even, odd) in enumerate(((1, 0), (0, 1))):
         for r in range(3):
@@ -368,9 +384,13 @@
             for t, frame in enumerate(halo_rows(chans, corners[even], corners[odd], 3 + r)):
                 e_ref[side, r, t, cols:] = frame
 
-    def slope2(t, r, at):
+        for t in range(frames):
+            for r in range(2):
+                e_ref[side, r, t] = e_ref[side, r, t] * g_ref[t, r + side * (rows + 2)]
+
+    def read2(t, r, at):
         if 2 <= r < 2 + rows:
-            return s2_ref[t, r - 2, at]
+            return g_ref[t, r, at]
         return e_ref[0, r, t, at] if r < 2 else e_ref[1, r - 2 - rows, t, at]
 
     def emit2(t, o, value):
@@ -384,7 +404,7 @@
         return pltpu.make_async_copy(stage_ref.at[t], out_hbm.at[t], sems.at[t])
 
     size2, size1 = (rows + 2) // 2, rows // 2
-    conv(lambda t, r, at: g_ref[t, r, at] * slope2(t, r, at), size2, width, s_ref, y_ref, u2_ref, emit2)
+    conv(read2, size2, width, s_ref, y_ref, u2_ref, emit2)
     conv(lambda t, r, at: x1_ref[t, r, at], size1, width, s_ref, y_ref, u1_ref, emit1, lambda t: copy_out(t).start())
     for t in range(frames):
         copy_out(t).wait()
@@ -477,13 +497,13 @@
     grad, u2, u1 = call(
         functools.partial(third_kernel, chans),
         (arr(frames, rows + 4, width, LANES), weights(size2), weights(size1)),
-        (cp, ra0, ra1, rc0, rc1, u3, second, first),
+        (cp, s2, ra0, ra1, rc0, rc1, u3, second, first),
         [vmem(frames, 6, width, LANES)] + scratch(size3),
     )
     return call(
         functools.partial(last_kernel, chans),
         arr(frames, rows, cols, chans),
-        (grad, s2, s1, ra0, ra1, rb0, rb1, rc0, rc1, u2, u1),
+        (grad, s1, ra0, ra1, rb0, rb1, rc0, rc1, u2, u1),
         [vmem(2, 3, frames, width, LANES), vmem(frames, rows + 2, width, LANES)]
         + scratch(size2)
         + [vmem(frames, rows, cols, chans), pltpu.SemaphoreType.DMA((frames,))],

time: 41.4 us -> 44.5 us (1.075)
  local copies, waits for them, and re-layouts: 0 us -> 1.74 us
  Pallas kernels: 18.1 us -> 19.4 us
    unnamed x0 -> x2, local copies, waits for them, and re-layouts: none -> 1.74 us
    pallas_call x5, Pallas kernels: 18.1 us -> 19.4 us  [call(): pl.pallas_call(body, out_shape=out_shape, in_specs=[HBM_SPEC if n in hbm...]
  transfers between devices with their start and end apart: 8 -> 8, of which waited for: 1 -> 1; matrix products, arithmetic and copies ran while one was open for 0% -> 0% of each run, Pallas kernels for 19% -> 22%
where the time goes in v11:
time: 44.5 us; the launch traced here: 44.3 us
  starting transfers between devices  20.5 us (46%)
  Pallas kernels  19.4 us (44%)
  waiting for transfers between devices  2.35 us (5%)
  local copies, waits for them, and re-layouts  1.74 us (4%)
    ppermute x8, starting transfers between devices, swap(): return lax.ppermute(value, axis, pairs)  20.5 us
    pallas_call x5, Pallas kernels, call(): pl.pallas_call(body, out_shape=out_shape, in_specs=[HBM_SPEC if n in hbm...  19.4 us
    ppermute x8, waiting for transfers between devices, swap(): return lax.ppermute(value, axis, pairs)  2.35 us
    unnamed x2, local copies, waits for them, and re-layouts  1.74 us
  transfers between devices with their start and end apart: 8, of which 1 were waited for; matrix products, arithmetic and copies ran while one was open for 0% of the time, Pallas kernels for 22%

profile of v11, /device:TPU:0, one launch (start us, length us, event | category | flops | bytes accessed | tf_op | source)
XLA Modules:
  0.0 44.3 jit_solution(17128704010511210624)
XLA Ops:
  0.0 1.9 %shard_map.64 = (f32[3,4,64,128]{3,2,1,0:T(8,128)S(1)}, f32[3,4,64,128]{3,2,1,0:T(8,128)S(1)}, f32[4,4,8,128]{3,2,1,0:T(8,128)S(1)}, f32[4,4,8,128]{3,2,1,0:T(8,...) custom-call(f32[4,4,64,96]{3,2,1,0:T(8,128)} %cot_hbm.1, ...), custom_call_target="tpu_custom_call" | custom-call | tf_op jit(solution)/shard_map/pallas_call | solution.py:430
  1.9 0.7 %collective-permute-start.2 = (f32[3,4,64,128]{3,2,1,0:T(8,128)S(1)}, f32[3,4,64,128]{3,2,1,0:T(8,128)S(1)}, u32[]{:S(2)}, u32[]{:S(2)}) collective-permute-start(f32[3,4,64,128]{3,2,1,0:T(8,128)S(1)} %get-tuple-element.40), channel_id=1, source_target_pairs={{4,8},{8,4},{5,9},{9,5},{6,10},{10,6},{7,11},{11,7},{20,24},{24,20... | collective-permute-start | bytes 1179656 | tf_op jit(solution)/shard_map/ppermute | solution.py:418
  2.6 5.9 %collective-permute-start.3 = (f32[3,4,64,128]{3,2,1,0:T(8,128)S(1)}, f32[3,4,64,128]{3,2,1,0:T(8,128)S(1)}, u32[]{:S(2)}, u32[]{:S(2)}) collective-permute-start(f32[3,4,64,128]{3,2,1,0:T(8,128)S(1)} %get-tuple-element.41), channel_id=1, source_target_pairs={{0,4},{4,0},{8,12},{12,8},{1,5},{5,1},{9,13},{13,9},{2,6},{6,2},{1... | collective-permute-start | bytes 1179656 | tf_op jit(solution)/shard_map/ppermute | solution.py:418
  8.5 0.7 %collective-permute-start = (f32[4,4,8,128]{3,2,1,0:T(8,128)S(1)}, f32[4,4,8,128]{3,2,1,0:T(8,128)S(1)}, u32[]{:S(2)}, u32[]{:S(2)}) collective-permute-start(f32[4,4,8,128]{3,2,1,0:T(8,128)S(1)} %get-tuple-element.29), channel_id=1, source_target_pairs={{1,2},{2,1},{5,6},{6,5},{9,10},{10,9},{13,14},{14,13},{17,18},{18,... | collective-permute-start | bytes 196616 | tf_op jit(solution)/shard_map/ppermute | solution.py:418
  9.1 2.9 %collective-permute-start.1 = (f32[4,4,8,128]{3,2,1,0:T(8,128)S(1)}, f32[4,4,8,128]{3,2,1,0:T(8,128)S(1)}, u32[]{:S(2)}, u32[]{:S(2)}) collective-permute-start(f32[4,4,8,128]{3,2,1,0:T(8,128)S(1)} %get-tuple-element.30), channel_id=1, source_target_pairs={{0,1},{1,0},{2,3},{3,2},{4,5},{5,4},{6,7},{7,6},{8,9},{9,8},{10,11... | collective-permute-start | bytes 196616 | tf_op jit(solution)/shard_map/ppermute | solution.py:418
  12.1 2.1 %shard_map.65 = (f32[3,2,64,128]{3,2,1,0:T(8,128)S(1)}, f32[3,2,64,128]{3,2,1,0:T(8,128)S(1)}, f32[4,4,72,128]{3,2,1,0:T(8,128)S(1)}, f32[4,4,72,128]{3,2,1,0:T(...) custom-call(f32[4,4,64,96]{3,2,1,0:T(8,128)S(1)} %get-tuple-element., ...), custom_call_target="tpu_custom_call" | custom-call | tf_op jit(solution)/shard_map/pallas_call | solution.py:430
  14.2 0.0 copy-start
  14.2 1.7 %copy-done = bf16[6,3,2,128,384]{4,3,2,1,0:T(8,128)(2,1)} copy-done((bf16[6,3,2,128,384]{4,3,2,1,0:T(8,128)(2,1)}, bf16[6,3,2,128,384]{4,3,2,1,0:T(8,128)(2,1)S(1)}, u32[]{:S(2)}) %copy-start) | copy-done | bytes 3538968
  16.0 0.0 collective-permute-done.rw0
  16.0 0.0 collective-permute-done.1.rw1
  16.0 0.1 shard_map.66
  16.1 0.7 %collective-permute-start.6 = (f32[3,2,64,128]{3,2,1,0:T(8,128)S(1)}, f32[3,2,64,128]{3,2,1,0:T(8,128)S(1)}, u32[]{:S(2)}, u32[]{:S(2)}) collective-permute-start(f32[3,2,64,128]{3,2,1,0:T(8,128)S(1)} %get-tuple-element.49), channel_id=1, source_target_pairs={{4,8},{8,4},{5,9},{9,5},{6,10},{10,6},{7,11},{11,7},{20,24},{24,20... | collective-permute-start | bytes 589832 | tf_op jit(solution)/shard_map/ppermute | solution.py:418
  16.8 1.8 %collective-permute-start.7 = (f32[3,2,64,128]{3,2,1,0:T(8,128)S(1)}, f32[3,2,64,128]{3,2,1,0:T(8,128)S(1)}, u32[]{:S(2)}, u32[]{:S(2)}) collective-permute-start(f32[3,2,64,128]{3,2,1,0:T(8,128)S(1)} %get-tuple-element.50), channel_id=1, source_target_pairs={{0,4},{4,0},{8,12},{12,8},{1,5},{5,1},{9,13},{13,9},{2,6},{6,2},{1... | collective-permute-start | bytes 589832 | tf_op jit(solution)/shard_map/ppermute | solution.py:418
  18.6 0.8 %collective-permute-start.4 = (f32[3,6,8,128]{3,2,1,0:T(8,128)S(1)}, f32[3,6,8,128]{3,2,1,0:T(8,128)S(1)}, u32[]{:S(2)}, u32[]{:S(2)}) collective-permute-start(f32[3,6,8,128]{3,2,1,0:T(8,128)S(1)} %get-tuple-element.42), channel_id=1, source_target_pairs={{4,8},{8,4},{5,9},{9,5},{6,10},{10,6},{7,11},{11,7},{20,24},{24,20... | collective-permute-start | bytes 221192 | tf_op jit(solution)/shard_map/ppermute | solution.py:418
  19.4 0.0 collective-permute-done.4.rc0
  19.4 7.0 %collective-permute-start.5 = (f32[3,6,8,128]{3,2,1,0:T(8,128)S(1)}, f32[3,6,8,128]{3,2,1,0:T(8,128)S(1)}, u32[]{:S(2)}, u32[]{:S(2)}) collective-permute-start(f32[3,6,8,128]{3,2,1,0:T(8,128)S(1)} %get-tuple-element.43), channel_id=1, source_target_pairs={{0,4},{4,0},{8,12},{12,8},{1,5},{5,1},{9,13},{13,9},{2,6},{6,2},{1... | collective-permute-start | bytes 221192 | tf_op jit(solution)/shard_map/ppermute | solution.py:418
  26.4 2.3 %collective-permute-done.5.rc1 = f32[3,6,8,128]{3,2,1,0:T(8,128)S(1)} collective-permute-done((f32[3,6,8,128]{3,2,1,0:T(8,128)S(1)}, f32[3,6,8,128]{3,2,1,0:T(8,128)S(1)}, u32[]{:S(2)}, u32[]{:S(2)}) %collective-permute-start.5) | collective-permute-done | bytes 73760 | tf_op jit(solution)/shard_map/ppermute | solution.py:418
  28.8 0.0 collective-permute-done.2.ra0
  28.8 0.0 collective-permute-done.3.ra1
  28.8 7.3 %shard_map.67 = (f32[4,8,72,128]{3,2,1,0:T(8,128)S(1)}, bf16[5,3,2,128,384]{4,3,2,1,0:T(8,128)(2,1)S(1)}, bf16[4,3,2,128,384]{4,3,2,1,0:T(8,128)(2,1)S(1)}) custom-call(f32[4,4,72,128]{3,2,1,0:T(8,128)S(1)} %get-tuple-element.38.cp_ref, f32[4,4,72,128]{3,2,1,0:T(8,128)S(1)} %get-tuple-element.39.s2_ref, f32[3,4,64,128]{3,2,1,0:T(8,128)S(1)} %collective-permute-done.2.ra0, ...), custom_call_target="tpu_custom_call" | custom-call | tf_op jit(solution)/shard_map/pallas_call | solution.py:430
  36.1 0.0 collective-permute-done.6.rb0
  36.1 0.0 collective-permute-done.7.rb1
  36.1 8.0 %shard_map.68 = f32[4,4,64,96]{3,2,1,0:T(8,128)} custom-call(f32[4,8,72,128]{3,2,1,0:T(8,128)S(1)} %get-tuple-element.47.g_ref, f32[4,4,72,128]{3,2,1,0:T(8,128)S(1)} %get-tuple-element.48.s1_ref, f32[3,4,64,128]{3,2,1,0:T(8,128)S(1)} %collective-permute-done.2.ra0, f32[3,4,64,128]{3,2,1,0:T(8,128)S(1)} %collective-permute-done.3.ra1, ...), custom_call_target="tpu_custom_call" | custom-call | tf_op jit(solution)/shard_map/pallas_call | solution.py:430
Async XLA Ops:
  1.9 26.9 %collective-permute-start.2 = (f32[3,4,64,128]{3,2,1,0:T(8,128)S(1)}, f32[3,4,64,128]{3,2,1,0:T(8,128)S(1)}, u32[]{:S(2)}, u32[]{:S(2)}) collective-permute-start(f32[3,4,64,128]{3,2,1,0:T(8,128)S(1)} %get-tuple-element.40), channel_id=1, source_target_pairs={{4,8},{8,4},{5,9},{9,5},{6,10},{10,6},{7,11},{11,7},{20,24},{24,20... | collective-permute-start | bytes 1179656 | tf_op jit(solution)/shard_map/ppermute | solution.py:418
  2.6 26.2 %collective-permute-start.3 = (f32[3,4,64,128]{3,2,1,0:T(8,128)S(1)}, f32[3,4,64,128]{3,2,1,0:T(8,128)S(1)}, u32[]{:S(2)}, u32[]{:S(2)}) collective-permute-start(f32[3,4,64,128]{3,2,1,0:T(8,128)S(1)} %get-tuple-element.41), channel_id=1, source_target_pairs={{0,4},{4,0},{8,12},{12,8},{1,5},{5,1},{9,13},{13,9},{2,6},{6,2},{1... | collective-permute-start | bytes 1179656 | tf_op jit(solution)/shard_map/ppermute | solution.py:418
  8.5 7.5 %collective-permute-start = (f32[4,4,8,128]{3,2,1,0:T(8,128)S(1)}, f32[4,4,8,128]{3,2,1,0:T(8,128)S(1)}, u32[]{:S(2)}, u32[]{:S(2)}) collective-permute-start(f32[4,4,8,128]{3,2,1,0:T(8,128)S(1)} %get-tuple-element.29), channel_id=1, source_target_pairs={{1,2},{2,1},{5,6},{6,5},{9,10},{10,9},{13,14},{14,13},{17,18},{18,... | collective-permute-start | bytes 196616 | tf_op jit(solution)/shard_map/ppermute | solution.py:418
  9.1 6.8 %collective-permute-start.1 = (f32[4,4,8,128]{3,2,1,0:T(8,128)S(1)}, f32[4,4,8,128]{3,2,1,0:T(8,128)S(1)}, u32[]{:S(2)}, u32[]{:S(2)}) collective-permute-start(f32[4,4,8,128]{3,2,1,0:T(8,128)S(1)} %get-tuple-element.30), channel_id=1, source_target_pairs={{0,1},{1,0},{2,3},{3,2},{4,5},{5,4},{6,7},{7,6},{8,9},{9,8},{10,11... | collective-permute-start | bytes 196616 | tf_op jit(solution)/shard_map/ppermute | solution.py:418
  14.2 1.8 %copy-start = (bf16[6,3,2,128,384]{4,3,2,1,0:T(8,128)(2,1)}, bf16[6,3,2,128,384]{4,3,2,1,0:T(8,128)(2,1)S(1)}, u32[]{:S(2)}) copy-start(bf16[6,3,2,128,384]{4,3,2,1,0:T(8,128)(2,1)S(1)} %get-tuple-element.44.u3_ref) | copy-start | bytes 10616836
  16.1 19.9 %collective-permute-start.6 = (f32[3,2,64,128]{3,2,1,0:T(8,128)S(1)}, f32[3,2,64,128]{3,2,1,0:T(8,128)S(1)}, u32[]{:S(2)}, u32[]{:S(2)}) collective-permute-start(f32[3,2,64,128]{3,2,1,0:T(8,128)S(1)} %get-tuple-element.49), channel_id=1, source_target_pairs={{4,8},{8,4},{5,9},{9,5},{6,10},{10,6},{7,11},{11,7},{20,24},{24,20... | collective-permute-start | bytes 589832 | tf_op jit(solution)/shard_map/ppermute | solution.py:418
  16.8 19.3 %collective-permute-start.7 = (f32[3,2,64,128]{3,2,1,0:T(8,128)S(1)}, f32[3,2,64,128]{3,2,1,0:T(8,128)S(1)}, u32[]{:S(2)}, u32[]{:S(2)}) collective-permute-start(f32[3,2,64,128]{3,2,1,0:T(8,128)S(1)} %get-tuple-element.50), channel_id=1, source_target_pairs={{0,4},{4,0},{8,12},{12,8},{1,5},{5,1},{9,13},{13,9},{2,6},{6,2},{1... | collective-permute-start | bytes 589832 | tf_op jit(solution)/shard_map/ppermute | solution.py:418
  18.6 0.8 %collective-permute-start.4 = (f32[3,6,8,128]{3,2,1,0:T(8,128)S(1)}, f32[3,6,8,128]{3,2,1,0:T(8,128)S(1)}, u32[]{:S(2)}, u32[]{:S(2)}) collective-permute-start(f32[3,6,8,128]{3,2,1,0:T(8,128)S(1)} %get-tuple-element.42), channel_id=1, source_target_pairs={{4,8},{8,4},{5,9},{9,5},{6,10},{10,6},{7,11},{11,7},{20,24},{24,20... | collective-permute-start | bytes 221192 | tf_op jit(solution)/shard_map/ppermute | solution.py:418
  19.4 9.4 %collective-permute-start.5 = (f32[3,6,8,128]{3,2,1,0:T(8,128)S(1)}, f32[3,6,8,128]{3,2,1,0:T(8,128)S(1)}, u32[]{:S(2)}, u32[]{:S(2)}) collective-permute-start(f32[3,6,8,128]{3,2,1,0:T(8,128)S(1)} %get-tuple-element.43), channel_id=1, source_target_pairs={{0,4},{4,0},{8,12},{12,8},{1,5},{5,1},{9,13},{13,9},{2,6},{6,2},{1... | collective-permute-start | bytes 221192 | tf_op jit(solution)/shard_map/ppermute | solution.py:418

commit v12 on v11

--- a/solution.py
+++ b/solution.py
@@ -292,7 +292,7 @@
     return roll(taps[:, :two], -1, 0) + taps[:, two : 2 * two] + roll(taps[:, 2 * two :], 1, 0)
 
 
-def conv(read, size, width, s_ref, y_ref, w_ref, emit, done=None, beside=None):
+def conv(read, size, width, s_ref, y_ref, w_ref, emit, done=None, beside=None, ahead=False):
     chunks = width // SUB
     points = len(POINTS[size])
 
@@ -309,7 +309,8 @@
             s_ref[p, blocks, pair, :, (2 + a) * LANES : (3 + a) * LANES] = (value - high.astype(F32)).astype(BF16)
 
     def first(c, carry):
-        fill(0, pl.ds(pl.multiple_of(c * SUB, SUB), SUB), pl.ds(c, 1))
+        for p in range(points if ahead else 1):
+            fill(p, pl.ds(pl.multiple_of(c * SUB, SUB), SUB), pl.ds(c, 1))
         return carry
 
     lax.fori_loop(0, chunks, first, 0)
@@ -323,7 +324,7 @@
     for p in range(points):
         near, far = right_operands(w_ref, p)
         own = product(s_ref[p].reshape(chunks * 4 * SUB, wide), near).reshape(chunks, 2, 2, SUB, 6 * LANES)
-        if p + 1 < points:
+        if p + 1 < points and not ahead:
             fill(p + 1, slice(0, width), slice(0, chunks))
         other_work(2 * p)
         later = product(s_ref[p, :, 1].reshape(chunks * 2 * SUB, wide), far).reshape(chunks, 2, SUB, 6 * LANES)
@@ -346,7 +347,7 @@
     return ungroup_frames([jnp.where(parity("ha") == 0, from_even[g, r], from_odd[g, r]) for g in range(3)], chans)
 
 
-def third_kernel(chans, cp_ref, s2_ref, ra0, ra1, rc0, rc1, u3_ref, w2_ref, w1_ref, out_ref, u2_ref, u1_ref, x_ref, s_ref, y_ref):
+def third_kernel(chans, cp_ref, ra0, ra1, rc0, rc1, u3_ref, w2_ref, w1_ref, out_ref, u2_ref, u1_ref, x_ref, s_ref, y_ref):
     rows, width = cp_ref.shape[1:3]
     cols = width - SUB
     for r in range(3):
@@ -362,17 +363,17 @@
         return x_ref[t, r if r < 3 else r - rows, at]
 
     def emit(t, o, value):
-        out_ref[t, o] = value * s2_ref[t, o - 2] if 2 <= o < 2 + rows else value
+        out_ref[t, o] = value
 
     steps = []
     for k in range(3):
         steps += prepare(w2_ref, u2_ref, POINTS[(rows + 2) // 2], k) + prepare(w1_ref, u1_ref, POINTS[rows // 2], k)
     beside = spread(steps, 2 * len(POINTS[rows]))
-    conv(read, rows, width, s_ref, y_ref, u3_ref, emit, beside=beside)
-
-
-def last_kernel(chans, g_ref, s1_ref, ra0, ra1, rb0, rb1, rc0, rc1, u2_ref, u1_ref, out_hbm,
-                e_ref, x1_ref, s_ref, y_ref, stage_ref, sems):
+    conv(read, rows, width, s_ref, y_ref, u3_ref, emit, beside=beside, ahead=True)
+
+
+def last_kernel(chans, g_ref, s2_ref, s1_ref, ra0, ra1, rb0, rb1, rc0, rc1, u2_ref, u1_ref, out_hbm,
+                e_ref, x2_ref, x1_ref, s_ref, y_ref, stage_ref, sems):
     frames, rows, width, _ = s1_ref.shape
     cols = width - SUB
     for side, (even, odd) in enumerate(((1, 0), (0, 1))):
@@ -386,12 +387,9 @@
 
         for t in range(frames):
             for r in range(2):
-                e_ref[side, r, t] = e_ref[side, r, t] * g_ref[t, r + side * (rows + 2)]
-
-    def read2(t, r, at):
-        if 2 <= r < 2 + rows:
-            return g_ref[t, r, at]
-        return e_ref[0, r, t, at] if r < 2 else e_ref[1, r - 2 - rows, t, at]
+                at = r + side * (rows + 2)
+                x2_ref[t, at] = e_ref[side, r, t] * g_ref[t, at]
+    x2_ref[:, 2 : 2 + rows] = s2_ref[...] * g_ref[:, 2 : 2 + rows]
 
     def emit2(t, o, value):
         slope = s1_ref[t, o - 1] if 1 <= o < 1 + rows else e_ref[0 if o < 1 else 1, 2, t]
@@ -404,7 +402,7 @@
         return pltpu.make_async_copy(stage_ref.at[t], out_hbm.at[t], sems.at[t])
 
     size2, size1 = (rows + 2) // 2, rows // 2
-    conv(read2, size2, width, s_ref, y_ref, u2_ref, emit2)
+    conv(lambda t, r, at: x2_ref[t, r, at], size2, width, s_ref, y_ref, u2_ref, emit2)
     conv(lambda t, r, at: x1_ref[t, r, at], size1, width, s_ref, y_ref, u1_ref, emit1, lambda t: copy_out(t).start())
     for t in range(frames):
         copy_out(t).wait()
@@ -425,7 +423,7 @@
     return got
 
 
-def call(body, out_shape, args, scratch=(), hbm=(), hbm_out=False, alias=None, vmem=40 << 20):
+def call(body, out_shape, args, scratch=(), hbm=(), hbm_out=False, alias=None, vmem=24 << 20):
     out = HBM_SPEC if hbm_out else VMEM_SPEC
     return pl.pallas_call(
         body,
@@ -497,14 +495,18 @@
     grad, u2, u1 = call(
         functools.partial(third_kernel, chans),
         (arr(frames, rows + 4, width, LANES), weights(size2), weights(size1)),
-        (cp, s2, ra0, ra1, rc0, rc1, u3, second, first),
+        (cp, ra0, ra1, rc0, rc1, u3, second, first),
         [vmem(frames, 6, width, LANES)] + scratch(size3),
     )
     return call(
         functools.partial(last_kernel, chans),
         arr(frames, rows, cols, chans),
-        (grad, s1, ra0, ra1, rb0, rb1, rc0, rc1, u2, u1),
-        [vmem(2, 3, frames, width, LANES), vmem(frames, rows + 2, width, LANES)]
+        (grad, s2, s1, ra0, ra1, rb0, rb1, rc0, rc1, u2, u1),
+        [
+            vmem(2, 3, frames, width, LANES),
+            vmem(frames, rows + 4, width, LANES),
+            vmem(frames, rows + 2, width, LANES),
+        ]
         + scratch(size2)
         + [vmem(frames, rows, cols, chans), pltpu.SemaphoreType.DMA((frames,))],
         hbm_out=True,

time: 44.5 us -> 41 us (0.921)
  local copies, waits for them, and re-layouts: 1.74 us -> 0 us
  Pallas kernels: 19.4 us -> 17.7 us
    unnamed x2 -> x0, local copies, waits for them, and re-layouts: 1.74 us -> none
    pallas_call x5, Pallas kernels: 19.4 us -> 17.7 us  [call(): pl.pallas_call(body, out_shape=out_shape, in_specs=[HBM_SPEC if n in hbm...]
  transfers between devices with their start and end apart: 8 -> 8, of which waited for: 1 -> 1; matrix products, arithmetic and copies ran while one was open for 0% -> 0% of each run, Pallas kernels for 22% -> 19%
where the time goes in v12:
time: 41 us; the launch traced here: 40.8 us
  starting transfers between devices  20.5 us (50%)
  Pallas kernels  17.7 us (43%)
  waiting for transfers between devices  2.35 us (6%)
    ppermute x8, starting transfers between devices, swap(): return lax.ppermute(value, axis, pairs)  20.5 us
    pallas_call x5, Pallas kernels, call(): pl.pallas_call(body, out_shape=out_shape, in_specs=[HBM_SPEC if n in hbm...  17.7 us
    ppermute x8, waiting for transfers between devices, swap(): return lax.ppermute(value, axis, pairs)  2.35 us
  transfers between devices with their start and end apart: 8, of which 1 were waited for; matrix products, arithmetic and copies ran while one was open for 0% of the time, Pallas kernels for 19%

profile of v12, /device:TPU:0, one launch (start us, length us, event | category | flops | bytes accessed | tf_op | source)
XLA Modules:
  0.0 40.8 jit_solution(17343648172219314853)
XLA Ops:
  0.0 1.9 %shard_map.64 = (f32[3,4,64,128]{3,2,1,0:T(8,128)S(1)}, f32[3,4,64,128]{3,2,1,0:T(8,128)S(1)}, f32[4,4,8,128]{3,2,1,0:T(8,128)S(1)}, f32[4,4,8,128]{3,2,1,0:T(8,...) custom-call(f32[4,4,64,96]{3,2,1,0:T(8,128)} %cot_hbm.1, ...), custom_call_target="tpu_custom_call" | custom-call | tf_op jit(solution)/shard_map/pallas_call | solution.py:428
  1.9 0.7 %collective-permute-start.2 = (f32[3,4,64,128]{3,2,1,0:T(8,128)S(1)}, f32[3,4,64,128]{3,2,1,0:T(8,128)S(1)}, u32[]{:S(2)}, u32[]{:S(2)}) collective-permute-start(f32[3,4,64,128]{3,2,1,0:T(8,128)S(1)} %get-tuple-element.39), channel_id=1, source_target_pairs={{4,8},{8,4},{5,9},{9,5},{6,10},{10,6},{7,11},{11,7},{20,24},{24,20... | collective-permute-start | bytes 1179656 | tf_op jit(solution)/shard_map/ppermute | solution.py:416
  2.6 5.9 %collective-permute-start.3 = (f32[3,4,64,128]{3,2,1,0:T(8,128)S(1)}, f32[3,4,64,128]{3,2,1,0:T(8,128)S(1)}, u32[]{:S(2)}, u32[]{:S(2)}) collective-permute-start(f32[3,4,64,128]{3,2,1,0:T(8,128)S(1)} %get-tuple-element.40), channel_id=1, source_target_pairs={{0,4},{4,0},{8,12},{12,8},{1,5},{5,1},{9,13},{13,9},{2,6},{6,2},{1... | collective-permute-start | bytes 1179656 | tf_op jit(solution)/shard_map/ppermute | solution.py:416
  8.5 0.7 %collective-permute-start = (f32[4,4,8,128]{3,2,1,0:T(8,128)S(1)}, f32[4,4,8,128]{3,2,1,0:T(8,128)S(1)}, u32[]{:S(2)}, u32[]{:S(2)}) collective-permute-start(f32[4,4,8,128]{3,2,1,0:T(8,128)S(1)} %get-tuple-element.29), channel_id=1, source_target_pairs={{1,2},{2,1},{5,6},{6,5},{9,10},{10,9},{13,14},{14,13},{17,18},{18,... | collective-permute-start | bytes 196616 | tf_op jit(solution)/shard_map/ppermute | solution.py:416
  9.1 2.9 %collective-permute-start.1 = (f32[4,4,8,128]{3,2,1,0:T(8,128)S(1)}, f32[4,4,8,128]{3,2,1,0:T(8,128)S(1)}, u32[]{:S(2)}, u32[]{:S(2)}) collective-permute-start(f32[4,4,8,128]{3,2,1,0:T(8,128)S(1)} %get-tuple-element.30), channel_id=1, source_target_pairs={{0,1},{1,0},{2,3},{3,2},{4,5},{5,4},{6,7},{7,6},{8,9},{9,8},{10,11... | collective-permute-start | bytes 196616 | tf_op jit(solution)/shard_map/ppermute | solution.py:416
  12.1 2.1 %shard_map.65 = (f32[3,2,64,128]{3,2,1,0:T(8,128)S(1)}, f32[3,2,64,128]{3,2,1,0:T(8,128)S(1)}, f32[4,4,72,128]{3,2,1,0:T(8,128)S(1)}, f32[4,4,72,128]{3,2,1,0:T(...) custom-call(f32[4,4,64,96]{3,2,1,0:T(8,128)S(1)} %get-tuple-element., ...), custom_call_target="tpu_custom_call" | custom-call | tf_op jit(solution)/shard_map/pallas_call | solution.py:428
  14.2 0.0 collective-permute-done.rw0
  14.2 0.0 collective-permute-done.1.rw1
  14.2 0.1 shard_map.66
  14.4 0.7 %collective-permute-start.6 = (f32[3,2,64,128]{3,2,1,0:T(8,128)S(1)}, f32[3,2,64,128]{3,2,1,0:T(8,128)S(1)}, u32[]{:S(2)}, u32[]{:S(2)}) collective-permute-start(f32[3,2,64,128]{3,2,1,0:T(8,128)S(1)} %get-tuple-element.49), channel_id=1, source_target_pairs={{4,8},{8,4},{5,9},{9,5},{6,10},{10,6},{7,11},{11,7},{20,24},{24,20... | collective-permute-start | bytes 589832 | tf_op jit(solution)/shard_map/ppermute | solution.py:416
  15.1 1.8 %collective-permute-start.7 = (f32[3,2,64,128]{3,2,1,0:T(8,128)S(1)}, f32[3,2,64,128]{3,2,1,0:T(8,128)S(1)}, u32[]{:S(2)}, u32[]{:S(2)}) collective-permute-start(f32[3,2,64,128]{3,2,1,0:T(8,128)S(1)} %get-tuple-element.50), channel_id=1, source_target_pairs={{0,4},{4,0},{8,12},{12,8},{1,5},{5,1},{9,13},{13,9},{2,6},{6,2},{1... | collective-permute-start | bytes 589832 | tf_op jit(solution)/shard_map/ppermute | solution.py:416
  16.8 0.8 %collective-permute-start.4 = (f32[3,6,8,128]{3,2,1,0:T(8,128)S(1)}, f32[3,6,8,128]{3,2,1,0:T(8,128)S(1)}, u32[]{:S(2)}, u32[]{:S(2)}) collective-permute-start(f32[3,6,8,128]{3,2,1,0:T(8,128)S(1)} %get-tuple-element.41), channel_id=1, source_target_pairs={{4,8},{8,4},{5,9},{9,5},{6,10},{10,6},{7,11},{11,7},{20,24},{24,20... | collective-permute-start | bytes 221192 | tf_op jit(solution)/shard_map/ppermute | solution.py:416
  17.7 0.0 collective-permute-done.4.rc0
  17.7 7.0 %collective-permute-start.5 = (f32[3,6,8,128]{3,2,1,0:T(8,128)S(1)}, f32[3,6,8,128]{3,2,1,0:T(8,128)S(1)}, u32[]{:S(2)}, u32[]{:S(2)}) collective-permute-start(f32[3,6,8,128]{3,2,1,0:T(8,128)S(1)} %get-tuple-element.42), channel_id=1, source_target_pairs={{0,4},{4,0},{8,12},{12,8},{1,5},{5,1},{9,13},{13,9},{2,6},{6,2},{1... | collective-permute-start | bytes 221192 | tf_op jit(solution)/shard_map/ppermute | solution.py:416
  24.7 2.3 %collective-permute-done.5.rc1 = f32[3,6,8,128]{3,2,1,0:T(8,128)S(1)} collective-permute-done((f32[3,6,8,128]{3,2,1,0:T(8,128)S(1)}, f32[3,6,8,128]{3,2,1,0:T(8,128)S(1)}, u32[]{:S(2)}, u32[]{:S(2)}) %collective-permute-start.5) | collective-permute-done | bytes 73760 | tf_op jit(solution)/shard_map/ppermute | solution.py:416
  27.0 0.0 collective-permute-done.2.ra0
  27.1 0.0 collective-permute-done.3.ra1
  27.1 5.5 %shard_map.67 = (f32[4,8,72,128]{3,2,1,0:T(8,128)S(1)}, bf16[5,3,2,128,384]{4,3,2,1,0:T(8,128)(2,1)S(1)}, bf16[4,3,2,128,384]{4,3,2,1,0:T(8,128)(2,1)S(1)}) custom-call(f32[4,4,72,128]{3,2,1,0:T(8,128)S(1)} %get-tuple-element.38.cp_ref, f32[3,4,64,128]{3,2,1,0:T(8,128)S(1)} %collective-permute-done.2.ra0, f32[3,4,64,128]{3,2,1,0:T(8,128)S(1)} %collective-permute-done.3.ra1, ...), custom_call_target="tpu_custom_call" | custom-call | tf_op jit(solution)/shard_map/pallas_call | solution.py:428
  32.6 0.0 collective-permute-done.6.rb0
  32.6 0.0 collective-permute-done.7.rb1
  32.6 8.0 %shard_map.68 = f32[4,4,64,96]{3,2,1,0:T(8,128)} custom-call(f32[4,8,72,128]{3,2,1,0:T(8,128)S(1)} %get-tuple-element.46.g_ref, f32[4,4,72,128]{3,2,1,0:T(8,128)S(1)} %get-tuple-element.47.s2_ref, f32[4,4,72,128]{3,2,1,0:T(8,128)S(1)} %get-tuple-element.48.s1_ref, f32[3,4,64,128]{3,2,1,0:T(8,128)S(1)} %collective-permute-done.2.ra0, ...), custom_call_target="tpu_custom_call" | custom-call | tf_op jit(solution)/shard_map/pallas_call | solution.py:428
Async XLA Ops:
  1.9 25.2 %collective-permute-start.2 = (f32[3,4,64,128]{3,2,1,0:T(8,128)S(1)}, f32[3,4,64,128]{3,2,1,0:T(8,128)S(1)}, u32[]{:S(2)}, u32[]{:S(2)}) collective-permute-start(f32[3,4,64,128]{3,2,1,0:T(8,128)S(1)} %get-tuple-element.39), channel_id=1, source_target_pairs={{4,8},{8,4},{5,9},{9,5},{6,10},{10,6},{7,11},{11,7},{20,24},{24,20... | collective-permute-start | bytes 1179656 | tf_op jit(solution)/shard_map/ppermute | solution.py:416
  2.6 24.5 %collective-permute-start.3 = (f32[3,4,64,128]{3,2,1,0:T(8,128)S(1)}, f32[3,4,64,128]{3,2,1,0:T(8,128)S(1)}, u32[]{:S(2)}, u32[]{:S(2)}) collective-permute-start(f32[3,4,64,128]{3,2,1,0:T(8,128)S(1)} %get-tuple-element.40), channel_id=1, source_target_pairs={{0,4},{4,0},{8,12},{12,8},{1,5},{5,1},{9,13},{13,9},{2,6},{6,2},{1... | collective-permute-start | bytes 1179656 | tf_op jit(solution)/shard_map/ppermute | solution.py:416
  8.5 5.7 %collective-permute-start = (f32[4,4,8,128]{3,2,1,0:T(8,128)S(1)}, f32[4,4,8,128]{3,2,1,0:T(8,128)S(1)}, u32[]{:S(2)}, u32[]{:S(2)}) collective-permute-start(f32[4,4,8,128]{3,2,1,0:T(8,128)S(1)} %get-tuple-element.29), channel_id=1, source_target_pairs={{1,2},{2,1},{5,6},{6,5},{9,10},{10,9},{13,14},{14,13},{17,18},{18,... | collective-permute-start | bytes 196616 | tf_op jit(solution)/shard_map/ppermute | solution.py:416
  9.1 5.1 %collective-permute-start.1 = (f32[4,4,8,128]{3,2,1,0:T(8,128)S(1)}, f32[4,4,8,128]{3,2,1,0:T(8,128)S(1)}, u32[]{:S(2)}, u32[]{:S(2)}) collective-permute-start(f32[4,4,8,128]{3,2,1,0:T(8,128)S(1)} %get-tuple-element.30), channel_id=1, source_target_pairs={{0,1},{1,0},{2,3},{3,2},{4,5},{5,4},{6,7},{7,6},{8,9},{9,8},{10,11... | collective-permute-start | bytes 196616 | tf_op jit(solution)/shard_map/ppermute | solution.py:416
  14.4 18.2 %collective-permute-start.6 = (f32[3,2,64,128]{3,2,1,0:T(8,128)S(1)}, f32[3,2,64,128]{3,2,1,0:T(8,128)S(1)}, u32[]{:S(2)}, u32[]{:S(2)}) collective-permute-start(f32[3,2,64,128]{3,2,1,0:T(8,128)S(1)} %get-tuple-element.49), channel_id=1, source_target_pairs={{4,8},{8,4},{5,9},{9,5},{6,10},{10,6},{7,11},{11,7},{20,24},{24,20... | collective-permute-start | bytes 589832 | tf_op jit(solution)/shard_map/ppermute | solution.py:416
  15.1 17.5 %collective-permute-start.7 = (f32[3,2,64,128]{3,2,1,0:T(8,128)S(1)}, f32[3,2,64,128]{3,2,1,0:T(8,128)S(1)}, u32[]{:S(2)}, u32[]{:S(2)}) collective-permute-start(f32[3,2,64,128]{3,2,1,0:T(8,128)S(1)} %get-tuple-element.50), channel_id=1, source_target_pairs={{0,4},{4,0},{8,12},{12,8},{1,5},{5,1},{9,13},{13,9},{2,6},{6,2},{1... | collective-permute-start | bytes 589832 | tf_op jit(solution)/shard_map/ppermute | solution.py:416
  16.8 0.8 %collective-permute-start.4 = (f32[3,6,8,128]{3,2,1,0:T(8,128)S(1)}, f32[3,6,8,128]{3,2,1,0:T(8,128)S(1)}, u32[]{:S(2)}, u32[]{:S(2)}) collective-permute-start(f32[3,6,8,128]{3,2,1,0:T(8,128)S(1)} %get-tuple-element.41), channel_id=1, source_target_pairs={{4,8},{8,4},{5,9},{9,5},{6,10},{10,6},{7,11},{11,7},{20,24},{24,20... | collective-permute-start | bytes 221192 | tf_op jit(solution)/shard_map/ppermute | solution.py:416
  17.7 9.4 %collective-permute-start.5 = (f32[3,6,8,128]{3,2,1,0:T(8,128)S(1)}, f32[3,6,8,128]{3,2,1,0:T(8,128)S(1)}, u32[]{:S(2)}, u32[]{:S(2)}) collective-permute-start(f32[3,6,8,128]{3,2,1,0:T(8,128)S(1)} %get-tuple-element.42), channel_id=1, source_target_pairs={{0,4},{4,0},{8,12},{12,8},{1,5},{5,1},{9,13},{13,9},{2,6},{6,2},{1... | collective-permute-start | bytes 221192 | tf_op jit(solution)/shard_map/ppermute | solution.py:416
